TPU v7x, 512 devices: a whole 4x4x16 slice. The times are simulated.
512 devices in a mesh: subj: 32 (over y, z_lo), slab: 16 (over x, z_hi, core).
Axes of the slice: x: 4, y: 4, z: 16 (z_hi: 2, z_lo: 8; z = z_hi * 8 + z_lo), core: 2. Of those that a mesh axis runs over, the one named last changes fastest.
Arguments:
- image: float32 [32, 192, 32, 192], P('subj', 'slab'), may hold values from -6 to 6
- velocity: float32 [32, 3, 192, 32, 192], P('subj', None, 'slab'), may hold values from -3 to 3
- template: float32 [192, 32, 192], P('slab', 'subj'), may hold values from -6 to 6
- z_kernel: float32 [192, 192], replicated, as said below
- x_kernel: float32 [192, 192], replicated, as said below
Outputs:
- velocity_update: float32 [32, 3, 192, 32, 192], P('subj', None, 'slab')
- new_template: float32 [192, 32, 192], P('slab', 'subj')
Inputs may be any that keep to these rules, and one draw needn't show every extreme that they name: `z_kernel`: entries are positive. `x_kernel`: entries are positive.
All inputs are finite; a program needn't handle non-finite values.
Results may differ from a plain program's by a relative error of at most 0.00028.
Values sent between devices are 32-bit elements; how exact they have to be, the bound alone decides.
No kernel may reach another device: no remote copies, remote signals or barrier semaphores. Data moves between devices by JAX's collectives and lax.ppermute only.
A program may use at most 64 MiB of HBM per device.

v0:
```python
import jax
import jax.numpy as jnp
from jax import lax
from jax.sharding import PartitionSpec as P


def with_halo(x, sides, width):
    for axis, dim in sides:
        size, length = (lax.axis_size(axis), x.shape[dim])
        up = [(i, (i + 1) % size) for i in range(size - 1)]
        down = [(j, i) for i, j in up]
        last = lax.slice_in_dim(x, length - width, length, axis=dim)
        leading = lax.slice_in_dim(x, 0, width, axis=dim)
        before = lax.ppermute(last, axis, up)
        after = lax.ppermute(leading, axis, down)
        x = jnp.concatenate([before, x, after], axis=dim)
    return x


def gradients(padded):
    slope_z = (padded[2:, 1:-1, 1:-1] - padded[:-2, 1:-1, 1:-1]) * 0.5
    slope_y = (padded[1:-1, 2:, 1:-1] - padded[1:-1, :-2, 1:-1]) * 0.5
    slope_x = (padded[1:-1, 1:-1, 2:] - padded[1:-1, 1:-1, :-2]) * 0.5
    return jnp.stack([slope_z, slope_y, slope_x])


def per_device(image, velocity, template, z_kernel, x_kernel):
    highest = lax.Precision.HIGHEST
    full_rows = lax.all_gather(template, "subj", axis=1, tiled=True)
    with_rims = with_halo(full_rows, (("slab", 0),), 1)
    padded = jnp.pad(with_rims, ((0, 0), (1, 1), (1, 1)))
    slopes = gradients(padded)
    warped = full_rows[None] + jnp.sum(velocity * slopes[None], 1)
    residual = image - warped
    forces = residual[:, None] * slopes[None]
    along_x = jnp.einsum("sczyx,wx->sczyw", forces, x_kernel, precision=highest)
    along_z = jnp.einsum(
        "vz,sczyx->scvyx",
        z_kernel,
        lax.all_to_all(along_x, "slab", split_axis=3, concat_axis=2, tiled=True),
        precision=highest,
    )
    velocity_update = lax.all_to_all(along_z, "slab", split_axis=2, concat_axis=3, tiled=True)
    local_sum = jnp.sum(residual, 0)
    subjects = lax.axis_size("subj") * image.shape[0]
    summed = lax.psum_scatter(local_sum, "subj", scatter_dimension=1, tiled=True)
    new_template = template + summed / subjects
    return (velocity_update, new_template)


def solution(mesh):
    in_specs = (
        P("subj", "slab", None, None),
        P("subj", None, "slab", None, None),
        P("slab", "subj", None),
        P(),
        P(),
    )
    out_specs = (P("subj", None, "slab", None, None), P("slab", "subj", None))
    return jax.shard_map(
        per_device, mesh=mesh, in_specs=in_specs, out_specs=out_specs, check_vma=False
    )
```

profile of v0, /device:TPU:4, one launch (start us, length us, event | category | flops | bytes accessed | tf_op | source)
XLA Modules:
  0.0 502.2 jit_solution(7305345701270509311)
XLA Ops:
  7.2 0.0 copy-start
  7.2 0.8 copy.43
  7.9 130.0 %all_gather.3 = f32[12,32,192]{2,0,1:T(8,128)S(1)} all-gather(f32[12,1,192]{2,0,1:T(8,128)S(1)} %copy.43), channel_id=1, replica_groups=mesh['subj'=32,'slab'=16] {'subj'}, dimensions={1}, use_global_device_ids=true | all-gather | bytes 304128 | tf_op jit(solution)/shard_map/all_gather | solution.py:29
  138.0 1.9 collective-permute-start.1
  139.9 13.3 %collective-permute-start = (f32[1,32,192]{2,0,1:T(1,128)S(1)}, f32[1,32,192]{2,0,1:T(1,128)S(1)}, u32[]{:S(2)}, u32[]{:S(2)}) collective-permute-start(f32[1,32,192]{2,0,1:T(1,128)S(1)} %get-tuple-element.13), channel_id=1, source_target_pairs={{1,0},{2,1},{3,2},{4,3},{5,4},{6,5},{7,6},{8,7},{9,8},{10,9},{11,1... | collective-permute-start | bytes 73736 | tf_op jit(solution)/shard_map/ppermute | solution.py:15
  153.2 1.6 collective-permute-done
  154.7 0.3 select_maximum_fusion
  155.1 0.0 copy-start.2
  155.1 0.6 fusion.10
  155.7 0.6 copy-done.2
  156.3 1.0 fusion
  157.4 0.3 fusion.14
  157.7 0.2 fusion.3
  158.0 0.5 copy-done.1
  158.5 1.7 convolution_bitcast_fusion.1
  160.2 1.2 copy.47
  161.4 70.8 %all_to_all.33 = f32[1,3,12,32,192]{4,0,2,1,3:T(1,128)S(1)} all-to-all(f32[1,3,12,32,192]{4,0,2,1,3:T(1,128)S(1)} %copy.47), channel_id=1, replica_groups=mesh['subj'=32,'slab'=16] {'slab'}, dimensions={3} | all-to-all | bytes 1769472 | tf_op jit(solution)/shard_map/all_to_all | solution.py:40
  232.3 1.3 copy.48
  233.6 0.0 copy-start.4
  233.6 0.6 copy.49
  234.2 0.3 copy-done.4
  234.5 2.3 convolution_bitcast_fusion
  236.8 1.5 copy.51
  238.4 8.6 %all-to-all-start.1 = ((f32[1,3,192,2,192]{4,3,1,0,2:T(2,128)}), f32[1,3,192,2,192]{4,3,1,0,2:T(2,128)S(1)}, u32[]{:S(2)}, u32[]{:S(2)}) async-start(f32[1,3,192,2,192]{4,3,1,0,2:T(2,128)} %copy.51), calls=%async_computation.1 | async-start | bytes 2359296 | tf_op jit(solution)/shard_map/all_to_all | solution.py:43
  246.9 0.0 reduce-scatter.2.cloned.1.call-start
  247.0 0.7 reduce-scatter.2.cloned.1.call-update
  247.6 243.6 %reduce-scatter.2.cloned.1.call-done = f32[12,1,192]{2,0,1:T(8,128)} async-done(((f32[12,32,192]{2,0,1:T(8,128)}), f32[12,1,192]{2,0,1:T(8,128)}) %reduce-scatter.2.cloned.1.call-update) | async-done | bytes 9232 | tf_op jit(solution)/shard_map/reduce_scatter | solution.py:46
  491.3 0.7 multiply_add_fusion
  492.0 0.6 copy.56
  492.6 0.4 copy.52
  493.0 1.2 copy.53
  494.2 1.1 copy.55
  (9 shorter events, 0.1 us)
Async XLA Ops:
  7.2 151.3 %copy-start = (f32[192,192]{1,0:T(8,128)S(1)}, f32[192,192]{1,0:T(8,128)}, u32[]{:S(2)}) copy-start(f32[192,192]{1,0:T(8,128)} %param.9) | copy-start | bytes 442372
  138.0 15.2 %collective-permute-start.1 = (f32[1,32,192]{2,0,1:T(1,128)S(1)}, f32[1,32,192]{2,0,1:T(1,128)S(1)}, u32[]{:S(2)}, u32[]{:S(2)}) collective-permute-start(f32[1,32,192]{2,0,1:T(1,128)S(1)} %get-tuple-element.12), channel_id=1, source_target_pairs={{0,1},{1,2},{2,3},{3,4},{4,5},{5,6},{6,7},{7,8},{8,9},{9,10},{10,1... | collective-permute-start | bytes 73736 | tf_op jit(solution)/shard_map/ppermute | solution.py:14
  139.9 14.8 %collective-permute-start = (f32[1,32,192]{2,0,1:T(1,128)S(1)}, f32[1,32,192]{2,0,1:T(1,128)S(1)}, u32[]{:S(2)}, u32[]{:S(2)}) collective-permute-start(f32[1,32,192]{2,0,1:T(1,128)S(1)} %get-tuple-element.13), channel_id=1, source_target_pairs={{1,0},{2,1},{3,2},{4,3},{5,4},{6,5},{7,6},{8,7},{9,8},{10,9},{11,1... | collective-permute-start | bytes 73736 | tf_op jit(solution)/shard_map/ppermute | solution.py:15
  155.1 1.3 copy-start.2
  156.3 1.1 copy-start.3
  157.7 0.8 copy-start.1
  233.6 0.9 copy-start.4
  238.4 252.9 %copy-start.5 = (f32[12,1,192]{2,1,0:T(1,128)S(1)}, f32[12,1,192]{2,1,0:T(1,128)}, u32[]{:S(2)}) copy-start(f32[12,1,192]{2,1,0:T(1,128)} %param.7) | copy-start | bytes 27652
  238.4 254.3 %all-to-all-start.1 = ((f32[1,3,192,2,192]{4,3,1,0,2:T(2,128)}), f32[1,3,192,2,192]{4,3,1,0,2:T(2,128)S(1)}, u32[]{:S(2)}, u32[]{:S(2)}) async-start(f32[1,3,192,2,192]{4,3,1,0,2:T(2,128)} %copy.51), calls=%async_computation.1 | async-start | bytes 2359296 | tf_op jit(solution)/shard_map/all_to_all | solution.py:43
  246.9 244.4 %reduce-scatter.2.cloned.1.call-start = ((), (), s32[]{:S(2)}) async-start(), calls=%async_computation.3 | async-start | bytes 540672 | tf_op jit(solution)/shard_map/reduce_scatter | solution.py:46
Sparse Core Ops, SparseCore 0:
  250.5 240.7 reduce-scatter.1
where the time goes:
time: 503 us; the launch traced here: 502 us
  waiting for transfers between devices  246 us (49%)
  blocking collectives  201 us (40%)
  starting transfers between devices  23.8 us (5%)
  between operations  14.2 us (3%)
  local copies, waits for them, and re-layouts  10.3 us (2%)
    reduce_scatter x1, waiting for transfers between devices, per_device(): lax.psum_scatter(local_sum, 'subj', scatter_dimension=1, tiled=True)  244 us
    all_gather x1, blocking collectives, per_device(): full_rows = lax.all_gather(template, 'subj', axis=1, tiled=True)  130 us
    all_to_all x1, blocking collectives, per_device(): lax.all_to_all(along_x, 'slab', split_axis=3, concat_axis=2, tiled=True)  70.8 us
    ppermute x1, starting transfers between devices, with_halo(): after = lax.ppermute(leading, axis, down)  13.3 us
  transfers between devices with their start and end apart: 4, of which 2 were waited for; matrix products, arithmetic and copies ran while one was open for 0% of the time, Pallas kernels for 0%

commit v1 on v0

v1 whole, which is shorter than its diff:
```python
import jax
import jax.numpy as jnp
from jax import lax
from jax.experimental import pallas as pl
from jax.experimental.pallas import tpu as pltpu
from jax.sharding import Mesh, PartitionSpec as P

ROW = ("y", "x", "c")
COL = ("zl", "zh")
LANES, WIDE = 128, 256


def split_lanes(a):
    return a[..., :LANES], a[..., LANES:]


def template_pieces(row):
    low, high = split_lanes(row)
    return jnp.concatenate([low, jnp.pad(high, ((0, 0), (0, 64)))], 0)


def gather_template(row, raw):
    piece = template_pieces(row)
    by_z = lax.all_to_all(
        jnp.broadcast_to(piece[None], (16, 24, LANES)), COL, 0, 0, tiled=True
    )
    by_z, raw = lax.optimization_barrier((by_z, raw))
    mine = lax.all_to_all(by_z.reshape(8, 2, 24, LANES), ("x", "c"), 0, 0, tiled=True)
    after = [(i, i + 1) for i in range(31)]
    prev = lax.ppermute(mine, ROW, after)
    succ = lax.ppermute(mine, ROW, [(j, i) for i, j in after])
    return prev, mine, succ, raw


def pack_raw(image, velocity):
    four = jnp.concatenate([image[None], velocity], 0)
    low, high = split_lanes(four)
    pairs = jnp.concatenate([high[0::2], high[1::2]], -1)
    six = jnp.concatenate([low, pairs], 0)
    return six.transpose(2, 0, 1, 3).reshape(32, 72, LANES)


def place(refs, half, out):
    for r, ref in enumerate(refs):
        out[r] = jnp.zeros((208, WIDE), jnp.float32)
        for x in range(4):
            for h in range(2):
                for c in range(2):
                    at = 8 + 48 * x + 24 * h + 12 * c
                    out[r, at : at + 12, :LANES] = ref[2 * x + c, h, :12]
                    out[r, at : at + 12, LANES:] = ref[2 * x + c, h, 12:]


def slopes_of(grid, start, rows):
    here = grid[1, pl.ds(start, rows), :]
    sz = (grid[1, pl.ds(start + 1, rows), :] - grid[1, pl.ds(start - 1, rows), :]) * 0.5
    sy = (grid[2, pl.ds(start, rows), :] - grid[0, pl.ds(start, rows), :]) * 0.5
    sx = (pltpu.roll(here, WIDE - 1, 1) - pltpu.roll(here, 1, 1)) * 0.5
    return here, sz, sy, sx


def template_kernel(prev, mine, succ, tmpl, slopes, grid):
    place((prev, mine, succ), None, grid)
    here, sz, sy, sx = slopes_of(grid, 8, 192)
    tmpl[...] = here
    lane = lax.broadcasted_iota(jnp.int32, (192, WIDE), 1)
    slopes[0] = sz
    slopes[1] = sy
    slopes[2] = jnp.where(lane < 192, sx, 0.0)


def template_and_slopes(prev, mine, succ):
    return pl.pallas_call(
        template_kernel,
        out_shape=(
            jax.ShapeDtypeStruct((192, WIDE), jnp.float32),
            jax.ShapeDtypeStruct((3, 192, WIDE), jnp.float32),
        ),
        scratch_shapes=[pltpu.VMEM((3, 208, WIDE), jnp.float32)],
    )(prev, mine, succ)


def halves(a, zh, axis=-2):
    lead = a.shape[:-2]
    b = a.reshape(*lead, 4, 2, 24, a.shape[-1])
    first, second = b[..., 0, :, :], b[..., 1, :, :]
    own = jnp.where(zh == 0, first, second).reshape(*lead, 96, a.shape[-1])
    other = jnp.where(zh == 0, second, first).reshape(*lead, 96, a.shape[-1])
    return own, other


def per_device(image, velocity, template, z_kernel, x_kernel):
    highest = lax.Precision.HIGHEST
    zh = lax.axis_index("zh")
    raw = lax.all_to_all(pack_raw(image[0], velocity[0]), ROW, 0, 0, tiled=True)
    prev, mine, succ, raw = gather_template(template[:, 0, :], raw)
    tmpl, slopes = template_and_slopes(prev, mine, succ)
    own_t, _ = halves(tmpl, zh)
    own_s, other_s = halves(slopes, zh)

    six = raw.reshape(4, 8, 6, 12, LANES).transpose(2, 0, 1, 3, 4).reshape(6, 4, 96, LANES)
    low, pairs = six[:4], six[4:]
    zero = jnp.zeros((4, 4, 96, 64), jnp.float32)
    high = jnp.stack([pairs[0, ..., :64], pairs[0, ..., 64:], pairs[1, ..., :64], pairs[1, ..., 64:]])
    four = jnp.concatenate([low, high, zero], -1)
    residual = four[0] - (own_t + jnp.sum(four[1:] * own_s[:, None], 0))

    sent = jnp.concatenate(
        [
            residual[..., :LANES],
            jnp.concatenate([residual[0::2, :, LANES:192], residual[1::2, :, LANES:192]], -1),
        ],
        0,
    )
    got = lax.ppermute(sent, "zh", [(0, 1), (1, 0)])
    high = jnp.stack([got[4, :, :64], got[4, :, 64:], got[5, :, :64], got[5, :, 64:]])
    other = jnp.concatenate([got[:4], high, zero[0]], -1)

    local = jnp.sum(residual, 0).reshape(8, 12, WIDE)
    local = jnp.concatenate([local[..., :LANES], local[..., LANES:]], 1)
    summed = jnp.sum(lax.all_to_all(local, "zl", 0, 0, tiled=True), 0)
    swap = [
        ((zl * 4 + x) * 2 + c, ((2 * x + c) * 4 + zl // 2) * 2 + zl % 2)
        for zl in range(8)
        for x in range(4)
        for c in range(2)
    ]
    summed = lax.ppermute(summed, ("zl", "x", "c"), swap)
    summed = jnp.concatenate([summed[:12], summed[12:, :64]], -1)
    new_template = template + summed[:, None, :] / 32

    forces = jnp.concatenate(
        [residual[:, None] * own_s[None], other[:, None] * other_s[None]], 2
    )
    k_own, _ = halves(z_kernel, zh)
    k_oo, k_op = halves(k_own.T, zh)
    k = jnp.concatenate([k_oo, k_op], 0)
    along_z = jnp.einsum("zv,sczx->scvx", k, forces[..., :192], precision=highest)
    update = jnp.einsum("scvx,wx->scvw", along_z, x_kernel, precision=highest)
    update = update.reshape(4, 3, 8, 12, 192).transpose(0, 2, 1, 3, 4).reshape(32, 3, 12, 192)
    low, high = split_lanes(update)
    high = jnp.concatenate([high[:, :, :6], high[:, :, 6:]], -1)
    packed = jnp.concatenate([low.reshape(32, 36, LANES), high.reshape(32, 18, LANES)], 1)
    back = lax.all_to_all(packed, ROW, 0, 0, tiled=True)
    low = back[:, :36].reshape(32, 3, 12, LANES)
    high = back[:, 36:].reshape(32, 3, 6, LANES)
    high = jnp.concatenate([high[..., :64], high[..., 64:]], 2)
    out = jnp.concatenate([low, high], -1).transpose(1, 2, 0, 3)
    return out[None], new_template


def solution(mesh):
    fine = Mesh(mesh.devices.reshape(4, 8, 4, 2, 2), ("y", "zl", "x", "zh", "c"))
    subj, slab = ("y", "zl"), ("x", "zh", "c")
    in_specs = (
        P(subj, slab, None, None),
        P(subj, None, slab, None, None),
        P(slab, subj, None),
        P(),
        P(),
    )
    out_specs = (P(subj, None, slab, None, None), P(slab, subj, None))
    return jax.shard_map(
        per_device, mesh=fine, in_specs=in_specs, out_specs=out_specs, check_vma=False
    )
```

time: 503 us -> 164 us (0.33)
  the two profiles are of different devices: /device:TPU:4 before, /device:TPU:1 now
where the time goes in v1:
time: 164 us; the launch traced here: 163 us
  waiting for transfers between devices  78.8 us (48%)
  starting transfers between devices  56.9 us (35%)
  local copies, waits for them, and re-layouts  10.3 us (6%)
  other arithmetic  9.69 us (6%)
  matrix products  4.42 us (3%)
  Pallas kernels  2.15 us (1%)
    ppermute x1, waiting for transfers between devices, per_device(): got = lax.ppermute(sent, 'zh', [(0, 1), (1, 0)])  27.7 us
    all_to_all x1, waiting for transfers between devices, per_device(): raw = lax.all_to_all(pack_raw(image[0], velocity[0]), ROW, 0, 0, tiled=True)  16.8 us
    all_to_all x1, starting transfers between devices, gather_template(): lax.all_to_all(jnp.broadcast_to(piece[None], (16, 24, LANES)), COL, 0, 0,...  15.8 us
    all_to_all x1, waiting for transfers between devices, gather_template(): lax.all_to_all(jnp.broadcast_to(piece[None], (16, 24, LANES)), COL, 0, 0,...  11.5 us
    all_to_all x1, starting transfers between devices, per_device(): raw = lax.all_to_all(pack_raw(image[0], velocity[0]), ROW, 0, 0, tiled=True)  11.1 us
    all_to_all x1, waiting for transfers between devices, per_device(): back = lax.all_to_all(packed, ROW, 0, 0, tiled=True)  9.76 us
    all_to_all x1, starting transfers between devices, per_device(): summed = jnp.sum(lax.all_to_all(local, 'zl', 0, 0, tiled=True), 0)  8.91 us
    all_to_all x1, starting transfers between devices, per_device(): back = lax.all_to_all(packed, ROW, 0, 0, tiled=True)  6.25 us
  transfers between devices with their start and end apart: 9, of which 8 were waited for; matrix products, arithmetic and copies ran while one was open for 9% of the time, Pallas kernels for 0%

profile of v1, /device:TPU:1, one launch (start us, length us, event | category | flops | bytes accessed | tf_op | source)
XLA Modules:
  0.0 163.5 jit_solution(10748000991348119336)
XLA Ops:
  0.7 0.8 copy.81
  1.5 0.7 broadcast_in_dim.6
  2.2 15.8 %all-to-all-start = ((f32[16,24,128]{2,1,0:T(8,128)}), f32[16,24,128]{2,1,0:T(8,128)}, u32[]{:S(2)}, u32[]{:S(2)}) async-start(f32[16,24,128]{2,1,0:T(8,128)} %broadcast_in_dim.6), calls=%async_computation | async-start | bytes 393216 | tf_op jit(solution)/shard_map/all_to_all | solution.py:24
  18.0 1.2 pad_maximum_fusion.5
  19.6 1.7 %copy.55 = f32[32,72,128]{2,1,0:T(8,128)} copy(f32[32,72,128]{2,0,1:T(8,128)S(1)} %bitcast.66) | data formatting | bytes 2359296 | tf_op jit(solution)/shard_map/reshape | solution.py:40
  21.3 11.5 %all-to-all-done = f32[16,24,128]{2,1,0:T(8,128)} async-done(((f32[16,24,128]{2,1,0:T(8,128)}), f32[16,24,128]{2,1,0:T(8,128)}, u32[]{:S(2)}, u32[]{:S(2)}) %all-to-all-start) | async-done | bytes 196640 | tf_op jit(solution)/shard_map/all_to_all | solution.py:24
  32.8 11.1 %all-to-all-start.1 = ((f32[32,72,128]{2,1,0:T(8,128)}), f32[32,72,128]{2,1,0:T(8,128)S(1)}, u32[]{:S(2)}, u32[]{:S(2)}) async-start(f32[32,72,128]{2,1,0:T(8,128)} %copy.55), calls=%async_computation.1 | async-start | bytes 2359296 | tf_op jit(solution)/shard_map/all_to_all | solution.py:95
  44.1 0.6 slice_select_fusion.5
  44.8 16.8 %all-to-all-done.1 = f32[32,72,128]{2,1,0:T(8,128)S(1)} async-done(((f32[32,72,128]{2,1,0:T(8,128)}), f32[32,72,128]{2,1,0:T(8,128)S(1)}, u32[]{:S(2)}, u32[]{:S(2)}) %all-to-all-start.1) | async-done | bytes 1179680 | tf_op jit(solution)/shard_map/all_to_all | solution.py:95
  62.2 4.9 %all-to-all-start.2 = ((f32[8,2,24,128]{3,2,1,0:T(8,128)}), f32[8,2,24,128]{3,2,1,0:T(8,128)S(1)}, u32[]{:S(2)}, u32[]{:S(2)}) async-start(f32[8,2,24,128]{3,2,1,0:T(8,128)} %bitcast.9), calls=%async_computation.2 | async-start | bytes 393216 | tf_op jit(solution)/shard_map/all_to_all | solution.py:28
  67.4 5.6 %all-to-all-done.2.mine = f32[8,2,24,128]{3,2,1,0:T(8,128)S(1)} async-done(((f32[8,2,24,128]{3,2,1,0:T(8,128)}), f32[8,2,24,128]{3,2,1,0:T(8,128)S(1)}, u32[]{:S(2)}, u32[]{:S(2)}) %all-to-all-start.2) | async-done | bytes 196640 | tf_op jit(solution)/shard_map/all_to_all | solution.py:28
  73.0 3.0 %collective-permute-start = (f32[8,2,24,128]{3,2,1,0:T(8,128)S(1)}, f32[8,2,24,128]{3,2,1,0:T(8,128)S(1)}, u32[]{:S(2)}, u32[]{:S(2)}) collective-permute-start(f32[8,2,24,128]{3,2,1,0:T(8,128)S(1)} %all-to-all-done.2.mine), channel_id=1, source_target_pairs={{0,1},{1,4},{4,5},{5,8},{8,9},{9,12},{12,13},{13,128},{128,129},{1... | collective-permute-start | bytes 589832 | tf_op jit(solution)/shard_map/ppermute | solution.py:30
  76.1 1.9 %collective-permute-start.1 = (f32[8,2,24,128]{3,2,1,0:T(8,128)S(1)}, f32[8,2,24,128]{3,2,1,0:T(8,128)}, u32[]{:S(2)}, u32[]{:S(2)}) collective-permute-start(f32[8,2,24,128]{3,2,1,0:T(8,128)S(1)} %all-to-all-done.2.mine), channel_id=1, source_target_pairs={{1,0},{4,1},{5,4},{8,5},{9,8},{12,9},{13,12},{128,13},{129,128},{1... | collective-permute-start | bytes 589832 | tf_op jit(solution)/shard_map/ppermute | solution.py:31
  78.6 0.7 copy-done.7
  79.3 3.8 %collective-permute-done.1.succ = f32[8,2,24,128]{3,2,1,0:T(8,128)} collective-permute-done((f32[8,2,24,128]{3,2,1,0:T(8,128)S(1)}, f32[8,2,24,128]{3,2,1,0:T(8,128)}, u32[]{:S(2)}, u32[]{:S(2)}) %collective-permute-start.1) | collective-permute-done | bytes 196640 | tf_op jit(solution)/shard_map/ppermute | solution.py:31
  83.1 2.2 %shard_map.68 = (f32[192,256]{1,0:T(8,128)}, f32[3,192,256]{2,1,0:T(8,128)}) custom-call(f32[8,2,24,128]{3,2,1,0:T(8,128)} %copy-done.7, f32[8,2,24,128]{3,2,1,0:T(8,128)} %copy-done.3, f32[8,2,24,128]{3,2,1,0:T(8,128)} %collective-permute-done.1.succ), custom_call_target="tpu_custom_call" | custom-call | tf_op jit(solution)/shard_map/pallas_call | solution.py:73
  85.3 1.1 slice_select_fusion.1
  86.4 1.0 slice_select_fusion.3
  90.0 3.1 %collective-permute-start.2 = (f32[6,96,128]{2,0,1:T(8,128)S(1)}, f32[6,96,128]{2,0,1:T(8,128)S(1)}, u32[]{:S(2)}, u32[]{:S(2)}) collective-permute-start(f32[6,96,128]{2,0,1:T(8,128)S(1)} %maximum_maximum_fusion.2), channel_id=1, source_target_pairs={{0,2},{2,0},{1,3},{3,1},{4,6},{6,4},{5,7},{7,5},{8,10},{10,8},{9,1... | collective-permute-start | bytes 884744 | tf_op jit(solution)/shard_map/ppermute | solution.py:115
  93.1 0.6 pad_maximum_fusion.7
  93.8 8.9 %all-to-all-start.4 = ((f32[8,24,128]{2,1,0:T(8,128)}), f32[8,24,128]{2,1,0:T(8,128)S(1)}, u32[]{:S(2)}, u32[]{:S(2)}) async-start(f32[8,24,128]{2,1,0:T(8,128)} %pad_maximum_fusion.7), calls=%async_computation.4 | async-start | bytes 196608 | tf_op jit(solution)/shard_map/all_to_all | solution.py:121
  102.8 27.7 %collective-permute-done.2 = f32[6,96,128]{2,0,1:T(8,128)S(1)} collective-permute-done((f32[6,96,128]{2,0,1:T(8,128)S(1)}, f32[6,96,128]{2,0,1:T(8,128)S(1)}, u32[]{:S(2)}, u32[]{:S(2)}) %collective-permute-start.2) | collective-permute-done | bytes 294944 | tf_op jit(solution)/shard_map/ppermute | solution.py:115
  132.2 2.1 %fusion.2 = f32[4,3,96,192]{2,3,1,0:T(8,128)S(1)} fusion(f32[4,3,96,256]{2,3,1,0:T(8,128)S(1)} %get-tuple-element.32, f32[4,3,96,256]{2,3,1,0:T(8,128)S(1)} %get-tuple-element.33, f32[96,96]{1,0:T(8,128)S(1)} %bitcast.81, f32[96,96]{1,0:T(8,128)S(1)} %bitcast.80), kind=kOutput, calls=%fused_computation.6 | convolution fusion | flops 510068736 | bytes 3317760 | tf_op jit(solution)/shard_map/zv,sczx->scvx/dot_general | solution.py:138
  134.3 2.4 %fusion.6 = f32[4,3,96,192]{3,2,1,0:T(8,128)S(1)} fusion(f32[4,3,96,192]{2,3,1,0:T(8,128)S(1)} %fusion.2, f32[192,192]{1,0:T(8,128)S(1)} %copy-done), kind=kOutput, calls=%fused_computation.24 | convolution fusion | flops 509607936 | bytes 1916928 | tf_op jit(solution)/shard_map/scvx,wx->scvw/dot_general | solution.py:139
  136.6 0.8 copy.65
  137.4 0.7 copy.80
  138.9 1.0 pad_maximum_fusion.4
  139.9 6.2 %all-to-all-start.3 = ((f32[32,54,128]{2,1,0:T(8,128)}), f32[32,54,128]{2,1,0:T(8,128)S(1)}, u32[]{:S(2)}, u32[]{:S(2)}) async-start(f32[32,54,128]{2,1,0:T(8,128)} %pad_maximum_fusion.4), calls=%async_computation.3 | async-start | bytes 1835008 | tf_op jit(solution)/shard_map/all_to_all | solution.py:144
  146.2 1.9 %collective-permute-start.3 = (f32[24,128]{1,0:T(8,128)S(1)}, f32[24,128]{1,0:T(8,128)S(1)}, u32[]{:S(2)}, u32[]{:S(2)}) collective-permute-start(f32[24,128]{1,0:T(8,128)S(1)} %reduce_sum.29), channel_id=1, source_target_pairs={{0,0},{1,16},{4,32},{5,48},{8,64},{9,80},{12,96},{13,112},{16,1},{... | collective-permute-start | bytes 36872 | tf_op jit(solution)/shard_map/ppermute | solution.py:128
  148.1 3.4 %collective-permute-done.3 = f32[24,128]{1,0:T(8,128)S(1)} collective-permute-done((f32[24,128]{1,0:T(8,128)S(1)}, f32[24,128]{1,0:T(8,128)S(1)}, u32[]{:S(2)}, u32[]{:S(2)}) %collective-permute-start.3) | collective-permute-done | bytes 12320 | tf_op jit(solution)/shard_map/ppermute | solution.py:128
  152.2 9.8 %all-to-all-done.3 = f32[32,54,128]{2,1,0:T(8,128)S(1)} async-done(((f32[32,54,128]{2,1,0:T(8,128)}), f32[32,54,128]{2,1,0:T(8,128)S(1)}, u32[]{:S(2)}, u32[]{:S(2)}) %all-to-all-start.3) | async-done | bytes 884768 | tf_op jit(solution)/shard_map/all_to_all | solution.py:144
  162.4 1.1 maximum_bitcast_fusion
  (68 shorter events, 8.3 us)
Async XLA Ops:
  0.6 133.6 %copy-start = (f32[192,192]{1,0:T(8,128)S(1)}, f32[192,192]{1,0:T(8,128)}, u32[]{:S(2)}) copy-start(f32[192,192]{1,0:T(8,128)} %param.9) | copy-start | bytes 442372
  0.6 18.5 %copy-start.1 = (f32[1,3,12,32,192]{4,3,2,1,0:T(8,128)S(1)}, f32[1,3,12,32,192]{4,3,2,1,0:T(8,128)}, u32[]{:S(2)}) copy-start(f32[1,3,12,32,192]{4,3,2,1,0:T(8,128)} %param.6) | copy-start | bytes 2654212
  0.7 18.5 %copy-start.2 = (f32[1,12,32,192]{3,2,1,0:T(8,128)S(1)}, f32[1,12,32,192]{3,2,1,0:T(8,128)}, u32[]{:S(2)}) copy-start(f32[1,12,32,192]{3,2,1,0:T(8,128)} %param.5) | copy-start | bytes 884740
  2.2 30.5 %all-to-all-start = ((f32[16,24,128]{2,1,0:T(8,128)}), f32[16,24,128]{2,1,0:T(8,128)}, u32[]{:S(2)}, u32[]{:S(2)}) async-start(f32[16,24,128]{2,1,0:T(8,128)} %broadcast_in_dim.6), calls=%async_computation | async-start | bytes 393216 | tf_op jit(solution)/shard_map/all_to_all | solution.py:24
  21.3 22.6 %copy-start.6 = (f32[192,192]{1,0:T(8,128)S(1)}, f32[192,192]{1,0:T(8,128)}, u32[]{:S(2)}) copy-start(f32[192,192]{1,0:T(8,128)} %param.8) | copy-start | bytes 442372
  32.8 28.8 %all-to-all-start.1 = ((f32[32,72,128]{2,1,0:T(8,128)}), f32[32,72,128]{2,1,0:T(8,128)S(1)}, u32[]{:S(2)}, u32[]{:S(2)}) async-start(f32[32,72,128]{2,1,0:T(8,128)} %copy.55), calls=%async_computation.1 | async-start | bytes 2359296 | tf_op jit(solution)/shard_map/all_to_all | solution.py:95
  62.2 10.8 %all-to-all-start.2 = ((f32[8,2,24,128]{3,2,1,0:T(8,128)}), f32[8,2,24,128]{3,2,1,0:T(8,128)S(1)}, u32[]{:S(2)}, u32[]{:S(2)}) async-start(f32[8,2,24,128]{3,2,1,0:T(8,128)} %bitcast.9), calls=%async_computation.2 | async-start | bytes 393216 | tf_op jit(solution)/shard_map/all_to_all | solution.py:28
  73.0 5.4 %copy-start.3 = (f32[8,2,24,128]{3,2,1,0:T(8,128)}, f32[8,2,24,128]{3,2,1,0:T(8,128)S(1)}, u32[]{:S(2)}) copy-start(f32[8,2,24,128]{3,2,1,0:T(8,128)S(1)} %all-to-all-done.2.mine) | copy-start | bytes 589828
  73.0 5.6 %collective-permute-start = (f32[8,2,24,128]{3,2,1,0:T(8,128)S(1)}, f32[8,2,24,128]{3,2,1,0:T(8,128)S(1)}, u32[]{:S(2)}, u32[]{:S(2)}) collective-permute-start(f32[8,2,24,128]{3,2,1,0:T(8,128)S(1)} %all-to-all-done.2.mine), channel_id=1, source_target_pairs={{0,1},{1,4},{4,5},{5,8},{8,9},{9,12},{12,13},{13,128},{128,129},{1... | collective-permute-start | bytes 589832 | tf_op jit(solution)/shard_map/ppermute | solution.py:30
  76.1 7.1 %collective-permute-start.1 = (f32[8,2,24,128]{3,2,1,0:T(8,128)S(1)}, f32[8,2,24,128]{3,2,1,0:T(8,128)}, u32[]{:S(2)}, u32[]{:S(2)}) collective-permute-start(f32[8,2,24,128]{3,2,1,0:T(8,128)S(1)} %all-to-all-done.2.mine), channel_id=1, source_target_pairs={{1,0},{4,1},{5,4},{8,5},{9,8},{12,9},{13,12},{128,13},{129,128},{1... | collective-permute-start | bytes 589832 | tf_op jit(solution)/shard_map/ppermute | solution.py:31
  78.6 0.7 copy-start.7
  90.0 40.5 %collective-permute-start.2 = (f32[6,96,128]{2,0,1:T(8,128)S(1)}, f32[6,96,128]{2,0,1:T(8,128)S(1)}, u32[]{:S(2)}, u32[]{:S(2)}) collective-permute-start(f32[6,96,128]{2,0,1:T(8,128)S(1)} %maximum_maximum_fusion.2), channel_id=1, source_target_pairs={{0,2},{2,0},{1,3},{3,1},{4,6},{6,4},{5,7},{7,5},{8,10},{10,8},{9,1... | collective-permute-start | bytes 884744 | tf_op jit(solution)/shard_map/ppermute | solution.py:115
  93.8 46.1 %all-to-all-start.4 = ((f32[8,24,128]{2,1,0:T(8,128)}), f32[8,24,128]{2,1,0:T(8,128)S(1)}, u32[]{:S(2)}, u32[]{:S(2)}) async-start(f32[8,24,128]{2,1,0:T(8,128)} %pad_maximum_fusion.7), calls=%async_computation.4 | async-start | bytes 196608 | tf_op jit(solution)/shard_map/all_to_all | solution.py:121
  131.4 0.8 copy-start.4
  131.4 0.8 copy-start.5
  138.9 12.6 %copy-start.8 = (f32[12,1,192]{2,1,0:T(1,128)S(1)}, f32[12,1,192]{2,1,0:T(1,128)}, u32[]{:S(2)}) copy-start(f32[12,1,192]{2,1,0:T(1,128)} %param.7) | copy-start | bytes 27652
  139.9 22.0 %all-to-all-start.3 = ((f32[32,54,128]{2,1,0:T(8,128)}), f32[32,54,128]{2,1,0:T(8,128)S(1)}, u32[]{:S(2)}, u32[]{:S(2)}) async-start(f32[32,54,128]{2,1,0:T(8,128)} %pad_maximum_fusion.4), calls=%async_computation.3 | async-start | bytes 1835008 | tf_op jit(solution)/shard_map/all_to_all | solution.py:144
  146.2 5.3 %collective-permute-start.3 = (f32[24,128]{1,0:T(8,128)S(1)}, f32[24,128]{1,0:T(8,128)S(1)}, u32[]{:S(2)}, u32[]{:S(2)}) collective-permute-start(f32[24,128]{1,0:T(8,128)S(1)} %reduce_sum.29), channel_id=1, source_target_pairs={{0,0},{1,16},{4,32},{5,48},{8,64},{9,80},{12,96},{13,112},{16,1},{... | collective-permute-start | bytes 36872 | tf_op jit(solution)/shard_map/ppermute | solution.py:128

commit v2 on v0

v2 whole, which is shorter than its diff:
```python
import jax
import jax.numpy as jnp
from jax import lax
from jax.experimental import pallas as pl
from jax.experimental.pallas import tpu as pltpu
from jax.sharding import Mesh, PartitionSpec as P

ROW = ("y", "x", "c")
COL = ("zl", "zh")
LANES, WIDE = 128, 256
F32 = jnp.float32
BF16 = jnp.bfloat16


def shape(*dims):
    return jax.ShapeDtypeStruct(dims, F32)


def vmem(n):
    return [pl.BlockSpec(memory_space=pltpu.VMEM)] * n


def smem():
    return pl.BlockSpec(memory_space=pltpu.SMEM)


def call(kernel, outs, scratch=()):
    def run(place, *args):
        return pl.pallas_call(
            kernel,
            out_shape=outs,
            in_specs=[smem(), *vmem(len(args))],
            out_specs=tuple(vmem(len(outs))),
            scratch_shapes=list(scratch),
        )(place, *args)

    return run


def piece_kernel(place, row, out):
    values = row[:, 0, :]
    for i in range(16):
        out[i, :12, :] = values[:, :LANES]
        out[i, 12:, :] = jnp.concatenate([values[:, LANES:], jnp.zeros((12, 64), F32)], 1)


def pack_kernel(place, image, velocity, *outs):
    for s, out in enumerate(outs):
        at = pl.multiple_of(8 * lax.rem(place[0] + s, 4), 8)
        rows = pl.ds(at, 8)
        for a in range(4):
            src = image if a == 0 else velocity.at[a - 1]
            out[a] = src[:, rows, :LANES]
        for k in range(2):
            first = image if k == 0 else velocity.at[1]
            second = velocity.at[2 * k]
            out[4 + k] = jnp.concatenate([first[:, rows, LANES:], second[:, rows, LANES:]], -1)


def residual_kernel(place, tmpl, prev_row, next_row, by_core, by_x, *rest):
    raws, (out, total) = rest[:4], rest[4:]
    zh, c = place[1], place[2]
    low, high = tmpl[zh, :12], tmpl[zh, 12:]
    here = jnp.concatenate([low, high], -1)

    at_x = jnp.logical_and(c == 0, zh == 0)
    z_from = jnp.where(c == 0, 1 - zh, zh)
    before = jnp.where(
        at_x,
        jnp.concatenate([by_x[1, 1], by_x[1, 3]], -1),
        jnp.concatenate([by_core[z_from, 1], by_core[z_from, 3]], -1),
    )
    at_x = jnp.logical_and(c == 1, zh == 1)
    z_from = jnp.where(c == 0, zh, 1 - zh)
    after = jnp.where(
        at_x,
        jnp.concatenate([by_x[0, 0], by_x[0, 2]], -1),
        jnp.concatenate([by_core[z_from, 0], by_core[z_from, 2]], -1),
    )
    up = jnp.concatenate([here[1:], after[None]], 0)
    down = jnp.concatenate([before[None], here[:-1]], 0)
    slope_z = (up - down) * 0.5

    line = lax.broadcasted_iota(jnp.int32, (12, 8, WIDE), 1)

    def edge(ref):
        e = jnp.concatenate([ref[zh, :12], ref[zh, 12:]], -1)
        return jnp.broadcast_to(e[:, None, :], (12, 8, WIDE))

    up = jnp.where(line == 7, edge(next_row), pltpu.roll(here, 7, 1))
    down = jnp.where(line == 0, edge(prev_row), pltpu.roll(here, 1, 1))
    slope_y = (up - down) * 0.5
    slope_x = (pltpu.roll(here, WIDE - 1, 2) - pltpu.roll(here, 1, 2)) * 0.5

    slopes = (slope_z, slope_y, slope_x)
    lane = lax.broadcasted_iota(jnp.int32, (12, 8, LANES), 2)
    sum_low = jnp.zeros((12, 8, LANES), F32)
    sum_high = jnp.zeros((12, 8, LANES), F32)
    highs = []
    for s, raw in enumerate(raws):
        warped = here[..., :LANES]
        motion = raw[1] * slopes[0][..., :LANES] + raw[2] * slopes[1][..., :LANES] + raw[3] * slopes[2][..., :LANES]
        r_low = raw[0] - (warped + motion)
        zero_one, two_three = raw[4], raw[5]
        swap_01, swap_23 = pltpu.roll(zero_one, 64, 2), pltpu.roll(two_three, 64, 2)
        motion = swap_01 * slopes[0][..., LANES:] + two_three * slopes[1][..., LANES:] + swap_23 * slopes[2][..., LANES:]
        r_high = zero_one - (here[..., LANES:] + motion)
        out[12 * s : 12 * s + 12] = r_low
        highs.append(r_high)
        sum_low += r_low
        sum_high += r_high
    for k in range(2):
        out[48 + 12 * k : 60 + 12 * k] = jnp.where(lane < 64, highs[2 * k], pltpu.roll(highs[2 * k + 1], 64, 2))
    total[:12] = sum_low
    total[12:] = sum_high


def main_kernel(place, rows, own, other, zk, xk, out, grid, force, part):
    y, zh = place[0], place[1]
    for r in range(3):
        grid[r] = jnp.zeros((208, WIDE), F32)
        for x in range(4):
            for h in range(2):
                for c in range(2):
                    at = 8 + 48 * x + 24 * h + 12 * c
                    grid[r, at : at + 12, :LANES] = rows[2 * x + c, r, h, :12]
                    grid[r, at : at + 12, LANES:] = rows[2 * x + c, r, h, 12:]
    here = grid[1, 8:200]
    low_lane = lax.broadcasted_iota(jnp.int32, (192, LANES), 1) < 64
    slopes = (
        (grid[1, 9:201] - grid[1, 7:199]) * 0.5,
        (grid[2, 8:200] - grid[0, 8:200]) * 0.5,
        (pltpu.roll(here, WIDE - 1, 1) - pltpu.roll(here, 1, 1)) * 0.5,
    )
    for c, slope in enumerate(slopes):
        high = slope[:, LANES:]
        part[c, :, :LANES] = slope[:, :LANES]
        part[c, :, LANES:] = jnp.where(low_lane, high, pltpu.roll(high, 64, 1))

    for ref, h in ((own, zh), (other, 1 - zh)):
        for x in range(4):
            at = pl.ds(pl.multiple_of(48 * x + 24 * h, 8), 24)
            for b in range(6):
                r = jnp.concatenate([ref[2 * x, 12 * b : 12 * b + 12], ref[2 * x + 1, 12 * b : 12 * b + 12]], 0)
                for c in range(3):
                    s = part[c, at, :LANES] if b < 4 else part[c, at, LANES:]
                    force[at, (c * 6 + b) * LANES : (c * 6 + b + 1) * LANES] = r * s

    def split(a):
        top = a.astype(BF16)
        return top, (a - top.astype(F32)).astype(BF16)

    def times(a, b):
        (a1, a0), (b1, b0) = a, b
        dot = lambda p, q: jnp.dot(p, q, preferred_element_type=F32)
        return dot(a1, b1) + (dot(a1, b0) + dot(a0, b1))

    zrows = jnp.concatenate(
        [zk[pl.ds(pl.multiple_of(48 * x + 24 * zh, 8), 24), :] for x in range(4)], 0
    )
    smooth = times(split(zrows), split(force[...]))

    xt = xk[...]
    zeros = jnp.zeros((64, 192), F32)
    for odd in range(2):
        cols = [xt[:LANES], zeros, xt[LANES:]] if odd else [xt[:LANES], xt[LANES:], zeros]
        weights = split(jnp.concatenate(cols, 0))
        left = []
        for s in (odd, odd + 2):
            for c in range(3):
                at = c * 6 * LANES
                left.append(
                    jnp.concatenate(
                        [
                            smooth[:, at + s * LANES : at + (s + 1) * LANES],
                            smooth[:, at + (4 + s // 2) * LANES : at + (5 + s // 2) * LANES],
                        ],
                        1,
                    )
                )
        update = times(split(jnp.concatenate(left, 0)), weights)
        for i, s in enumerate((odd, odd + 2)):
            to = 8 * lax.rem(y + 4 - s, 4)
            for c in range(3):
                for j in range(8):
                    at = (i * 3 + c) * 96 + 12 * j
                    piece = update[at : at + 12]
                    out[to + j, 12 * c : 12 * c + 12, :] = piece[:, :LANES]
                    out[to + j, 36 + 6 * c : 42 + 6 * c, :] = jnp.concatenate(
                        [piece[:6, LANES:], piece[6:, LANES:]], 1
                    )


def per_device(image, velocity, template, z_kernel, x_kernel):
    place = jnp.stack([lax.axis_index(a) for a in ("y", "zh", "c")]).astype(jnp.int32)

    (piece,) = call(piece_kernel, (shape(16, 24, LANES),))(place, template)
    gathered = lax.all_to_all(piece, COL, 0, 0, tiled=True).reshape(8, 2, 24, LANES)

    raws = call(pack_kernel, (shape(6, 12, 8, LANES),) * 4)(place, image[0], velocity[0])
    raws = [raws[0]] + [
        lax.ppermute(raws[s], "y", [(i, (i + s) % 4) for i in range(4)]) for s in (1, 2, 3)
    ]

    prev_row = lax.ppermute(gathered[7], "y", [(i, i + 1) for i in range(3)])
    next_row = lax.ppermute(gathered[0], "y", [(i + 1, i) for i in range(3)])
    ends = jnp.stack([gathered[:, :, i] for i in (0, 11, 12, 23)], 2).transpose(1, 2, 0, 3)
    by_core = lax.ppermute(ends, "c", [(0, 1), (1, 0)])
    by_x = lax.ppermute(ends, ("x", "c"), [(2 * i + 1, 2 * i + 2) for i in range(3)] + [(2 * i + 2, 2 * i + 1) for i in range(3)])
    tmpl = gathered.transpose(1, 2, 0, 3)

    residual, total = call(residual_kernel, (shape(72, 8, LANES), shape(24, 8, LANES)))(
        place, tmpl, prev_row, next_row, by_core, by_x, *raws
    )
    own = lax.all_to_all(residual.transpose(1, 0, 2), ("x", "c"), 0, 0, tiled=True)
    other = lax.ppermute(own, "zh", [(0, 1), (1, 0)])

    summed = lax.psum_scatter(total, "zl", scatter_dimension=1, tiled=True)
    summed = jnp.concatenate([summed[:12], summed[12:, :, :64]], -1)
    new_template = template + summed / 32

    ten = jnp.concatenate([prev_row[None], gathered, next_row[None]], 0)
    rows = jnp.stack([ten[i : i + 8] for i in range(3)], 1)
    rows = lax.all_to_all(rows, ("x", "c"), 0, 0, tiled=True)

    (packed,) = call(
        main_kernel,
        (shape(32, 54, LANES),),
        (
            pltpu.VMEM((3, 208, WIDE), F32),
            pltpu.VMEM((192, 18 * LANES), F32),
            pltpu.VMEM((3, 192, WIDE), F32),
        ),
    )(place, rows, own, other, z_kernel, x_kernel.T)
    back = lax.all_to_all(packed, ROW, 0, 0, tiled=True)
    low = back[:, :36].reshape(32, 3, 12, LANES)
    high = back[:, 36:].reshape(32, 3, 6, LANES)
    high = jnp.concatenate([high[..., :64], high[..., 64:]], 2)
    out = jnp.concatenate([low, high], -1).transpose(1, 2, 0, 3)
    return out[None], new_template


def solution(mesh):
    fine = Mesh(mesh.devices.reshape(4, 8, 4, 2, 2), ("y", "zl", "x", "zh", "c"))
    subj, slab = ("y", "zl"), ("x", "zh", "c")
    in_specs = (
        P(subj, slab, None, None),
        P(subj, None, slab, None, None),
        P(slab, subj, None),
        P(),
        P(),
    )
    out_specs = (P(subj, None, slab, None, None), P(slab, subj, None))
    return jax.shard_map(
        per_device, mesh=fine, in_specs=in_specs, out_specs=out_specs, check_vma=False
    )
```

time: 503 us -> 256 us (0.51)
  the two profiles are of different devices: /device:TPU:4 before, /device:TPU:1 now
where the time goes in v2:
time: 256 us; the launch traced here: 251 us
  waiting for transfers between devices  147 us (57%)
  starting transfers between devices  65.7 us (26%)
  between operations  14.3 us (6%)
  local copies, waits for them, and re-layouts  11.5 us (4%)
  Pallas kernels  10.3 us (4%)
  other arithmetic  2.62 us (1%)
    unnamed x2, waiting for transfers between devices  109 us
    ppermute x1, waiting for transfers between devices, per_device(): other = lax.ppermute(own, 'zh', [(0, 1), (1, 0)])  27.9 us
    all_to_all x1, starting transfers between devices, per_device(): lax.all_to_all(piece, COL, 0, 0, tiled=True).reshape(8, 2, 24, LANES)  15.7 us
    ppermute x3, starting transfers between devices, per_device(): lax.ppermute(raws[s], 'y', [(i, (i + s) % 4) for i in range(4)])  10.7 us
    pallas_call x4, Pallas kernels, run(): pl.pallas_call(kernel, out_shape=outs, in_specs=[smem(), *vmem(len(args))...  10.3 us
    all_to_all x1, starting transfers between devices, per_device(): back = lax.all_to_all(packed, ROW, 0, 0, tiled=True)  8.1 us
    ppermute x1, starting transfers between devices, per_device(): other = lax.ppermute(own, 'zh', [(0, 1), (1, 0)])  7.82 us
    ppermute x1, starting transfers between devices, per_device(): by_core = lax.ppermute(ends, 'c', [(0, 1), (1, 0)])  5.95 us
  transfers between devices with their start and end apart: 13, of which 6 were waited for; matrix products, arithmetic and copies ran while one was open for 4% of the time, Pallas kernels for 1%

profile of v2, /device:TPU:1, one launch (start us, length us, event | category | flops | bytes accessed | tf_op | source)
XLA Modules:
  0.0 251.5 jit_solution(9809083234416069968)
XLA Ops:
  7.8 1.4 shard_map.68
  9.2 15.7 %all-to-all-start = ((f32[16,24,128]{2,1,0:T(8,128)}), f32[16,24,128]{2,1,0:T(8,128)S(1)}, u32[]{:S(2)}, u32[]{:S(2)}) async-start(f32[16,24,128]{2,1,0:T(8,128)} %shard_map.68), calls=%async_computation | async-start | bytes 393216 | tf_op jit(solution)/shard_map/all_to_all | solution.py:198
  24.9 2.6 %shard_map.69 = (f32[6,12,8,128]{3,2,1,0:T(8,128)}, f32[6,12,8,128]{3,2,1,0:T(8,128)}, f32[6,12,8,128]{3,2,1,0:T(8,128)}, f32[6,12,8,128]{3,2,1,0:T(8,128)}) custom-call(s32[3]{0:T(128)} %pad_add_fusion.place, f32[12,32,192]{2,1,0:T(8,128)} %bitcast.41, f32[3,12,32,192]{3,2,1,0:T(8,128)} %bitcast.39), custom_call_target="tpu_custom_call" | custom-call | tf_op jit(solution)/shard_map/pallas_call | solution.py:29
  27.5 3.2 %collective-permute-start.4 = (f32[6,12,8,128]{3,2,1,0:T(8,128)}, f32[6,12,8,128]{3,2,1,0:T(8,128)S(1)}, u32[]{:S(2)}, u32[]{:S(2)}) collective-permute-start(f32[6,12,8,128]{3,2,1,0:T(8,128)} %get-tuple-element.9), channel_id=1, source_target_pairs={{0,128},{128,256},{256,384},{384,0},{1,129},{129,257},{257,385},{3... | collective-permute-start | bytes 884744 | tf_op jit(solution)/shard_map/ppermute | solution.py:202
  30.7 4.5 %collective-permute-start.5 = (f32[6,12,8,128]{3,2,1,0:T(8,128)}, f32[6,12,8,128]{3,2,1,0:T(8,128)S(1)}, u32[]{:S(2)}, u32[]{:S(2)}) collective-permute-start(f32[6,12,8,128]{3,2,1,0:T(8,128)} %get-tuple-element.10), channel_id=1, source_target_pairs={{0,256},{128,384},{256,0},{384,128},{1,257},{129,385},{257,1},{385... | collective-permute-start | bytes 884744 | tf_op jit(solution)/shard_map/ppermute | solution.py:202
  35.2 3.0 %collective-permute-start.6 = (f32[6,12,8,128]{3,2,1,0:T(8,128)}, f32[6,12,8,128]{3,2,1,0:T(8,128)S(1)}, u32[]{:S(2)}, u32[]{:S(2)}) collective-permute-start(f32[6,12,8,128]{3,2,1,0:T(8,128)} %get-tuple-element.11), channel_id=1, source_target_pairs={{0,384},{128,0},{256,128},{384,256},{1,385},{129,1},{257,129},{385... | collective-permute-start | bytes 884744 | tf_op jit(solution)/shard_map/ppermute | solution.py:202
  38.2 1.4 all-to-all-done
  39.7 6.0 %collective-permute-start.2 = (f32[2,4,8,128]{3,1,0,2:T(4,128)S(1)}, f32[2,4,8,128]{3,1,0,2:T(4,128)S(1)}, u32[]{:S(2)}, u32[]{:S(2)}) collective-permute-start(f32[2,4,8,128]{3,1,0,2:T(4,128)S(1)} %maximum_bitcast_fusion.1), channel_id=1, source_target_pairs={{0,1},{1,0},{2,3},{3,2},{4,5},{5,4},{6,7},{7,6},{8,9},{9,8},{10,11... | collective-permute-start | bytes 98312 | tf_op jit(solution)/shard_map/ppermute | solution.py:208
  45.6 3.0 %collective-permute-start.3 = (f32[2,4,8,128]{3,1,0,2:T(4,128)S(1)}, f32[2,4,8,128]{3,1,0,2:T(4,128)S(1)}, u32[]{:S(2)}, u32[]{:S(2)}) collective-permute-start(f32[2,4,8,128]{3,1,0,2:T(4,128)S(1)} %maximum_bitcast_fusion.1), channel_id=1, source_target_pairs={{1,4},{5,8},{9,12},{4,1},{8,5},{12,9},{3,6},{7,10},{11,14},{6,3},{... | collective-permute-start | bytes 98312 | tf_op jit(solution)/shard_map/ppermute | solution.py:209
  48.7 3.2 %collective-permute-start = (f32[2,24,128]{2,1,0:T(8,128)S(1)}, f32[2,24,128]{2,1,0:T(8,128)S(1)}, u32[]{:S(2)}, u32[]{:S(2)}) collective-permute-start(f32[2,24,128]{2,1,0:T(8,128)S(1)} %get-tuple-element.22), channel_id=1, source_target_pairs={{0,128},{128,256},{256,384},{1,129},{129,257},{257,385},{2,130},{1... | collective-permute-start | bytes 73736 | tf_op jit(solution)/shard_map/ppermute | solution.py:205
  51.9 1.3 collective-permute-start.1
  53.2 0.7 copy.28.tmpl
  55.2 1.3 collective-permute-done.1.next_row
  57.1 2.4 shard_map.70
  59.5 1.7 copy.40
  61.2 5.3 %all-to-all-start.2 = ((f32[8,72,128]{2,1,0:T(8,128)}), f32[8,72,128]{2,1,0:T(8,128)S(1)}, u32[]{:S(2)}, u32[]{:S(2)}) async-start(f32[8,72,128]{2,1,0:T(8,128)} %bitcast.31), calls=%async_computation.2 | async-start | bytes 589824 | tf_op jit(solution)/shard_map/all_to_all | solution.py:215
  66.6 0.9 pad_maximum_fusion
  67.4 5.9 %all-to-all-done.2.own = f32[8,72,128]{2,1,0:T(8,128)S(1)} async-done(((f32[8,72,128]{2,1,0:T(8,128)}), f32[8,72,128]{2,1,0:T(8,128)S(1)}, u32[]{:S(2)}, u32[]{:S(2)}) %all-to-all-start.2) | async-done | bytes 294944 | tf_op jit(solution)/shard_map/all_to_all | solution.py:215
  73.3 4.5 %all-to-all-start.1 = ((f32[8,3,2,24,128]{4,3,2,1,0:T(8,128)}), f32[8,3,2,24,128]{4,3,2,1,0:T(8,128)S(1)}, u32[]{:S(2)}, u32[]{:S(2)}) async-start(f32[8,3,2,24,128]{4,3,2,1,0:T(8,128)} %pad_maximum_fusion), calls=%async_computation.1 | async-start | bytes 1179648 | tf_op jit(solution)/shard_map/all_to_all | solution.py:224
  77.8 7.8 %collective-permute-start.7 = (f32[8,72,128]{2,1,0:T(8,128)S(1)}, f32[8,72,128]{2,1,0:T(8,128)S(1)}, u32[]{:S(2)}, u32[]{:S(2)}) collective-permute-start(f32[8,72,128]{2,1,0:T(8,128)S(1)} %all-to-all-done.2.own), channel_id=1, source_target_pairs={{0,2},{2,0},{1,3},{3,1},{4,6},{6,4},{5,7},{7,5},{8,10},{10,8},{9,1... | collective-permute-start | bytes 884744 | tf_op jit(solution)/shard_map/ppermute | solution.py:216
  85.7 0.8 copy.32
  86.5 1.6 all-to-all-done.1.rows
  88.0 27.9 %collective-permute-done.7.other = f32[8,72,128]{2,1,0:T(8,128)S(1)} collective-permute-done((f32[8,72,128]{2,1,0:T(8,128)S(1)}, f32[8,72,128]{2,1,0:T(8,128)S(1)}, u32[]{:S(2)}, u32[]{:S(2)}) %collective-permute-start.7) | collective-permute-done | bytes 294944 | tf_op jit(solution)/shard_map/ppermute | solution.py:216
  115.9 0.7 copy-done.5
  116.6 3.9 %shard_map.71 = f32[32,54,128]{2,1,0:T(8,128)} custom-call(s32[3]{0:T(128)} %pad_add_fusion.place, f32[8,3,2,24,128]{4,3,2,1,0:T(8,128)} %copy-done, f32[8,72,128]{2,1,0:T(8,128)} %copy-done.1, f32[8,72,128]{2,1,0:T(8,128)} %copy-done.5, f32[192,192]{1,0:T(8,128)} %zk.1, f32[192,192]{1,0:T(8,128)} %bitcast.40), custom_call_target="tpu_custom_call" | custom-call | tf_op jit(solution)/shard_map/pallas_call | solution.py:29
  120.6 8.1 %all-to-all-start.3 = ((f32[32,54,128]{2,1,0:T(8,128)}), f32[32,54,128]{2,1,0:T(8,128)S(1)}, u32[]{:S(2)}, u32[]{:S(2)}) async-start(f32[32,54,128]{2,1,0:T(8,128)} %shard_map.71), calls=%async_computation.3 | async-start | bytes 1835008 | tf_op jit(solution)/shard_map/all_to_all | solution.py:235
  128.7 0.6 copy.35
  129.4 1.3 dynamic-slice
  130.7 109.1 %all-reduce.3.cloned.1.call-done = f32[24,8,128]{2,0,1:T(8,128)} async-done(((f32[24,8,128]{2,0,1:T(8,128)}), f32[24,8,128]{2,0,1:T(8,128)}) %all-reduce.3.cloned.1.call-update) | async-done | bytes 98320
  239.8 1.3 constant_dynamic-slice_fusion
  241.1 1.4 constant_dynamic-slice_fusion.1
  243.5 1.1 maximum_bitcast_fusion
  (49 shorter events, 3.6 us)
Async XLA Ops:
  9.2 30.4 %all-to-all-start = ((f32[16,24,128]{2,1,0:T(8,128)}), f32[16,24,128]{2,1,0:T(8,128)S(1)}, u32[]{:S(2)}, u32[]{:S(2)}) async-start(f32[16,24,128]{2,1,0:T(8,128)} %shard_map.68), calls=%async_computation | async-start | bytes 393216 | tf_op jit(solution)/shard_map/all_to_all | solution.py:198
  27.5 27.7 %collective-permute-start.4 = (f32[6,12,8,128]{3,2,1,0:T(8,128)}, f32[6,12,8,128]{3,2,1,0:T(8,128)S(1)}, u32[]{:S(2)}, u32[]{:S(2)}) collective-permute-start(f32[6,12,8,128]{3,2,1,0:T(8,128)} %get-tuple-element.9), channel_id=1, source_target_pairs={{0,128},{128,256},{256,384},{384,0},{1,129},{129,257},{257,385},{3... | collective-permute-start | bytes 884744 | tf_op jit(solution)/shard_map/ppermute | solution.py:202
  30.7 24.5 %collective-permute-start.5 = (f32[6,12,8,128]{3,2,1,0:T(8,128)}, f32[6,12,8,128]{3,2,1,0:T(8,128)S(1)}, u32[]{:S(2)}, u32[]{:S(2)}) collective-permute-start(f32[6,12,8,128]{3,2,1,0:T(8,128)} %get-tuple-element.10), channel_id=1, source_target_pairs={{0,256},{128,384},{256,0},{384,128},{1,257},{129,385},{257,1},{385... | collective-permute-start | bytes 884744 | tf_op jit(solution)/shard_map/ppermute | solution.py:202
  35.2 20.0 %collective-permute-start.6 = (f32[6,12,8,128]{3,2,1,0:T(8,128)}, f32[6,12,8,128]{3,2,1,0:T(8,128)S(1)}, u32[]{:S(2)}, u32[]{:S(2)}) collective-permute-start(f32[6,12,8,128]{3,2,1,0:T(8,128)} %get-tuple-element.11), channel_id=1, source_target_pairs={{0,384},{128,0},{256,128},{384,256},{1,385},{129,1},{257,129},{385... | collective-permute-start | bytes 884744 | tf_op jit(solution)/shard_map/ppermute | solution.py:202
  39.7 9.0 %collective-permute-start.2 = (f32[2,4,8,128]{3,1,0,2:T(4,128)S(1)}, f32[2,4,8,128]{3,1,0,2:T(4,128)S(1)}, u32[]{:S(2)}, u32[]{:S(2)}) collective-permute-start(f32[2,4,8,128]{3,1,0,2:T(4,128)S(1)} %maximum_bitcast_fusion.1), channel_id=1, source_target_pairs={{0,1},{1,0},{2,3},{3,2},{4,5},{5,4},{6,7},{7,6},{8,9},{9,8},{10,11... | collective-permute-start | bytes 98312 | tf_op jit(solution)/shard_map/ppermute | solution.py:208
  45.6 6.3 %collective-permute-start.3 = (f32[2,4,8,128]{3,1,0,2:T(4,128)S(1)}, f32[2,4,8,128]{3,1,0,2:T(4,128)S(1)}, u32[]{:S(2)}, u32[]{:S(2)}) collective-permute-start(f32[2,4,8,128]{3,1,0,2:T(4,128)S(1)} %maximum_bitcast_fusion.1), channel_id=1, source_target_pairs={{1,4},{5,8},{9,12},{4,1},{8,5},{12,9},{3,6},{7,10},{11,14},{6,3},{... | collective-permute-start | bytes 98312 | tf_op jit(solution)/shard_map/ppermute | solution.py:209
  48.7 6.5 %collective-permute-start = (f32[2,24,128]{2,1,0:T(8,128)S(1)}, f32[2,24,128]{2,1,0:T(8,128)S(1)}, u32[]{:S(2)}, u32[]{:S(2)}) collective-permute-start(f32[2,24,128]{2,1,0:T(8,128)S(1)} %get-tuple-element.22), channel_id=1, source_target_pairs={{0,128},{128,256},{256,384},{1,129},{129,257},{257,385},{2,130},{1... | collective-permute-start | bytes 73736 | tf_op jit(solution)/shard_map/ppermute | solution.py:205
  51.9 4.6 %collective-permute-start.1 = (f32[2,24,128]{2,1,0:T(8,128)S(1)}, f32[2,24,128]{2,1,0:T(8,128)S(1)}, u32[]{:S(2)}, u32[]{:S(2)}) collective-permute-start(f32[2,24,128]{2,1,0:T(8,128)S(1)} %get-tuple-element.23), channel_id=1, source_target_pairs={{128,0},{256,128},{384,256},{129,1},{257,129},{385,257},{130,2},{2... | collective-permute-start | bytes 73736 | tf_op jit(solution)/shard_map/ppermute | solution.py:206
  55.2 1.3 copy-start.2
  55.2 1.3 copy-start.3
  55.2 1.3 copy-start.4
  55.2 1.3 copy-start.7
  56.5 0.6 copy-start.9
  59.4 7.1 %copy-start.8 = (f32[2,24,128]{2,1,0:T(8,128)S(1)}, f32[2,24,128]{2,1,0:T(8,128)}, u32[]{:S(2)}) copy-start(f32[2,24,128]{2,1,0:T(8,128)} %copy-done.7) | copy-start | bytes 73732
  59.5 7.1 %copy-start.10 = (f32[2,24,128]{2,1,0:T(8,128)S(1)}, f32[2,24,128]{2,1,0:T(8,128)}, u32[]{:S(2)}) copy-start(f32[2,24,128]{2,1,0:T(8,128)} %copy-done.9) | copy-start | bytes 73732
  61.2 12.1 %all-to-all-start.2 = ((f32[8,72,128]{2,1,0:T(8,128)}), f32[8,72,128]{2,1,0:T(8,128)S(1)}, u32[]{:S(2)}, u32[]{:S(2)}) async-start(f32[8,72,128]{2,1,0:T(8,128)} %bitcast.31), calls=%async_computation.2 | async-start | bytes 589824 | tf_op jit(solution)/shard_map/all_to_all | solution.py:215
  66.5 19.1 %copy-start.6 = (f32[192,192]{1,0:T(8,128)S(1)}, f32[192,192]{1,0:T(8,128)}, u32[]{:S(2)}) copy-start(f32[192,192]{1,0:T(8,128)} %param.9) | copy-start | bytes 442372
  73.3 42.6 %copy-start.1 = (f32[8,72,128]{2,1,0:T(8,128)}, f32[8,72,128]{2,1,0:T(8,128)S(1)}, u32[]{:S(2)}) copy-start(f32[8,72,128]{2,1,0:T(8,128)S(1)} %all-to-all-done.2.own) | copy-start | bytes 884740
  73.3 14.7 %all-to-all-start.1 = ((f32[8,3,2,24,128]{4,3,2,1,0:T(8,128)}), f32[8,3,2,24,128]{4,3,2,1,0:T(8,128)S(1)}, u32[]{:S(2)}, u32[]{:S(2)}) async-start(f32[8,3,2,24,128]{4,3,2,1,0:T(8,128)} %pad_maximum_fusion), calls=%async_computation.1 | async-start | bytes 1179648 | tf_op jit(solution)/shard_map/all_to_all | solution.py:224
  77.8 38.1 %collective-permute-start.7 = (f32[8,72,128]{2,1,0:T(8,128)S(1)}, f32[8,72,128]{2,1,0:T(8,128)S(1)}, u32[]{:S(2)}, u32[]{:S(2)}) collective-permute-start(f32[8,72,128]{2,1,0:T(8,128)S(1)} %all-to-all-done.2.own), channel_id=1, source_target_pairs={{0,2},{2,0},{1,3},{3,1},{4,6},{6,4},{5,7},{7,5},{8,10},{10,8},{9,1... | collective-permute-start | bytes 884744 | tf_op jit(solution)/shard_map/ppermute | solution.py:216
  88.0 27.9 %copy-start = (f32[8,3,2,24,128]{4,3,2,1,0:T(8,128)}, f32[8,3,2,24,128]{4,3,2,1,0:T(8,128)S(1)}, u32[]{:S(2)}) copy-start(f32[8,3,2,24,128]{4,3,2,1,0:T(8,128)S(1)} %all-to-all-done.1.rows) | copy-start | bytes 1769476
  115.9 0.7 copy-start.5
  120.6 8.2 %copy-start.11 = (f32[24,8,128]{2,1,0:T(8,128)S(1)}, f32[24,8,128]{2,1,0:T(8,128)}, u32[]{:S(2)}) copy-start(f32[24,8,128]{2,1,0:T(8,128)} %get-tuple-element.13) | copy-start | bytes 294916
  120.6 121.9 %copy-start.12 = (f32[12,1,192]{2,1,0:T(1,128)S(1)}, f32[12,1,192]{2,1,0:T(1,128)}, u32[]{:S(2)}) copy-start(f32[12,1,192]{2,1,0:T(1,128)} %row.1) | copy-start | bytes 27652
  120.6 122.5 %all-to-all-start.3 = ((f32[32,54,128]{2,1,0:T(8,128)}), f32[32,54,128]{2,1,0:T(8,128)S(1)}, u32[]{:S(2)}, u32[]{:S(2)}) async-start(f32[32,54,128]{2,1,0:T(8,128)} %shard_map.71), calls=%async_computation.3 | async-start | bytes 1835008 | tf_op jit(solution)/shard_map/all_to_all | solution.py:235
  128.7 111.1 %all-reduce.3.cloned.1.call-start = ((), (), s32[]{:S(2)}) async-start(), calls=%async_computation.4 | async-start | bytes 196608
Sparse Core Ops, SparseCore 0:
  132.4 107.2 all-reduce.2

commit v3 on v2

--- a/solution.py
+++ b/solution.py
@@ -115,16 +115,17 @@
     total[12:] = sum_high
 
 
-def main_kernel(place, rows, own, other, zk, xk, out, grid, force, part):
+def main_kernel(place, prev, mine, succ, got, zk, xk, out, grid, force):
     y, zh = place[0], place[1]
-    for r in range(3):
-        grid[r] = jnp.zeros((208, WIDE), F32)
+    for r, ref in enumerate((prev, mine, succ)):
+        grid[r, :8] = jnp.zeros((8, WIDE), F32)
+        grid[r, 200:] = jnp.zeros((8, WIDE), F32)
         for x in range(4):
             for h in range(2):
                 for c in range(2):
                     at = 8 + 48 * x + 24 * h + 12 * c
-                    grid[r, at : at + 12, :LANES] = rows[2 * x + c, r, h, :12]
-                    grid[r, at : at + 12, LANES:] = rows[2 * x + c, r, h, 12:]
+                    grid[r, at : at + 12, :LANES] = ref[2 * x + c, h, :12]
+                    grid[r, at : at + 12, LANES:] = ref[2 * x + c, h, 12:]
     here = grid[1, 8:200]
     low_lane = lax.broadcasted_iota(jnp.int32, (192, LANES), 1) < 64
     slopes = (
@@ -132,19 +133,13 @@
         (grid[2, 8:200] - grid[0, 8:200]) * 0.5,
         (pltpu.roll(here, WIDE - 1, 1) - pltpu.roll(here, 1, 1)) * 0.5,
     )
-    for c, slope in enumerate(slopes):
-        high = slope[:, LANES:]
-        part[c, :, :LANES] = slope[:, :LANES]
-        part[c, :, LANES:] = jnp.where(low_lane, high, pltpu.roll(high, 64, 1))
-
-    for ref, h in ((own, zh), (other, 1 - zh)):
-        for x in range(4):
-            at = pl.ds(pl.multiple_of(48 * x + 24 * h, 8), 24)
-            for b in range(6):
-                r = jnp.concatenate([ref[2 * x, 12 * b : 12 * b + 12], ref[2 * x + 1, 12 * b : 12 * b + 12]], 0)
-                for c in range(3):
-                    s = part[c, at, :LANES] if b < 4 else part[c, at, LANES:]
-                    force[at, (c * 6 + b) * LANES : (c * 6 + b + 1) * LANES] = r * s
+    slopes = [(a[:, :LANES], jnp.where(low_lane, a[:, LANES:], pltpu.roll(a[:, LANES:], 64, 1))) for a in slopes]
+    for k in range(8):
+        at = slice(24 * k, 24 * k + 24)
+        for b in range(6):
+            r = jnp.concatenate([got[2 * k, 12 * b : 12 * b + 12], got[2 * k + 1, 12 * b : 12 * b + 12]], 0)
+            for c in range(3):
+                force[at, (c * 6 + b) * LANES : (c * 6 + b + 1) * LANES] = r * slopes[c][b // 4][at]
 
     def split(a):
         top = a.astype(BF16)
@@ -208,30 +203,34 @@
     by_core = lax.ppermute(ends, "c", [(0, 1), (1, 0)])
     by_x = lax.ppermute(ends, ("x", "c"), [(2 * i + 1, 2 * i + 2) for i in range(3)] + [(2 * i + 2, 2 * i + 1) for i in range(3)])
     tmpl = gathered.transpose(1, 2, 0, 3)
+    mine = lax.all_to_all(gathered, ("x", "c"), 0, 0, tiled=True)
 
     residual, total = call(residual_kernel, (shape(72, 8, LANES), shape(24, 8, LANES)))(
         place, tmpl, prev_row, next_row, by_core, by_x, *raws
     )
-    own = lax.all_to_all(residual.transpose(1, 0, 2), ("x", "c"), 0, 0, tiled=True)
-    other = lax.ppermute(own, "zh", [(0, 1), (1, 0)])
-
-    summed = lax.psum_scatter(total, "zl", scatter_dimension=1, tiled=True)
-    summed = jnp.concatenate([summed[:12], summed[12:, :, :64]], -1)
+    residual, mine = lax.optimization_barrier((residual, mine))
+    by_row = residual.transpose(1, 0, 2).reshape(4, 1, 2, 72, LANES)
+    by_row = jnp.broadcast_to(by_row, (4, 2, 2, 72, LANES)).reshape(16, 72, LANES)
+    got = lax.all_to_all(by_row, ("x", "zh", "c"), 0, 0, tiled=True)
+    along = [(i, i + 1) for i in range(31)]
+    prev = lax.ppermute(mine, ROW, along)
+    succ = lax.ppermute(mine, ROW, [(j, i) for i, j in along])
+
+    total, zl = total.transpose(1, 0, 2), lax.axis_index("zl")
+    for step in (4, 2, 1):
+        high = (zl // step) % 2
+        keep = lax.dynamic_slice_in_dim(total, high * step, step)
+        give = lax.dynamic_slice_in_dim(total, (1 - high) * step, step)
+        total = keep + lax.ppermute(give, "zl", [(i, i ^ step) for i in range(8)])
+    total = total[0]
+    summed = jnp.concatenate([total[:12], total[12:, :64]], -1)[:, None]
     new_template = template + summed / 32
-
-    ten = jnp.concatenate([prev_row[None], gathered, next_row[None]], 0)
-    rows = jnp.stack([ten[i : i + 8] for i in range(3)], 1)
-    rows = lax.all_to_all(rows, ("x", "c"), 0, 0, tiled=True)
 
     (packed,) = call(
         main_kernel,
         (shape(32, 54, LANES),),
-        (
-            pltpu.VMEM((3, 208, WIDE), F32),
-            pltpu.VMEM((192, 18 * LANES), F32),
-            pltpu.VMEM((3, 192, WIDE), F32),
-        ),
-    )(place, rows, own, other, z_kernel, x_kernel.T)
+        (pltpu.VMEM((3, 208, WIDE), F32), pltpu.VMEM((192, 18 * LANES), F32)),
+    )(place, prev, mine, succ, got, z_kernel, x_kernel.T)
     back = lax.all_to_all(packed, ROW, 0, 0, tiled=True)
     low = back[:, :36].reshape(32, 3, 12, LANES)
     high = back[:, 36:].reshape(32, 3, 6, LANES)

time: 256 us -> 148 us (0.58); the launches traced: 251 us -> 146 us
  waiting for transfers between devices: 147 us -> 38 us
  starting transfers between devices: 65.7 us -> 84.3 us
  between operations: 14.3 us -> 1.1 us
    unnamed x2 -> x0, waiting for transfers between devices: 109 us -> none
    all_to_all x1, waiting for transfers between devices: 0.01 us -> 15.1 us  [per_device(): back = lax.all_to_all(packed, ROW, 0, 0, tiled=True)]
    all_to_all x2, starting transfers between devices: 9.82 us -> 19.7 us  [the longest x1 11.4 us: per_device(): got = lax.all_to_all(by_row, ('x', 'zh', 'c'), 0, 0, tiled=True)]
    all_to_all x2, waiting for transfers between devices: 7.47 us -> 0.01 us  [the longest x1 0.01 us: per_device(): mine = lax.all_to_all(gathered, ('x', 'c'), 0, 0, tiled=True)]
    ppermute x1 -> x5, waiting for transfers between devices: 27.9 us -> 21.5 us  [the longest x3 21.5 us: per_device(): total = keep + lax.ppermute(give, 'zl', [(i, i ^ step) for i in range(8)])]
    ppermute x1 -> x5, starting transfers between devices: 7.82 us -> 13.9 us  [the longest x3 8.13 us: per_device(): total = keep + lax.ppermute(give, 'zl', [(i, i ^ step) for i in range(8)])]
    all_to_all x1, starting transfers between devices: 8.1 us -> 13.5 us  [per_device(): back = lax.all_to_all(packed, ROW, 0, 0, tiled=True)]
    ppermute x1, starting transfers between devices: 5.95 us -> 1.92 us  [per_device(): by_core = lax.ppermute(ends, 'c', [(0, 1), (1, 0)])]
  transfers between devices with their start and end apart: 13 -> 16, of which waited for: 6 -> 3; matrix products, arithmetic and copies ran while one was open for 4% -> 5% of each run, Pallas kernels for 1% -> 6%
where the time goes in v3:
time: 148 us; the launch traced here: 146 us
  starting transfers between devices  84.3 us (57%)
  waiting for transfers between devices  38 us (26%)
  local copies, waits for them, and re-layouts  10.5 us (7%)
  Pallas kernels  10.1 us (7%)
  other arithmetic  2.41 us (2%)
    ppermute x3, waiting for transfers between devices, per_device(): total = keep + lax.ppermute(give, 'zl', [(i, i ^ step) for i in range(8)])  21.5 us
    all_to_all x1, starting transfers between devices, per_device(): lax.all_to_all(piece, COL, 0, 0, tiled=True).reshape(8, 2, 24, LANES)  15.8 us
    all_to_all x1, waiting for transfers between devices, per_device(): back = lax.all_to_all(packed, ROW, 0, 0, tiled=True)  15.1 us
    all_to_all x1, starting transfers between devices, per_device(): back = lax.all_to_all(packed, ROW, 0, 0, tiled=True)  13.5 us
    all_to_all x1, starting transfers between devices, per_device(): got = lax.all_to_all(by_row, ('x', 'zh', 'c'), 0, 0, tiled=True)  11.4 us
    ppermute x3, starting transfers between devices, per_device(): lax.ppermute(raws[s], 'y', [(i, (i + s) % 4) for i in range(4)])  10.7 us
    pallas_call x4, Pallas kernels, run(): pl.pallas_call(kernel, out_shape=outs, in_specs=[smem(), *vmem(len(args))...  10.1 us
    all_to_all x1, starting transfers between devices, per_device(): mine = lax.all_to_all(gathered, ('x', 'c'), 0, 0, tiled=True)  8.34 us
  transfers between devices with their start and end apart: 16, of which 3 were waited for; matrix products, arithmetic and copies ran while one was open for 5% of the time, Pallas kernels for 6%

profile of v3, /device:TPU:1, one launch (start us, length us, event | category | flops | bytes accessed | tf_op | source)
XLA Modules:
  0.0 146.4 jit_solution(17319198074454290100)
XLA Ops:
  1.2 1.4 shard_map.68
  2.6 15.8 %all-to-all-start = ((f32[16,24,128]{2,1,0:T(8,128)}), f32[16,24,128]{2,1,0:T(8,128)}, u32[]{:S(2)}, u32[]{:S(2)}) async-start(f32[16,24,128]{2,1,0:T(8,128)} %shard_map.68), calls=%async_computation | async-start | bytes 393216 | tf_op jit(solution)/shard_map/all_to_all | solution.py:193
  18.4 2.6 %shard_map.69 = (f32[6,12,8,128]{3,2,1,0:T(8,128)}, f32[6,12,8,128]{3,2,1,0:T(8,128)}, f32[6,12,8,128]{3,2,1,0:T(8,128)}, f32[6,12,8,128]{3,2,1,0:T(8,128)}) custom-call(s32[3]{0:T(128)} %pad_add_fusion.place, f32[12,32,192]{2,1,0:T(8,128)} %bitcast.34, f32[3,12,32,192]{3,2,1,0:T(8,128)} %bitcast.32), custom_call_target="tpu_custom_call" | custom-call | tf_op jit(solution)/shard_map/pallas_call | solution.py:29
  21.0 3.2 %collective-permute-start.4 = (f32[6,12,8,128]{3,2,1,0:T(8,128)}, f32[6,12,8,128]{3,2,1,0:T(8,128)S(1)}, u32[]{:S(2)}, u32[]{:S(2)}) collective-permute-start(f32[6,12,8,128]{3,2,1,0:T(8,128)} %get-tuple-element.11), channel_id=1, source_target_pairs={{0,128},{128,256},{256,384},{384,0},{1,129},{129,257},{257,385},{3... | collective-permute-start | bytes 884744 | tf_op jit(solution)/shard_map/ppermute | solution.py:197
  24.2 4.5 %collective-permute-start.5 = (f32[6,12,8,128]{3,2,1,0:T(8,128)}, f32[6,12,8,128]{3,2,1,0:T(8,128)S(1)}, u32[]{:S(2)}, u32[]{:S(2)}) collective-permute-start(f32[6,12,8,128]{3,2,1,0:T(8,128)} %get-tuple-element.12), channel_id=1, source_target_pairs={{0,256},{128,384},{256,0},{384,128},{1,257},{129,385},{257,1},{385... | collective-permute-start | bytes 884744 | tf_op jit(solution)/shard_map/ppermute | solution.py:197
  28.7 3.0 %collective-permute-start.6 = (f32[6,12,8,128]{3,2,1,0:T(8,128)}, f32[6,12,8,128]{3,2,1,0:T(8,128)S(1)}, u32[]{:S(2)}, u32[]{:S(2)}) collective-permute-start(f32[6,12,8,128]{3,2,1,0:T(8,128)} %get-tuple-element.13), channel_id=1, source_target_pairs={{0,384},{128,0},{256,128},{384,256},{1,385},{129,1},{257,129},{385... | collective-permute-start | bytes 884744 | tf_op jit(solution)/shard_map/ppermute | solution.py:197
  31.7 1.5 %all-to-all-done = f32[16,24,128]{2,1,0:T(8,128)} async-done(((f32[16,24,128]{2,1,0:T(8,128)}), f32[16,24,128]{2,1,0:T(8,128)}, u32[]{:S(2)}, u32[]{:S(2)}) %all-to-all-start) | async-done | bytes 196640 | tf_op jit(solution)/shard_map/all_to_all | solution.py:193
  33.2 8.3 %all-to-all-start.1 = ((f32[8,2,24,128]{3,2,1,0:T(8,128)}), f32[8,2,24,128]{3,2,1,0:T(8,128)S(1)}, u32[]{:S(2)}, u32[]{:S(2)}) async-start(f32[8,2,24,128]{3,2,1,0:T(8,128)} %bitcast.3), calls=%async_computation.1 | async-start | bytes 393216 | tf_op jit(solution)/shard_map/all_to_all | solution.py:206
  41.5 0.9 slice.52
  42.4 0.9 fusion.2
  43.3 3.5 %collective-permute-start.3 = (f32[2,4,8,128]{3,1,0,2:T(4,128)S(1)}, f32[2,4,8,128]{3,1,0,2:T(4,128)S(1)}, u32[]{:S(2)}, u32[]{:S(2)}) collective-permute-start(f32[2,4,8,128]{3,1,0,2:T(4,128)S(1)} %maximum_bitcast_fusion.1), channel_id=1, source_target_pairs={{1,4},{5,8},{9,12},{4,1},{8,5},{12,9},{3,6},{7,10},{11,14},{6,3},{... | collective-permute-start | bytes 98312 | tf_op jit(solution)/shard_map/ppermute | solution.py:204
  46.9 1.9 %collective-permute-start.2 = (f32[2,4,8,128]{3,1,0,2:T(4,128)S(1)}, f32[2,4,8,128]{3,1,0,2:T(4,128)S(1)}, u32[]{:S(2)}, u32[]{:S(2)}) collective-permute-start(f32[2,4,8,128]{3,1,0,2:T(4,128)S(1)} %maximum_bitcast_fusion.1), channel_id=1, source_target_pairs={{0,1},{1,0},{2,3},{3,2},{4,5},{5,4},{6,7},{7,6},{8,9},{9,8},{10,11... | collective-permute-start | bytes 98312 | tf_op jit(solution)/shard_map/ppermute | solution.py:203
  48.8 0.8 fusion.3
  49.6 1.3 collective-permute-start.1
  50.9 4.0 %collective-permute-start = (f32[2,24,128]{2,1,0:T(8,128)S(1)}, f32[2,24,128]{2,1,0:T(8,128)S(1)}, u32[]{:S(2)}, u32[]{:S(2)}) collective-permute-start(f32[2,24,128]{2,1,0:T(8,128)S(1)} %get-tuple-element.23), channel_id=1, source_target_pairs={{0,128},{128,256},{256,384},{1,129},{129,257},{257,385},{2,130},{1... | collective-permute-start | bytes 73736 | tf_op jit(solution)/shard_map/ppermute | solution.py:200
  54.9 1.7 %copy.16.tmpl = f32[2,24,8,128]{3,2,1,0:T(8,128)} copy(f32[2,24,8,128]{3,1,0,2:T(8,128)} %bitcast.4) | data formatting | bytes 393216 | tf_op jit(solution)/shard_map/transpose | solution.py:205
  57.8 0.6 copy-done.2
  58.7 2.4 %shard_map.70 = (f32[72,8,128]{2,1,0:T(8,128)}, f32[24,8,128]{2,1,0:T(8,128)}) custom-call(s32[3]{0:T(128)} %pad_add_fusion.place, f32[2,24,8,128]{3,2,1,0:T(8,128)} %copy.16.tmpl, f32[2,24,128]{2,1,0:T(8,128)} %copy-done.11, f32[2,24,128]{2,1,0:T(8,128)} %copy-done.10, f32[2,4,8,128]{3,2,1,0:T(8,128)} %copy.17.by_core, f32[2,4,8,128]{3,2,1,0:T(8,128)} %copy.18.by_x, ...), custom_call_target="tpu_custom_call" | custom-call | tf_op jit(solution)/shard_map/pallas_call | solution.py:29
  61.1 1.1 copy.19
  62.2 0.9 broadcast_in_dim.12
  63.1 11.4 %all-to-all-start.2 = ((f32[16,72,128]{2,1,0:T(8,128)}), f32[16,72,128]{2,1,0:T(8,128)S(1)}, u32[]{:S(2)}, u32[]{:S(2)}) async-start(f32[16,72,128]{2,1,0:T(8,128)} %bitcast.10), calls=%async_computation.2 | async-start | bytes 1179648 | tf_op jit(solution)/shard_map/all_to_all | solution.py:214
  74.5 2.2 %collective-permute-start.9 = (f32[4,24,128]{2,0,1:T(4,128)S(1)}, f32[4,24,128]{2,0,1:T(4,128)S(1)}, u32[]{:S(2)}, u32[]{:S(2)}) collective-permute-start(f32[4,24,128]{2,0,1:T(4,128)S(1)} %dynamic-slice_bitcast_fusion), channel_id=1, source_target_pairs={{0,64},{16,80},{32,96},{48,112},{64,0},{80,16},{96,32},{112,48},{1... | collective-permute-start | bytes 147464 | tf_op jit(solution)/shard_map/ppermute | solution.py:224
  76.7 21.5 %collective-permute-done.9 = f32[4,24,128]{2,0,1:T(4,128)S(1)} collective-permute-done((f32[4,24,128]{2,0,1:T(4,128)S(1)}, f32[4,24,128]{2,0,1:T(4,128)S(1)}, u32[]{:S(2)}, u32[]{:S(2)}) %collective-permute-start.9) | collective-permute-done | bytes 49184 | tf_op jit(solution)/shard_map/ppermute | solution.py:224
  98.2 1.9 %collective-permute-start.10 = (f32[2,24,128]{2,0,1:T(2,128)S(1)}, f32[2,24,128]{2,0,1:T(2,128)S(1)}, u32[]{:S(2)}, u32[]{:S(2)}) collective-permute-start(f32[2,24,128]{2,0,1:T(2,128)S(1)} %constant_dynamic-slice_fusion.1), channel_id=1, source_target_pairs={{0,32},{16,48},{32,0},{48,16},{64,96},{80,112},{96,64},{112,80},{1... | collective-permute-start | bytes 73736 | tf_op jit(solution)/shard_map/ppermute | solution.py:224
  100.2 2.5 %collective-permute-start.8 = (f32[8,2,24,128]{3,2,1,0:T(8,128)S(1)}, f32[8,2,24,128]{3,2,1,0:T(8,128)S(1)}, u32[]{:S(2)}, u32[]{:S(2)}) collective-permute-start(f32[8,2,24,128]{3,2,1,0:T(8,128)S(1)} %all-to-all-done.1.mine), channel_id=1, source_target_pairs={{1,0},{4,1},{5,4},{8,5},{9,8},{12,9},{13,12},{128,13},{129,128},{1... | collective-permute-start | bytes 589832 | tf_op jit(solution)/shard_map/ppermute | solution.py:217
  102.6 3.3 %collective-permute-start.7 = (f32[8,2,24,128]{3,2,1,0:T(8,128)S(1)}, f32[8,2,24,128]{3,2,1,0:T(8,128)S(1)}, u32[]{:S(2)}, u32[]{:S(2)}) collective-permute-start(f32[8,2,24,128]{3,2,1,0:T(8,128)S(1)} %all-to-all-done.1.mine), channel_id=1, source_target_pairs={{0,1},{1,4},{4,5},{5,8},{8,9},{9,12},{12,13},{13,128},{128,129},{1... | collective-permute-start | bytes 589832 | tf_op jit(solution)/shard_map/ppermute | solution.py:216
  106.0 4.0 %collective-permute-start.11 = (f32[1,24,128]{2,0,1:T(1,128)S(1)}, f32[1,24,128]{2,0,1:T(1,128)S(1)}, u32[]{:S(2)}, u32[]{:S(2)}) collective-permute-start(f32[1,24,128]{2,0,1:T(1,128)S(1)} %constant_dynamic-slice_fusion), channel_id=1, source_target_pairs={{0,16},{16,0},{32,48},{48,32},{64,80},{80,64},{96,112},{112,96},{1... | collective-permute-start | bytes 36872 | tf_op jit(solution)/shard_map/ppermute | solution.py:224
  110.1 0.8 copy.20
  111.9 3.7 %shard_map.71 = f32[32,54,128]{2,1,0:T(8,128)} custom-call(s32[3]{0:T(128)} %pad_add_fusion.place, f32[8,2,24,128]{3,2,1,0:T(8,128)} %copy-done.7, f32[8,2,24,128]{3,2,1,0:T(8,128)} %copy-done.1, f32[8,2,24,128]{3,2,1,0:T(8,128)} %copy-done.6, f32[16,72,128]{2,1,0:T(8,128)} %copy-done, f32[192,192]{1,0:T(8,128)} %zk.1, f32[192,192]{1,0:T(8,128)} %bitcast.33), custom_call_target="tpu_custom_call" | custom-call | tf_op jit(solution)/shard_map/pallas_call | solution.py:29
  115.6 13.5 %all-to-all-start.3 = ((f32[32,54,128]{2,1,0:T(8,128)}), f32[32,54,128]{2,1,0:T(8,128)S(1)}, u32[]{:S(2)}, u32[]{:S(2)}) async-start(f32[32,54,128]{2,1,0:T(8,128)} %shard_map.71), calls=%async_computation.3 | async-start | bytes 1835008 | tf_op jit(solution)/shard_map/all_to_all | solution.py:234
  129.8 15.1 %all-to-all-done.3 = f32[32,54,128]{2,1,0:T(8,128)S(1)} async-done(((f32[32,54,128]{2,1,0:T(8,128)}), f32[32,54,128]{2,1,0:T(8,128)S(1)}, u32[]{:S(2)}, u32[]{:S(2)}) %all-to-all-start.3) | async-done | bytes 884768 | tf_op jit(solution)/shard_map/all_to_all | solution.py:234
  145.3 1.1 maximum_bitcast_fusion
  (55 shorter events, 4.2 us)
Async XLA Ops:
  2.6 30.5 %all-to-all-start = ((f32[16,24,128]{2,1,0:T(8,128)}), f32[16,24,128]{2,1,0:T(8,128)}, u32[]{:S(2)}, u32[]{:S(2)}) async-start(f32[16,24,128]{2,1,0:T(8,128)} %shard_map.68), calls=%async_computation | async-start | bytes 393216 | tf_op jit(solution)/shard_map/all_to_all | solution.py:193
  21.0 36.8 %collective-permute-start.4 = (f32[6,12,8,128]{3,2,1,0:T(8,128)}, f32[6,12,8,128]{3,2,1,0:T(8,128)S(1)}, u32[]{:S(2)}, u32[]{:S(2)}) collective-permute-start(f32[6,12,8,128]{3,2,1,0:T(8,128)} %get-tuple-element.11), channel_id=1, source_target_pairs={{0,128},{128,256},{256,384},{384,0},{1,129},{129,257},{257,385},{3... | collective-permute-start | bytes 884744 | tf_op jit(solution)/shard_map/ppermute | solution.py:197
  24.2 33.6 %collective-permute-start.5 = (f32[6,12,8,128]{3,2,1,0:T(8,128)}, f32[6,12,8,128]{3,2,1,0:T(8,128)S(1)}, u32[]{:S(2)}, u32[]{:S(2)}) collective-permute-start(f32[6,12,8,128]{3,2,1,0:T(8,128)} %get-tuple-element.12), channel_id=1, source_target_pairs={{0,256},{128,384},{256,0},{384,128},{1,257},{129,385},{257,1},{385... | collective-permute-start | bytes 884744 | tf_op jit(solution)/shard_map/ppermute | solution.py:197
  28.7 29.1 %collective-permute-start.6 = (f32[6,12,8,128]{3,2,1,0:T(8,128)}, f32[6,12,8,128]{3,2,1,0:T(8,128)S(1)}, u32[]{:S(2)}, u32[]{:S(2)}) collective-permute-start(f32[6,12,8,128]{3,2,1,0:T(8,128)} %get-tuple-element.13), channel_id=1, source_target_pairs={{0,384},{128,0},{256,128},{384,256},{1,385},{129,1},{257,129},{385... | collective-permute-start | bytes 884744 | tf_op jit(solution)/shard_map/ppermute | solution.py:197
  33.2 27.9 %all-to-all-start.1 = ((f32[8,2,24,128]{3,2,1,0:T(8,128)}), f32[8,2,24,128]{3,2,1,0:T(8,128)S(1)}, u32[]{:S(2)}, u32[]{:S(2)}) async-start(f32[8,2,24,128]{3,2,1,0:T(8,128)} %bitcast.3), calls=%async_computation.1 | async-start | bytes 393216 | tf_op jit(solution)/shard_map/all_to_all | solution.py:206
  43.3 6.2 %collective-permute-start.3 = (f32[2,4,8,128]{3,1,0,2:T(4,128)S(1)}, f32[2,4,8,128]{3,1,0,2:T(4,128)S(1)}, u32[]{:S(2)}, u32[]{:S(2)}) collective-permute-start(f32[2,4,8,128]{3,1,0,2:T(4,128)S(1)} %maximum_bitcast_fusion.1), channel_id=1, source_target_pairs={{1,4},{5,8},{9,12},{4,1},{8,5},{12,9},{3,6},{7,10},{11,14},{6,3},{... | collective-permute-start | bytes 98312 | tf_op jit(solution)/shard_map/ppermute | solution.py:204
  46.9 4.0 %collective-permute-start.2 = (f32[2,4,8,128]{3,1,0,2:T(4,128)S(1)}, f32[2,4,8,128]{3,1,0,2:T(4,128)S(1)}, u32[]{:S(2)}, u32[]{:S(2)}) collective-permute-start(f32[2,4,8,128]{3,1,0,2:T(4,128)S(1)} %maximum_bitcast_fusion.1), channel_id=1, source_target_pairs={{0,1},{1,0},{2,3},{3,2},{4,5},{5,4},{6,7},{7,6},{8,9},{9,8},{10,11... | collective-permute-start | bytes 98312 | tf_op jit(solution)/shard_map/ppermute | solution.py:203
  49.6 8.2 %collective-permute-start.1 = (f32[2,24,128]{2,1,0:T(8,128)S(1)}, f32[2,24,128]{2,1,0:T(8,128)S(1)}, u32[]{:S(2)}, u32[]{:S(2)}) collective-permute-start(f32[2,24,128]{2,1,0:T(8,128)S(1)} %get-tuple-element.22), channel_id=1, source_target_pairs={{128,0},{256,128},{384,256},{129,1},{257,129},{385,257},{130,2},{2... | collective-permute-start | bytes 73736 | tf_op jit(solution)/shard_map/ppermute | solution.py:201
  50.9 7.0 %collective-permute-start = (f32[2,24,128]{2,1,0:T(8,128)S(1)}, f32[2,24,128]{2,1,0:T(8,128)S(1)}, u32[]{:S(2)}, u32[]{:S(2)}) collective-permute-start(f32[2,24,128]{2,1,0:T(8,128)S(1)} %get-tuple-element.23), channel_id=1, source_target_pairs={{0,128},{128,256},{256,384},{1,129},{129,257},{257,385},{2,130},{1... | collective-permute-start | bytes 73736 | tf_op jit(solution)/shard_map/ppermute | solution.py:200
  57.8 0.7 copy-start.2
  57.8 0.8 copy-start.3
  57.8 0.9 copy-start.4
  57.8 0.9 copy-start.10
  57.8 0.9 copy-start.11
  61.1 41.5 %copy-start.1 = (f32[8,2,24,128]{3,2,1,0:T(8,128)}, f32[8,2,24,128]{3,2,1,0:T(8,128)S(1)}, u32[]{:S(2)}) copy-start(f32[8,2,24,128]{3,2,1,0:T(8,128)S(1)} %all-to-all-done.1.mine) | copy-start | bytes 589828
  62.2 12.2 %copy-start.8 = (f32[24,8,128]{2,1,0:T(8,128)S(1)}, f32[24,8,128]{2,1,0:T(8,128)}, u32[]{:S(2)}) copy-start(f32[24,8,128]{2,1,0:T(8,128)} %get-tuple-element.17) | copy-start | bytes 294916
  62.2 47.9 %copy-start.5 = (f32[192,192]{1,0:T(8,128)S(1)}, f32[192,192]{1,0:T(8,128)}, u32[]{:S(2)}) copy-start(f32[192,192]{1,0:T(8,128)} %param.9) | copy-start | bytes 442372
  63.1 47.8 %all-to-all-start.2 = ((f32[16,72,128]{2,1,0:T(8,128)}), f32[16,72,128]{2,1,0:T(8,128)S(1)}, u32[]{:S(2)}, u32[]{:S(2)}) async-start(f32[16,72,128]{2,1,0:T(8,128)} %bitcast.10), calls=%async_computation.2 | async-start | bytes 1179648 | tf_op jit(solution)/shard_map/all_to_all | solution.py:214
  74.5 23.7 %collective-permute-start.9 = (f32[4,24,128]{2,0,1:T(4,128)S(1)}, f32[4,24,128]{2,0,1:T(4,128)S(1)}, u32[]{:S(2)}, u32[]{:S(2)}) collective-permute-start(f32[4,24,128]{2,0,1:T(4,128)S(1)} %dynamic-slice_bitcast_fusion), channel_id=1, source_target_pairs={{0,64},{16,80},{32,96},{48,112},{64,0},{80,16},{96,32},{112,48},{1... | collective-permute-start | bytes 147464 | tf_op jit(solution)/shard_map/ppermute | solution.py:224
  98.2 7.8 %collective-permute-start.10 = (f32[2,24,128]{2,0,1:T(2,128)S(1)}, f32[2,24,128]{2,0,1:T(2,128)S(1)}, u32[]{:S(2)}, u32[]{:S(2)}) collective-permute-start(f32[2,24,128]{2,0,1:T(2,128)S(1)} %constant_dynamic-slice_fusion.1), channel_id=1, source_target_pairs={{0,32},{16,48},{32,0},{48,16},{64,96},{80,112},{96,64},{112,80},{1... | collective-permute-start | bytes 73736 | tf_op jit(solution)/shard_map/ppermute | solution.py:224
  100.2 10.7 %collective-permute-start.8 = (f32[8,2,24,128]{3,2,1,0:T(8,128)S(1)}, f32[8,2,24,128]{3,2,1,0:T(8,128)S(1)}, u32[]{:S(2)}, u32[]{:S(2)}) collective-permute-start(f32[8,2,24,128]{3,2,1,0:T(8,128)S(1)} %all-to-all-done.1.mine), channel_id=1, source_target_pairs={{1,0},{4,1},{5,4},{8,5},{9,8},{12,9},{13,12},{128,13},{129,128},{1... | collective-permute-start | bytes 589832 | tf_op jit(solution)/shard_map/ppermute | solution.py:217
  102.6 8.2 %collective-permute-start.7 = (f32[8,2,24,128]{3,2,1,0:T(8,128)S(1)}, f32[8,2,24,128]{3,2,1,0:T(8,128)S(1)}, u32[]{:S(2)}, u32[]{:S(2)}) collective-permute-start(f32[8,2,24,128]{3,2,1,0:T(8,128)S(1)} %all-to-all-done.1.mine), channel_id=1, source_target_pairs={{0,1},{1,4},{4,5},{5,8},{8,9},{9,12},{12,13},{13,128},{128,129},{1... | collective-permute-start | bytes 589832 | tf_op jit(solution)/shard_map/ppermute | solution.py:216
  106.0 23.1 %collective-permute-start.11 = (f32[1,24,128]{2,0,1:T(1,128)S(1)}, f32[1,24,128]{2,0,1:T(1,128)S(1)}, u32[]{:S(2)}, u32[]{:S(2)}) collective-permute-start(f32[1,24,128]{2,0,1:T(1,128)S(1)} %constant_dynamic-slice_fusion), channel_id=1, source_target_pairs={{0,16},{16,0},{32,48},{48,32},{64,80},{80,64},{96,112},{112,96},{1... | collective-permute-start | bytes 36872 | tf_op jit(solution)/shard_map/ppermute | solution.py:224
  110.9 0.7 copy-start.6
  110.9 0.8 copy-start.7
  110.9 0.9 copy-start
  115.6 13.6 %copy-start.9 = (f32[12,1,192]{2,1,0:T(1,128)S(1)}, f32[12,1,192]{2,1,0:T(1,128)}, u32[]{:S(2)}) copy-start(f32[12,1,192]{2,1,0:T(1,128)} %row.1) | copy-start | bytes 27652
  115.6 29.3 %all-to-all-start.3 = ((f32[32,54,128]{2,1,0:T(8,128)}), f32[32,54,128]{2,1,0:T(8,128)S(1)}, u32[]{:S(2)}, u32[]{:S(2)}) async-start(f32[32,54,128]{2,1,0:T(8,128)} %shard_map.71), calls=%async_computation.3 | async-start | bytes 1835008 | tf_op jit(solution)/shard_map/all_to_all | solution.py:234

commit v4 on v3

--- a/solution.py
+++ b/solution.py
@@ -57,9 +57,21 @@
             out[4 + k] = jnp.concatenate([first[:, rows, LANES:], second[:, rows, LANES:]], -1)
 
 
+def halo_kernel(place, gathered, tmpl, ends, first, last):
+    for h in range(2):
+        for k in range(3):
+            block = jnp.swapaxes(gathered[:, h, 8 * k : 8 * k + 8], 0, 1)
+            tmpl[h, 8 * k : 8 * k + 8] = block
+            for i, p in enumerate((0, 11, 12, 23)):
+                if p // 8 == k:
+                    ends[h, i] = block[p % 8]
+        first[h] = gathered[0, h]
+        last[h] = gathered[7, h]
+
+
 def residual_kernel(place, tmpl, prev_row, next_row, by_core, by_x, *rest):
-    raws, (out, total) = rest[:4], rest[4:]
-    zh, c = place[1], place[2]
+    raws, out, parts, (rows, total) = rest[:4], rest[4], rest[5:9], rest[9:]
+    zh, c, zl = place[1], place[2], place[3]
     low, high = tmpl[zh, :12], tmpl[zh, 12:]
     here = jnp.concatenate([low, high], -1)
 
@@ -105,18 +117,32 @@
         swap_01, swap_23 = pltpu.roll(zero_one, 64, 2), pltpu.roll(two_three, 64, 2)
         motion = swap_01 * slopes[0][..., LANES:] + two_three * slopes[1][..., LANES:] + swap_23 * slopes[2][..., LANES:]
         r_high = zero_one - (here[..., LANES:] + motion)
-        out[12 * s : 12 * s + 12] = r_low
+        rows[12 * s : 12 * s + 12] = r_low
         highs.append(r_high)
         sum_low += r_low
         sum_high += r_high
     for k in range(2):
-        out[48 + 12 * k : 60 + 12 * k] = jnp.where(lane < 64, highs[2 * k], pltpu.roll(highs[2 * k + 1], 64, 2))
-    total[:12] = sum_low
-    total[12:] = sum_high
-
-
-def main_kernel(place, prev, mine, succ, got, zk, xk, out, grid, force):
-    y, zh = place[0], place[1]
+        rows[48 + 12 * k : 60 + 12 * k] = jnp.where(lane < 64, highs[2 * k], pltpu.roll(highs[2 * k + 1], 64, 2))
+    rows[72:84] = sum_low
+    rows[84:] = sum_high
+    for k in range(12):
+        block = jnp.swapaxes(rows[8 * k : 8 * k + 8], 0, 1)
+        if k >= 9:
+            total[:, 8 * (k - 9) : 8 * (k - 8)] = block
+            continue
+        for i in range(8):
+            x, core = i // 2, i % 2
+            for h in range(2):
+                out[4 * x + 2 * h + core, 8 * k : 8 * k + 8] = block[i]
+    for t, part in enumerate(parts):
+        part[...] = total[pl.ds(2 * lax.bitwise_xor(zl // 2, t), 2)]
+
+
+def main_kernel(place, prev, mine, succ, got, zk, xk, *rest):
+    parts, (out, keep, give, grid, force) = rest[:4], rest[4:]
+    y, zh, odd_row = place[0], place[1], lax.rem(place[3], 2)
+    for ref, i in ((keep, odd_row), (give, 1 - odd_row)):
+        ref[...] = parts[0][i] + parts[1][i] + parts[2][i] + parts[3][i]
     for r, ref in enumerate((prev, mine, succ)):
         grid[r, :8] = jnp.zeros((8, WIDE), F32)
         grid[r, 200:] = jnp.zeros((8, WIDE), F32)
@@ -187,7 +213,7 @@
 
 
 def per_device(image, velocity, template, z_kernel, x_kernel):
-    place = jnp.stack([lax.axis_index(a) for a in ("y", "zh", "c")]).astype(jnp.int32)
+    place = jnp.stack([lax.axis_index(a) for a in ("y", "zh", "c", "zl")]).astype(jnp.int32)
 
     (piece,) = call(piece_kernel, (shape(16, 24, LANES),))(place, template)
     gathered = lax.all_to_all(piece, COL, 0, 0, tiled=True).reshape(8, 2, 24, LANES)
@@ -197,40 +223,40 @@
         lax.ppermute(raws[s], "y", [(i, (i + s) % 4) for i in range(4)]) for s in (1, 2, 3)
     ]
 
-    prev_row = lax.ppermute(gathered[7], "y", [(i, i + 1) for i in range(3)])
-    next_row = lax.ppermute(gathered[0], "y", [(i + 1, i) for i in range(3)])
-    ends = jnp.stack([gathered[:, :, i] for i in (0, 11, 12, 23)], 2).transpose(1, 2, 0, 3)
+    tmpl, ends, first, last = call(
+        halo_kernel,
+        (shape(2, 24, 8, LANES), shape(2, 4, 8, LANES), shape(2, 24, LANES), shape(2, 24, LANES)),
+    )(place, gathered)
     by_core = lax.ppermute(ends, "c", [(0, 1), (1, 0)])
     by_x = lax.ppermute(ends, ("x", "c"), [(2 * i + 1, 2 * i + 2) for i in range(3)] + [(2 * i + 2, 2 * i + 1) for i in range(3)])
-    tmpl = gathered.transpose(1, 2, 0, 3)
+    prev_row = lax.ppermute(last, "y", [(i, i + 1) for i in range(3)])
+    next_row = lax.ppermute(first, "y", [(i + 1, i) for i in range(3)])
+    gathered, by_core = lax.optimization_barrier((gathered, by_core))
     mine = lax.all_to_all(gathered, ("x", "c"), 0, 0, tiled=True)
 
-    residual, total = call(residual_kernel, (shape(72, 8, LANES), shape(24, 8, LANES)))(
-        place, tmpl, prev_row, next_row, by_core, by_x, *raws
-    )
-    residual, mine = lax.optimization_barrier((residual, mine))
-    by_row = residual.transpose(1, 0, 2).reshape(4, 1, 2, 72, LANES)
-    by_row = jnp.broadcast_to(by_row, (4, 2, 2, 72, LANES)).reshape(16, 72, LANES)
+    by_row, *parts = call(
+        residual_kernel,
+        (shape(16, 72, LANES), *[shape(2, 24, LANES)] * 4),
+        (pltpu.VMEM((96, 8, LANES), F32), pltpu.VMEM((8, 24, LANES), F32)),
+    )(place, tmpl, prev_row, next_row, by_core, by_x, *raws)
+    by_row, mine = lax.optimization_barrier((by_row, mine))
     got = lax.all_to_all(by_row, ("x", "zh", "c"), 0, 0, tiled=True)
     along = [(i, i + 1) for i in range(31)]
     prev = lax.ppermute(mine, ROW, along)
     succ = lax.ppermute(mine, ROW, [(j, i) for i, j in along])
 
-    total, zl = total.transpose(1, 0, 2), lax.axis_index("zl")
-    for step in (4, 2, 1):
-        high = (zl // step) % 2
-        keep = lax.dynamic_slice_in_dim(total, high * step, step)
-        give = lax.dynamic_slice_in_dim(total, (1 - high) * step, step)
-        total = keep + lax.ppermute(give, "zl", [(i, i ^ step) for i in range(8)])
-    total = total[0]
+    for t in (1, 2, 3):
+        parts[t] = lax.ppermute(parts[t], "zl", [(i, i ^ (2 * t)) for i in range(8)])
+
+    packed, keep, give = call(
+        main_kernel,
+        (shape(32, 54, LANES), shape(24, LANES), shape(24, LANES)),
+        (pltpu.VMEM((3, 208, WIDE), F32), pltpu.VMEM((192, 18 * LANES), F32)),
+    )(place, prev, mine, succ, got, z_kernel, x_kernel.T, *parts)
+    total = keep + lax.ppermute(give, "zl", [(i, i ^ 1) for i in range(8)])
     summed = jnp.concatenate([total[:12], total[12:, :64]], -1)[:, None]
     new_template = template + summed / 32
 
-    (packed,) = call(
-        main_kernel,
-        (shape(32, 54, LANES),),
-        (pltpu.VMEM((3, 208, WIDE), F32), pltpu.VMEM((192, 18 * LANES), F32)),
-    )(place, prev, mine, succ, got, z_kernel, x_kernel.T)
     back = lax.all_to_all(packed, ROW, 0, 0, tiled=True)
     low = back[:, :36].reshape(32, 3, 12, LANES)
     high = back[:, 36:].reshape(32, 3, 6, LANES)

time: 148 us -> 138 us (0.932)
  waiting for transfers between devices: 38 us -> 25.2 us
  starting transfers between devices: 84.3 us -> 93.6 us
  local copies, waits for them, and re-layouts: 10.5 us -> 3.9 us
  Pallas kernels: 10.1 us -> 12 us
    ppermute x5 -> x6, waiting for transfers between devices: 21.5 us -> 9.63 us  [the longest x3 4.37 us: per_device(): parts[t] = lax.ppermute(parts[t], 'zl', [(i, i ^ 2 * t) for i in range(8)])]
    ppermute x5 -> x6, starting transfers between devices: 13.4 us -> 18.8 us  [the longest x3 11.4 us: per_device(): parts[t] = lax.ppermute(parts[t], 'zl', [(i, i ^ 2 * t) for i in range(8)])]
    all_to_all x1, starting transfers between devices: 13.5 us -> 18.3 us  [per_device(): back = lax.all_to_all(packed, ROW, 0, 0, tiled=True)]
    all_to_all x1, waiting for transfers between devices: 15.1 us -> 10.4 us  [per_device(): back = lax.all_to_all(packed, ROW, 0, 0, tiled=True)]
    ppermute x1, starting transfers between devices: 1.92 us -> 5.94 us  [per_device(): by_core = lax.ppermute(ends, 'c', [(0, 1), (1, 0)])]
    all_to_all x1, starting transfers between devices: 8.34 us -> 4.64 us  [per_device(): mine = lax.all_to_all(gathered, ('x', 'c'), 0, 0, tiled=True)]
    all_to_all x1, waiting for transfers between devices: 0.01 us -> 2.71 us  [per_device(): got = lax.all_to_all(by_row, ('x', 'zh', 'c'), 0, 0, tiled=True)]
    slice x3 -> x0, local copies, waits for them, and re-layouts: 2.53 us -> none  [the longest x2 1.77 us: per_device(): gathered[:, :, i]]
  transfers between devices with their start and end apart: 16 -> 17, of which waited for: 3 -> 8; matrix products, arithmetic and copies ran while one was open for 5% -> 1% of each run, Pallas kernels for 6% -> 5%
where the time goes in v4:
time: 138 us; the launch traced here: 137 us
  starting transfers between devices  93.6 us (68%)
  waiting for transfers between devices  25.2 us (18%)
  Pallas kernels  12 us (9%)
  local copies, waits for them, and re-layouts  3.9 us (3%)
  other arithmetic  1.72 us (1%)
    all_to_all x1, starting transfers between devices, per_device(): back = lax.all_to_all(packed, ROW, 0, 0, tiled=True)  18.3 us
    all_to_all x1, starting transfers between devices, per_device(): lax.all_to_all(piece, COL, 0, 0, tiled=True).reshape(8, 2, 24, LANES)  15.7 us
    pallas_call x5, Pallas kernels, run(): pl.pallas_call(kernel, out_shape=outs, in_specs=[smem(), *vmem(len(args))...  12 us
    ppermute x3, starting transfers between devices, per_device(): parts[t] = lax.ppermute(parts[t], 'zl', [(i, i ^ 2 * t) for i in range(8)])  11.4 us
    ppermute x3, starting transfers between devices, per_device(): lax.ppermute(raws[s], 'y', [(i, (i + s) % 4) for i in range(4)])  10.7 us
    all_to_all x1, starting transfers between devices, per_device(): got = lax.all_to_all(by_row, ('x', 'zh', 'c'), 0, 0, tiled=True)  10.5 us
    all_to_all x1, waiting for transfers between devices, per_device(): back = lax.all_to_all(packed, ROW, 0, 0, tiled=True)  10.4 us
    ppermute x1, starting transfers between devices, per_device(): by_core = lax.ppermute(ends, 'c', [(0, 1), (1, 0)])  5.94 us
  transfers between devices with their start and end apart: 17, of which 8 were waited for; matrix products, arithmetic and copies ran while one was open for 1% of the time, Pallas kernels for 5%

profile of v4, /device:TPU:1, one launch (start us, length us, event | category | flops | bytes accessed | tf_op | source)
XLA Modules:
  0.0 137.4 jit_solution(2549574015937067666)
XLA Ops:
  1.2 1.4 %shard_map.68 = f32[16,24,128]{2,1,0:T(8,128)} custom-call(s32[4]{0:T(128)} %pad_add_fusion.place, f32[12,1,192]{2,1,0:T(1,128)} %row.1), custom_call_target="tpu_custom_call" | custom-call | tf_op jit(solution)/shard_map/pallas_call | solution.py:29
  2.7 15.7 %all-to-all-start = ((f32[16,24,128]{2,1,0:T(8,128)}), f32[16,24,128]{2,1,0:T(8,128)S(1)}, u32[]{:S(2)}, u32[]{:S(2)}) async-start(f32[16,24,128]{2,1,0:T(8,128)} %shard_map.68), calls=%async_computation | async-start | bytes 393216 | tf_op jit(solution)/shard_map/all_to_all | solution.py:219
  18.4 2.6 %shard_map.70 = (f32[6,12,8,128]{3,2,1,0:T(8,128)}, f32[6,12,8,128]{3,2,1,0:T(8,128)}, f32[6,12,8,128]{3,2,1,0:T(8,128)}, f32[6,12,8,128]{3,2,1,0:T(8,128)}) custom-call(s32[4]{0:T(128)} %pad_add_fusion.place, f32[12,32,192]{2,1,0:T(8,128)} %bitcast.24, f32[3,12,32,192]{3,2,1,0:T(8,128)} %bitcast.22), custom_call_target="tpu_custom_call" | custom-call | tf_op jit(solution)/shard_map/pallas_call | solution.py:29
  21.0 3.2 %collective-permute-start.4 = (f32[6,12,8,128]{3,2,1,0:T(8,128)}, f32[6,12,8,128]{3,2,1,0:T(8,128)S(1)}, u32[]{:S(2)}, u32[]{:S(2)}) collective-permute-start(f32[6,12,8,128]{3,2,1,0:T(8,128)} %get-tuple-element.28), channel_id=1, source_target_pairs={{0,128},{128,256},{256,384},{384,0},{1,129},{129,257},{257,385},{3... | collective-permute-start | bytes 884744 | tf_op jit(solution)/shard_map/ppermute | solution.py:223
  24.2 4.5 %collective-permute-start.5 = (f32[6,12,8,128]{3,2,1,0:T(8,128)}, f32[6,12,8,128]{3,2,1,0:T(8,128)S(1)}, u32[]{:S(2)}, u32[]{:S(2)}) collective-permute-start(f32[6,12,8,128]{3,2,1,0:T(8,128)} %get-tuple-element.29), channel_id=1, source_target_pairs={{0,256},{128,384},{256,0},{384,128},{1,257},{129,385},{257,1},{385... | collective-permute-start | bytes 884744 | tf_op jit(solution)/shard_map/ppermute | solution.py:223
  28.7 3.0 %collective-permute-start.6 = (f32[6,12,8,128]{3,2,1,0:T(8,128)}, f32[6,12,8,128]{3,2,1,0:T(8,128)S(1)}, u32[]{:S(2)}, u32[]{:S(2)}) collective-permute-start(f32[6,12,8,128]{3,2,1,0:T(8,128)} %get-tuple-element.30), channel_id=1, source_target_pairs={{0,384},{128,0},{256,128},{384,256},{1,385},{129,1},{257,129},{385... | collective-permute-start | bytes 884744 | tf_op jit(solution)/shard_map/ppermute | solution.py:223
  31.7 1.4 %all-to-all-done = f32[16,24,128]{2,1,0:T(8,128)S(1)} async-done(((f32[16,24,128]{2,1,0:T(8,128)}), f32[16,24,128]{2,1,0:T(8,128)S(1)}, u32[]{:S(2)}, u32[]{:S(2)}) %all-to-all-start) | async-done | bytes 196640 | tf_op jit(solution)/shard_map/all_to_all | solution.py:219
  33.8 1.7 %shard_map.69 = (f32[2,24,8,128]{3,2,1,0:T(8,128)}, f32[2,4,8,128]{3,2,1,0:T(8,128)}, f32[2,24,128]{2,1,0:T(8,128)}, f32[2,24,128]{2,1,0:T(8,128)}) custom-call(s32[4]{0:T(128)} %pad_add_fusion.place, f32[8,2,24,128]{3,2,1,0:T(8,128)} %bitcast.20), custom_call_target="tpu_custom_call" | custom-call | tf_op jit(solution)/shard_map/pallas_call | solution.py:29
  35.4 5.9 %collective-permute-start.2 = (f32[2,4,8,128]{3,2,1,0:T(8,128)}, f32[2,4,8,128]{3,2,1,0:T(8,128)S(1)}, u32[]{:S(2)}, u32[]{:S(2)}) collective-permute-start(f32[2,4,8,128]{3,2,1,0:T(8,128)} %get-tuple-element.25), channel_id=1, source_target_pairs={{0,1},{1,0},{2,3},{3,2},{4,5},{5,4},{6,7},{7,6},{8,9},{9,8},{10,11... | collective-permute-start | bytes 98312 | tf_op jit(solution)/shard_map/ppermute | solution.py:230
  41.4 1.0 collective-permute-done.2.by_core
  42.4 4.6 %all-to-all-start.1 = ((f32[8,2,24,128]{3,2,1,0:T(8,128)}), f32[8,2,24,128]{3,2,1,0:T(8,128)S(1)}, u32[]{:S(2)}, u32[]{:S(2)}) async-start(f32[8,2,24,128]{3,2,1,0:T(8,128)} %bitcast.21), calls=%async_computation.1 | async-start | bytes 393216 | tf_op jit(solution)/shard_map/all_to_all | solution.py:235
  47.1 3.5 %collective-permute-start.3 = (f32[2,4,8,128]{3,2,1,0:T(8,128)}, f32[2,4,8,128]{3,2,1,0:T(8,128)S(1)}, u32[]{:S(2)}, u32[]{:S(2)}) collective-permute-start(f32[2,4,8,128]{3,2,1,0:T(8,128)} %get-tuple-element.25), channel_id=1, source_target_pairs={{1,4},{5,8},{9,12},{4,1},{8,5},{12,9},{3,6},{7,10},{11,14},{6,3},{... | collective-permute-start | bytes 98312 | tf_op jit(solution)/shard_map/ppermute | solution.py:231
  50.6 3.2 %collective-permute-start = (f32[2,24,128]{2,1,0:T(8,128)}, f32[2,24,128]{2,1,0:T(8,128)S(1)}, u32[]{:S(2)}, u32[]{:S(2)}) collective-permute-start(f32[2,24,128]{2,1,0:T(8,128)} %get-tuple-element.23), channel_id=1, source_target_pairs={{0,128},{128,256},{256,384},{1,129},{129,257},{257,385},{2,130},{1... | collective-permute-start | bytes 73736 | tf_op jit(solution)/shard_map/ppermute | solution.py:232
  53.9 1.3 collective-permute-start.1
  55.2 3.4 %collective-permute-done.1.next_row = f32[2,24,128]{2,1,0:T(8,128)S(1)} collective-permute-done((f32[2,24,128]{2,1,0:T(8,128)}, f32[2,24,128]{2,1,0:T(8,128)S(1)}, u32[]{:S(2)}, u32[]{:S(2)}) %collective-permute-start.1) | collective-permute-done | bytes 24608 | tf_op jit(solution)/shard_map/ppermute | solution.py:233
  59.3 2.6 %shard_map.71 = (f32[16,72,128]{2,1,0:T(8,128)}, f32[2,24,128]{2,1,0:T(8,128)}, f32[2,24,128]{2,1,0:T(8,128)}, f32[2,24,128]{2,1,0:T(8,128)}, f32[2,24,128]{2,1,0:T(8,128)}) custom-call(s32[4]{0:T(128)} %pad_add_fusion.place, f32[2,24,8,128]{3,2,1,0:T(8,128)} %get-tuple-element.22.tmpl, f32[2,24,128]{2,1,0:T(8,128)} %copy-done.12, f32[2,24,128]{2,1,0:T(8,128)} %copy-done.16, ...), custom_call_target="tpu_custom_call" | custom-call | tf_op jit(solution)/shard_map/pallas_call | solution.py:29
  61.9 10.5 %all-to-all-start.2 = ((f32[16,72,128]{2,1,0:T(8,128)}), f32[16,72,128]{2,1,0:T(8,128)S(1)}, u32[]{:S(2)}, u32[]{:S(2)}) async-start(f32[16,72,128]{2,1,0:T(8,128)} %get-tuple-element.34), calls=%async_computation.2 | async-start | bytes 1179648 | tf_op jit(solution)/shard_map/all_to_all | solution.py:243
  72.3 3.5 %collective-permute-start.7 = (f32[8,2,24,128]{3,2,1,0:T(8,128)S(1)}, f32[8,2,24,128]{3,2,1,0:T(8,128)S(1)}, u32[]{:S(2)}, u32[]{:S(2)}) collective-permute-start(f32[8,2,24,128]{3,2,1,0:T(8,128)S(1)} %all-to-all-done.1.mine), channel_id=1, source_target_pairs={{0,1},{1,4},{4,5},{5,8},{8,9},{9,12},{12,13},{13,128},{128,129},{1... | collective-permute-start | bytes 589832 | tf_op jit(solution)/shard_map/ppermute | solution.py:245
  75.9 1.9 %collective-permute-start.8 = (f32[8,2,24,128]{3,2,1,0:T(8,128)S(1)}, f32[8,2,24,128]{3,2,1,0:T(8,128)S(1)}, u32[]{:S(2)}, u32[]{:S(2)}) collective-permute-start(f32[8,2,24,128]{3,2,1,0:T(8,128)S(1)} %all-to-all-done.1.mine), channel_id=1, source_target_pairs={{1,0},{4,1},{5,4},{8,5},{9,8},{12,9},{13,12},{128,13},{129,128},{1... | collective-permute-start | bytes 589832 | tf_op jit(solution)/shard_map/ppermute | solution.py:246
  77.8 2.8 %collective-permute-start.10 = (f32[2,24,128]{2,1,0:T(8,128)S(1)}, f32[2,24,128]{2,1,0:T(8,128)S(1)}, u32[]{:S(2)}, u32[]{:S(2)}) collective-permute-start(f32[2,24,128]{2,1,0:T(8,128)S(1)} %copy-done.20), channel_id=1, source_target_pairs={{0,64},{16,80},{32,96},{48,112},{64,0},{80,16},{96,32},{112,48},{1... | collective-permute-start | bytes 73736 | tf_op jit(solution)/shard_map/ppermute | solution.py:249
  80.7 6.4 %collective-permute-start.11 = (f32[2,24,128]{2,1,0:T(8,128)S(1)}, f32[2,24,128]{2,1,0:T(8,128)S(1)}, u32[]{:S(2)}, u32[]{:S(2)}) collective-permute-start(f32[2,24,128]{2,1,0:T(8,128)S(1)} %copy-done.19), channel_id=1, source_target_pairs={{0,96},{16,112},{32,64},{48,80},{64,32},{80,48},{96,0},{112,16},{1... | collective-permute-start | bytes 73736 | tf_op jit(solution)/shard_map/ppermute | solution.py:249
  87.0 2.2 %collective-permute-start.9 = (f32[2,24,128]{2,1,0:T(8,128)S(1)}, f32[2,24,128]{2,1,0:T(8,128)S(1)}, u32[]{:S(2)}, u32[]{:S(2)}) collective-permute-start(f32[2,24,128]{2,1,0:T(8,128)S(1)} %copy-done.18), channel_id=1, source_target_pairs={{0,32},{16,48},{32,0},{48,16},{64,96},{80,112},{96,64},{112,80},{1... | collective-permute-start | bytes 73736 | tf_op jit(solution)/shard_map/ppermute | solution.py:249
  89.2 0.8 copy.13
  90.0 3.7 %collective-permute-done.10.rest_2_ = f32[2,24,128]{2,1,0:T(8,128)S(1)} collective-permute-done((f32[2,24,128]{2,1,0:T(8,128)S(1)}, f32[2,24,128]{2,1,0:T(8,128)S(1)}, u32[]{:S(2)}, u32[]{:S(2)}) %collective-permute-start.10) | collective-permute-done | bytes 24608 | tf_op jit(solution)/shard_map/ppermute | solution.py:249
  94.4 2.7 %all-to-all-done.2.got = f32[16,72,128]{2,1,0:T(8,128)S(1)} async-done(((f32[16,72,128]{2,1,0:T(8,128)}), f32[16,72,128]{2,1,0:T(8,128)S(1)}, u32[]{:S(2)}, u32[]{:S(2)}) %all-to-all-start.2) | async-done | bytes 589856 | tf_op jit(solution)/shard_map/all_to_all | solution.py:243
  97.2 0.8 copy-done
  98.0 3.8 %shard_map.72 = (f32[32,54,128]{2,1,0:T(8,128)}, f32[24,128]{1,0:T(8,128)}, f32[24,128]{1,0:T(8,128)}) custom-call(s32[4]{0:T(128)} %pad_add_fusion.place, f32[8,2,24,128]{3,2,1,0:T(8,128)} %copy-done.6, f32[8,2,24,128]{3,2,1,0:T(8,128)} %copy-done.2, f32[8,2,24,128]{3,2,1,0:T(8,128)} %copy-done.7, f32[16,72,128]{2,1,0:T(8,128)} %copy-done, f32[192,192]{1,0:T(8,128)} %zk.1, ...), custom_call_target="tpu_custom_call" | custom-call | tf_op jit(solution)/shard_map/pallas_call | solution.py:29
  101.7 18.3 %all-to-all-start.3 = ((f32[32,54,128]{2,1,0:T(8,128)}), f32[32,54,128]{2,1,0:T(8,128)S(1)}, u32[]{:S(2)}, u32[]{:S(2)}) async-start(f32[32,54,128]{2,1,0:T(8,128)} %get-tuple-element.39), calls=%async_computation.3 | async-start | bytes 1835008 | tf_op jit(solution)/shard_map/all_to_all | solution.py:260
  120.1 2.9 %collective-permute-start.12 = (f32[24,128]{1,0:T(8,128)S(1)}, f32[24,128]{1,0:T(8,128)S(1)}, u32[]{:S(2)}, u32[]{:S(2)}) collective-permute-start(f32[24,128]{1,0:T(8,128)S(1)} %copy-done.21), channel_id=1, source_target_pairs={{0,16},{16,0},{32,48},{48,32},{64,80},{80,64},{96,112},{112,96},{1... | collective-permute-start | bytes 36872 | tf_op jit(solution)/shard_map/ppermute | solution.py:256
  123.0 1.8 %collective-permute-done.12 = f32[24,128]{1,0:T(8,128)S(1)} collective-permute-done((f32[24,128]{1,0:T(8,128)S(1)}, f32[24,128]{1,0:T(8,128)S(1)}, u32[]{:S(2)}, u32[]{:S(2)}) %collective-permute-start.12) | collective-permute-done | bytes 12320 | tf_op jit(solution)/shard_map/ppermute | solution.py:256
  125.5 10.4 %all-to-all-done.3 = f32[32,54,128]{2,1,0:T(8,128)S(1)} async-done(((f32[32,54,128]{2,1,0:T(8,128)}), f32[32,54,128]{2,1,0:T(8,128)S(1)}, u32[]{:S(2)}, u32[]{:S(2)}) %all-to-all-start.3) | async-done | bytes 884768 | tf_op jit(solution)/shard_map/all_to_all | solution.py:260
  136.3 1.1 maximum_bitcast_fusion
  (64 shorter events, 3.6 us)
Async XLA Ops:
  2.7 30.4 %all-to-all-start = ((f32[16,24,128]{2,1,0:T(8,128)}), f32[16,24,128]{2,1,0:T(8,128)S(1)}, u32[]{:S(2)}, u32[]{:S(2)}) async-start(f32[16,24,128]{2,1,0:T(8,128)} %shard_map.68), calls=%async_computation | async-start | bytes 393216 | tf_op jit(solution)/shard_map/all_to_all | solution.py:219
  21.0 32.9 %collective-permute-start.4 = (f32[6,12,8,128]{3,2,1,0:T(8,128)}, f32[6,12,8,128]{3,2,1,0:T(8,128)S(1)}, u32[]{:S(2)}, u32[]{:S(2)}) collective-permute-start(f32[6,12,8,128]{3,2,1,0:T(8,128)} %get-tuple-element.28), channel_id=1, source_target_pairs={{0,128},{128,256},{256,384},{384,0},{1,129},{129,257},{257,385},{3... | collective-permute-start | bytes 884744 | tf_op jit(solution)/shard_map/ppermute | solution.py:223
  24.2 31.0 %collective-permute-start.5 = (f32[6,12,8,128]{3,2,1,0:T(8,128)}, f32[6,12,8,128]{3,2,1,0:T(8,128)S(1)}, u32[]{:S(2)}, u32[]{:S(2)}) collective-permute-start(f32[6,12,8,128]{3,2,1,0:T(8,128)} %get-tuple-element.29), channel_id=1, source_target_pairs={{0,256},{128,384},{256,0},{384,128},{1,257},{129,385},{257,1},{385... | collective-permute-start | bytes 884744 | tf_op jit(solution)/shard_map/ppermute | solution.py:223
  28.7 26.5 %collective-permute-start.6 = (f32[6,12,8,128]{3,2,1,0:T(8,128)}, f32[6,12,8,128]{3,2,1,0:T(8,128)S(1)}, u32[]{:S(2)}, u32[]{:S(2)}) collective-permute-start(f32[6,12,8,128]{3,2,1,0:T(8,128)} %get-tuple-element.30), channel_id=1, source_target_pairs={{0,384},{128,0},{256,128},{384,256},{1,385},{129,1},{257,129},{385... | collective-permute-start | bytes 884744 | tf_op jit(solution)/shard_map/ppermute | solution.py:223
  35.4 7.0 %collective-permute-start.2 = (f32[2,4,8,128]{3,2,1,0:T(8,128)}, f32[2,4,8,128]{3,2,1,0:T(8,128)S(1)}, u32[]{:S(2)}, u32[]{:S(2)}) collective-permute-start(f32[2,4,8,128]{3,2,1,0:T(8,128)} %get-tuple-element.25), channel_id=1, source_target_pairs={{0,1},{1,0},{2,3},{3,2},{4,5},{5,4},{6,7},{7,6},{8,9},{9,8},{10,11... | collective-permute-start | bytes 98312 | tf_op jit(solution)/shard_map/ppermute | solution.py:230
  42.4 16.2 %copy-start.10 = (f32[2,4,8,128]{3,2,1,0:T(8,128)}, f32[2,4,8,128]{3,2,1,0:T(8,128)S(1)}, u32[]{:S(2)}) copy-start(f32[2,4,8,128]{3,2,1,0:T(8,128)S(1)} %collective-permute-done.2.by_core) | copy-start | bytes 98308
  42.4 19.4 %all-to-all-start.1 = ((f32[8,2,24,128]{3,2,1,0:T(8,128)}), f32[8,2,24,128]{3,2,1,0:T(8,128)S(1)}, u32[]{:S(2)}, u32[]{:S(2)}) async-start(f32[8,2,24,128]{3,2,1,0:T(8,128)} %bitcast.21), calls=%async_computation.1 | async-start | bytes 393216 | tf_op jit(solution)/shard_map/all_to_all | solution.py:235
  47.1 11.6 %collective-permute-start.3 = (f32[2,4,8,128]{3,2,1,0:T(8,128)}, f32[2,4,8,128]{3,2,1,0:T(8,128)S(1)}, u32[]{:S(2)}, u32[]{:S(2)}) collective-permute-start(f32[2,4,8,128]{3,2,1,0:T(8,128)} %get-tuple-element.25), channel_id=1, source_target_pairs={{1,4},{5,8},{9,12},{4,1},{8,5},{12,9},{3,6},{7,10},{11,14},{6,3},{... | collective-permute-start | bytes 98312 | tf_op jit(solution)/shard_map/ppermute | solution.py:231
  50.6 4.6 %collective-permute-start = (f32[2,24,128]{2,1,0:T(8,128)}, f32[2,24,128]{2,1,0:T(8,128)S(1)}, u32[]{:S(2)}, u32[]{:S(2)}) collective-permute-start(f32[2,24,128]{2,1,0:T(8,128)} %get-tuple-element.23), channel_id=1, source_target_pairs={{0,128},{128,256},{256,384},{1,129},{129,257},{257,385},{2,130},{1... | collective-permute-start | bytes 73736 | tf_op jit(solution)/shard_map/ppermute | solution.py:232
  53.8 4.8 %copy-start.3 = (f32[6,12,8,128]{3,2,1,0:T(8,128)}, f32[6,12,8,128]{3,2,1,0:T(8,128)S(1)}, u32[]{:S(2)}) copy-start(f32[6,12,8,128]{3,2,1,0:T(8,128)S(1)} %collective-permute-done.4.rest_1_) | copy-start | bytes 884740
  53.9 4.8 %collective-permute-start.1 = (f32[2,24,128]{2,1,0:T(8,128)}, f32[2,24,128]{2,1,0:T(8,128)S(1)}, u32[]{:S(2)}, u32[]{:S(2)}) collective-permute-start(f32[2,24,128]{2,1,0:T(8,128)} %get-tuple-element.24), channel_id=1, source_target_pairs={{128,0},{256,128},{384,256},{129,1},{257,129},{385,257},{130,2},{2... | collective-permute-start | bytes 73736 | tf_op jit(solution)/shard_map/ppermute | solution.py:233
  55.2 3.5 %copy-start.4 = (f32[6,12,8,128]{3,2,1,0:T(8,128)}, f32[6,12,8,128]{3,2,1,0:T(8,128)S(1)}, u32[]{:S(2)}) copy-start(f32[6,12,8,128]{3,2,1,0:T(8,128)S(1)} %collective-permute-done.5.rest_2_) | copy-start | bytes 884740
  55.2 3.5 %copy-start.5 = (f32[6,12,8,128]{3,2,1,0:T(8,128)}, f32[6,12,8,128]{3,2,1,0:T(8,128)S(1)}, u32[]{:S(2)}) copy-start(f32[6,12,8,128]{3,2,1,0:T(8,128)S(1)} %collective-permute-done.6.rest_3_) | copy-start | bytes 884740
  55.2 3.5 %copy-start.12 = (f32[2,24,128]{2,1,0:T(8,128)}, f32[2,24,128]{2,1,0:T(8,128)S(1)}, u32[]{:S(2)}) copy-start(f32[2,24,128]{2,1,0:T(8,128)S(1)} %collective-permute-done.prev_row) | copy-start | bytes 73732
  59.3 30.0 %copy-start.8 = (f32[192,192]{1,0:T(8,128)S(1)}, f32[192,192]{1,0:T(8,128)}, u32[]{:S(2)}) copy-start(f32[192,192]{1,0:T(8,128)} %param.9) | copy-start | bytes 442372
  61.8 16.0 %copy-start.20 = (f32[2,24,128]{2,1,0:T(8,128)S(1)}, f32[2,24,128]{2,1,0:T(8,128)}, u32[]{:S(2)}) copy-start(f32[2,24,128]{2,1,0:T(8,128)} %get-tuple-element.37) | copy-start | bytes 73732
  61.8 18.8 %copy-start.19 = (f32[2,24,128]{2,1,0:T(8,128)S(1)}, f32[2,24,128]{2,1,0:T(8,128)}, u32[]{:S(2)}) copy-start(f32[2,24,128]{2,1,0:T(8,128)} %get-tuple-element.38) | copy-start | bytes 73732
  61.8 25.2 %copy-start.18 = (f32[2,24,128]{2,1,0:T(8,128)S(1)}, f32[2,24,128]{2,1,0:T(8,128)}, u32[]{:S(2)}) copy-start(f32[2,24,128]{2,1,0:T(8,128)} %get-tuple-element.36) | copy-start | bytes 73732
  61.9 35.3 %copy-start.2 = (f32[8,2,24,128]{3,2,1,0:T(8,128)}, f32[8,2,24,128]{3,2,1,0:T(8,128)S(1)}, u32[]{:S(2)}) copy-start(f32[8,2,24,128]{3,2,1,0:T(8,128)S(1)} %all-to-all-done.1.mine) | copy-start | bytes 589828
  61.9 35.3 %all-to-all-start.2 = ((f32[16,72,128]{2,1,0:T(8,128)}), f32[16,72,128]{2,1,0:T(8,128)S(1)}, u32[]{:S(2)}, u32[]{:S(2)}) async-start(f32[16,72,128]{2,1,0:T(8,128)} %get-tuple-element.34), calls=%async_computation.2 | async-start | bytes 1179648 | tf_op jit(solution)/shard_map/all_to_all | solution.py:243
  72.3 22.1 %collective-permute-start.7 = (f32[8,2,24,128]{3,2,1,0:T(8,128)S(1)}, f32[8,2,24,128]{3,2,1,0:T(8,128)S(1)}, u32[]{:S(2)}, u32[]{:S(2)}) collective-permute-start(f32[8,2,24,128]{3,2,1,0:T(8,128)S(1)} %all-to-all-done.1.mine), channel_id=1, source_target_pairs={{0,1},{1,4},{4,5},{5,8},{8,9},{9,12},{12,13},{13,128},{128,129},{1... | collective-permute-start | bytes 589832 | tf_op jit(solution)/shard_map/ppermute | solution.py:245
  75.9 18.5 %collective-permute-start.8 = (f32[8,2,24,128]{3,2,1,0:T(8,128)S(1)}, f32[8,2,24,128]{3,2,1,0:T(8,128)S(1)}, u32[]{:S(2)}, u32[]{:S(2)}) collective-permute-start(f32[8,2,24,128]{3,2,1,0:T(8,128)S(1)} %all-to-all-done.1.mine), channel_id=1, source_target_pairs={{1,0},{4,1},{5,4},{8,5},{9,8},{12,9},{13,12},{128,13},{129,128},{1... | collective-permute-start | bytes 589832 | tf_op jit(solution)/shard_map/ppermute | solution.py:246
  77.8 15.9 %collective-permute-start.10 = (f32[2,24,128]{2,1,0:T(8,128)S(1)}, f32[2,24,128]{2,1,0:T(8,128)S(1)}, u32[]{:S(2)}, u32[]{:S(2)}) collective-permute-start(f32[2,24,128]{2,1,0:T(8,128)S(1)} %copy-done.20), channel_id=1, source_target_pairs={{0,64},{16,80},{32,96},{48,112},{64,0},{80,16},{96,32},{112,48},{1... | collective-permute-start | bytes 73736 | tf_op jit(solution)/shard_map/ppermute | solution.py:249
  80.7 13.1 %collective-permute-start.11 = (f32[2,24,128]{2,1,0:T(8,128)S(1)}, f32[2,24,128]{2,1,0:T(8,128)S(1)}, u32[]{:S(2)}, u32[]{:S(2)}) collective-permute-start(f32[2,24,128]{2,1,0:T(8,128)S(1)} %copy-done.19), channel_id=1, source_target_pairs={{0,96},{16,112},{32,64},{48,80},{64,32},{80,48},{96,0},{112,16},{1... | collective-permute-start | bytes 73736 | tf_op jit(solution)/shard_map/ppermute | solution.py:249
  87.0 7.4 %collective-permute-start.9 = (f32[2,24,128]{2,1,0:T(8,128)S(1)}, f32[2,24,128]{2,1,0:T(8,128)S(1)}, u32[]{:S(2)}, u32[]{:S(2)}) collective-permute-start(f32[2,24,128]{2,1,0:T(8,128)S(1)} %copy-done.18), channel_id=1, source_target_pairs={{0,32},{16,48},{32,0},{48,16},{64,96},{80,112},{96,64},{112,80},{1... | collective-permute-start | bytes 73736 | tf_op jit(solution)/shard_map/ppermute | solution.py:249
  93.7 3.4 %copy-start.13 = (f32[2,24,128]{2,1,0:T(8,128)}, f32[2,24,128]{2,1,0:T(8,128)S(1)}, u32[]{:S(2)}) copy-start(f32[2,24,128]{2,1,0:T(8,128)S(1)} %collective-permute-done.10.rest_2_) | copy-start | bytes 73732
  93.7 3.4 %copy-start.14 = (f32[2,24,128]{2,1,0:T(8,128)}, f32[2,24,128]{2,1,0:T(8,128)S(1)}, u32[]{:S(2)}) copy-start(f32[2,24,128]{2,1,0:T(8,128)S(1)} %collective-permute-done.11.rest_3_) | copy-start | bytes 73732
  101.7 18.4 %copy-start.21 = (f32[24,128]{1,0:T(8,128)S(1)}, f32[24,128]{1,0:T(8,128)}, u32[]{:S(2)}) copy-start(f32[24,128]{1,0:T(8,128)} %get-tuple-element.41) | copy-start | bytes 36868
  101.7 23.1 %copy-start.17 = (f32[24,128]{1,0:T(8,128)S(1)}, f32[24,128]{1,0:T(8,128)}, u32[]{:S(2)}) copy-start(f32[24,128]{1,0:T(8,128)} %get-tuple-element.40) | copy-start | bytes 36868
  101.7 23.1 %copy-start.9 = (f32[12,1,192]{2,1,0:T(1,128)S(1)}, f32[12,1,192]{2,1,0:T(1,128)}, u32[]{:S(2)}) copy-start(f32[12,1,192]{2,1,0:T(1,128)} %row.1) | copy-start | bytes 27652
  101.7 34.1 %all-to-all-start.3 = ((f32[32,54,128]{2,1,0:T(8,128)}), f32[32,54,128]{2,1,0:T(8,128)S(1)}, u32[]{:S(2)}, u32[]{:S(2)}) async-start(f32[32,54,128]{2,1,0:T(8,128)} %get-tuple-element.39), calls=%async_computation.3 | async-start | bytes 1835008 | tf_op jit(solution)/shard_map/all_to_all | solution.py:260
  120.1 4.7 %collective-permute-start.12 = (f32[24,128]{1,0:T(8,128)S(1)}, f32[24,128]{1,0:T(8,128)S(1)}, u32[]{:S(2)}, u32[]{:S(2)}) collective-permute-start(f32[24,128]{1,0:T(8,128)S(1)} %copy-done.21), channel_id=1, source_target_pairs={{0,16},{16,0},{32,48},{48,32},{64,80},{80,64},{96,112},{112,96},{1... | collective-permute-start | bytes 36872 | tf_op jit(solution)/shard_map/ppermute | solution.py:256
  (7 other events, 11.0 us)

commit v5 on v4

--- a/solution.py
+++ b/solution.py
@@ -26,25 +26,40 @@
 
 def call(kernel, outs, scratch=()):
     def run(place, *args):
+        args = [pltpu.with_memory_space_constraint(a, pltpu.VMEM) for a in args]
+        first = [] if place is None else [place]
         return pl.pallas_call(
             kernel,
             out_shape=outs,
-            in_specs=[smem(), *vmem(len(args))],
+            in_specs=[*([smem()] * len(first)), *vmem(len(args))],
             out_specs=tuple(vmem(len(outs))),
             scratch_shapes=list(scratch),
-        )(place, *args)
+        )(*first, *args)
 
     return run
 
 
-def piece_kernel(place, row, out):
+def piece_kernel(row, out):
     values = row[:, 0, :]
     for i in range(16):
         out[i, :12, :] = values[:, :LANES]
         out[i, 12:, :] = jnp.concatenate([values[:, LANES:], jnp.zeros((12, 64), F32)], 1)
 
 
-def pack_kernel(place, image, velocity, *outs):
+def split(a):
+    top = a.astype(BF16)
+    return top, (a - top.astype(F32)).astype(BF16)
+
+
+def pack_kernel(place, image, velocity, zk, xk, *rest):
+    outs, (zw, xw) = rest[:4], rest[4:]
+    zrows = [zk[pl.ds(pl.multiple_of(48 * x + 24 * place[1], 8), 24), :] for x in range(4)]
+    zw[0], zw[1] = split(jnp.concatenate(zrows, 0))
+    xt = xk[...].T
+    zeros = jnp.zeros((64, 192), F32)
+    for odd in range(2):
+        cols = [xt[:LANES], zeros, xt[LANES:]] if odd else [xt[:LANES], xt[LANES:], zeros]
+        xw[odd, 0], xw[odd, 1] = split(jnp.concatenate(cols, 0))
     for s, out in enumerate(outs):
         at = pl.multiple_of(8 * lax.rem(place[0] + s, 4), 8)
         rows = pl.ds(at, 8)
@@ -138,20 +153,34 @@
         part[...] = total[pl.ds(2 * lax.bitwise_xor(zl // 2, t), 2)]
 
 
-def main_kernel(place, prev, mine, succ, got, zk, xk, *rest):
-    parts, (out, keep, give, grid, force) = rest[:4], rest[4:]
-    y, zh, odd_row = place[0], place[1], lax.rem(place[3], 2)
+def spread_kernel(place, gathered, prev_row, next_row, *rest):
+    outs, ten = rest[:4], rest[4]
+    c, x = place[2], place[4]
+    ten[0] = prev_row[...]
+    ten[1:9] = gathered[...]
+    ten[9] = next_row[...]
+    for t, out in enumerate(outs):
+        for i, core in enumerate((c, 1 - c)):
+            out[i] = ten[pl.ds(2 * lax.rem(x + t, 4) + core, 3)]
+
+
+def main_kernel(place, *refs):
+    rows, (crossed, got, zw, xw), parts = refs[:4], refs[4:8], refs[8:12]
+    out, keep, give, grid, force = refs[12:]
+    y, c, x, odd_row = place[0], place[2], place[4], lax.rem(place[3], 2)
     for ref, i in ((keep, odd_row), (give, 1 - odd_row)):
         ref[...] = parts[0][i] + parts[1][i] + parts[2][i] + parts[3][i]
-    for r, ref in enumerate((prev, mine, succ)):
+
+    for r in range(3):
         grid[r, :8] = jnp.zeros((8, WIDE), F32)
         grid[r, 200:] = jnp.zeros((8, WIDE), F32)
-        for x in range(4):
+        for t in range(4):
             for h in range(2):
-                for c in range(2):
-                    at = 8 + 48 * x + 24 * h + 12 * c
-                    grid[r, at : at + 12, :LANES] = ref[2 * x + c, h, :12]
-                    grid[r, at : at + 12, LANES:] = ref[2 * x + c, h, 12:]
+                mine, other = rows[t][0, r, h], crossed[t, r, h]
+                first, second = jnp.where(c == 0, mine, other), jnp.where(c == 0, other, mine)
+                at = pl.ds(pl.multiple_of(8 + 48 * lax.rem(x + 4 - t, 4) + 24 * h, 8), 24)
+                grid[r, at, :LANES] = jnp.concatenate([first[:12], second[:12]], 0)
+                grid[r, at, LANES:] = jnp.concatenate([first[12:], second[12:]], 0)
     here = grid[1, 8:200]
     low_lane = lax.broadcasted_iota(jnp.int32, (192, LANES), 1) < 64
     slopes = (
@@ -167,25 +196,13 @@
             for c in range(3):
                 force[at, (c * 6 + b) * LANES : (c * 6 + b + 1) * LANES] = r * slopes[c][b // 4][at]
 
-    def split(a):
-        top = a.astype(BF16)
-        return top, (a - top.astype(F32)).astype(BF16)
-
-    def times(a, b):
-        (a1, a0), (b1, b0) = a, b
+    def times(a1, a0, b1, b0):
         dot = lambda p, q: jnp.dot(p, q, preferred_element_type=F32)
         return dot(a1, b1) + (dot(a1, b0) + dot(a0, b1))
 
-    zrows = jnp.concatenate(
-        [zk[pl.ds(pl.multiple_of(48 * x + 24 * zh, 8), 24), :] for x in range(4)], 0
-    )
-    smooth = times(split(zrows), split(force[...]))
-
-    xt = xk[...]
-    zeros = jnp.zeros((64, 192), F32)
+    smooth = times(zw[0], zw[1], *split(force[...]))
+
     for odd in range(2):
-        cols = [xt[:LANES], zeros, xt[LANES:]] if odd else [xt[:LANES], xt[LANES:], zeros]
-        weights = split(jnp.concatenate(cols, 0))
         left = []
         for s in (odd, odd + 2):
             for c in range(3):
@@ -199,7 +216,7 @@
                         1,
                     )
                 )
-        update = times(split(jnp.concatenate(left, 0)), weights)
+        update = times(*split(jnp.concatenate(left, 0)), xw[odd, 0], xw[odd, 1])
         for i, s in enumerate((odd, odd + 2)):
             to = 8 * lax.rem(y + 4 - s, 4)
             for c in range(3):
@@ -213,12 +230,19 @@
 
 
 def per_device(image, velocity, template, z_kernel, x_kernel):
-    place = jnp.stack([lax.axis_index(a) for a in ("y", "zh", "c", "zl")]).astype(jnp.int32)
-
-    (piece,) = call(piece_kernel, (shape(16, 24, LANES),))(place, template)
+    place = jnp.stack([lax.axis_index(a) for a in ("y", "zh", "c", "zl", "x")]).astype(jnp.int32)
+
+    (piece,) = call(piece_kernel, (shape(16, 24, LANES),))(None, template)
     gathered = lax.all_to_all(piece, COL, 0, 0, tiled=True).reshape(8, 2, 24, LANES)
 
-    raws = call(pack_kernel, (shape(6, 12, 8, LANES),) * 4)(place, image[0], velocity[0])
+    *raws, zw, xw = call(
+        pack_kernel,
+        (
+            *[shape(6, 12, 8, LANES)] * 4,
+            jax.ShapeDtypeStruct((2, 96, 192), BF16),
+            jax.ShapeDtypeStruct((2, 2, 256, 192), BF16),
+        ),
+    )(place, image[0], velocity[0], z_kernel, x_kernel)
     raws = [raws[0]] + [
         lax.ppermute(raws[s], "y", [(i, (i + s) % 4) for i in range(4)]) for s in (1, 2, 3)
     ]
@@ -231,19 +255,22 @@
     by_x = lax.ppermute(ends, ("x", "c"), [(2 * i + 1, 2 * i + 2) for i in range(3)] + [(2 * i + 2, 2 * i + 1) for i in range(3)])
     prev_row = lax.ppermute(last, "y", [(i, i + 1) for i in range(3)])
     next_row = lax.ppermute(first, "y", [(i + 1, i) for i in range(3)])
-    gathered, by_core = lax.optimization_barrier((gathered, by_core))
-    mine = lax.all_to_all(gathered, ("x", "c"), 0, 0, tiled=True)
 
     by_row, *parts = call(
         residual_kernel,
         (shape(16, 72, LANES), *[shape(2, 24, LANES)] * 4),
         (pltpu.VMEM((96, 8, LANES), F32), pltpu.VMEM((8, 24, LANES), F32)),
     )(place, tmpl, prev_row, next_row, by_core, by_x, *raws)
-    by_row, mine = lax.optimization_barrier((by_row, mine))
     got = lax.all_to_all(by_row, ("x", "zh", "c"), 0, 0, tiled=True)
-    along = [(i, i + 1) for i in range(31)]
-    prev = lax.ppermute(mine, ROW, along)
-    succ = lax.ppermute(mine, ROW, [(j, i) for i, j in along])
+
+    rows = list(
+        call(spread_kernel, (shape(2, 3, 2, 24, LANES),) * 4, (pltpu.VMEM((10, 2, 24, LANES), F32),))(
+            place, gathered, prev_row, next_row
+        )
+    )
+    for t in (1, 2, 3):
+        rows[t] = lax.ppermute(rows[t], "x", [(i, (i + t) % 4) for i in range(4)])
+    crossed = lax.ppermute(jnp.stack([r[1] for r in rows]), "c", [(0, 1), (1, 0)])
 
     for t in (1, 2, 3):
         parts[t] = lax.ppermute(parts[t], "zl", [(i, i ^ (2 * t)) for i in range(8)])
@@ -252,7 +279,7 @@
         main_kernel,
         (shape(32, 54, LANES), shape(24, LANES), shape(24, LANES)),
         (pltpu.VMEM((3, 208, WIDE), F32), pltpu.VMEM((192, 18 * LANES), F32)),
-    )(place, prev, mine, succ, got, z_kernel, x_kernel.T, *parts)
+    )(place, *rows, crossed, got, zw, xw, *parts)
     total = keep + lax.ppermute(give, "zl", [(i, i ^ 1) for i in range(8)])
     summed = jnp.concatenate([total[:12], total[12:, :64]], -1)[:, None]
     new_template = template + summed / 32

time: 138 us -> 140 us (1.014)
  local copies, waits for them, and re-layouts: 3.9 us -> 9.3 us
  starting transfers between devices: 93.6 us -> 89.2 us
  waiting for transfers between devices: 25.2 us -> 27.3 us
    all_to_all x1, starting transfers between devices: 18.3 us -> 5.87 us  [per_device(): back = lax.all_to_all(packed, ROW, 0, 0, tiled=True)]
    ppermute x2 -> x4, starting transfers between devices: 5.45 us -> 13.6 us  [the longest x3 10.8 us: per_device(): rows[t] = lax.ppermute(rows[t], 'x', [(i, (i + t) % 4) for i in range(4)])]
    all_to_all x1, starting transfers between devices: 10.5 us -> 17.3 us  [per_device(): got = lax.all_to_all(by_row, ('x', 'zh', 'c'), 0, 0, tiled=True)]
    ppermute x2 -> x4, waiting for transfers between devices: 0.01 us -> 4.65 us  [the longest x3 4.65 us: per_device(): rows[t] = lax.ppermute(rows[t], 'x', [(i, (i + t) % 4) for i in range(4)])]
    all_to_all x1 -> x0, starting transfers between devices: 4.64 us -> none  [per_device(): mine = lax.all_to_all(gathered, ('x', 'c'), 0, 0, tiled=True)]
    unnamed x46 -> x35, local copies, waits for them, and re-layouts: 3.49 us -> 7.36 us
    all_to_all x1, waiting for transfers between devices: 2.71 us -> 0.01 us  [per_device(): got = lax.all_to_all(by_row, ('x', 'zh', 'c'), 0, 0, tiled=True)]
    ppermute x1, starting transfers between devices: 5.94 us -> 3.69 us  [per_device(): by_core = lax.ppermute(ends, 'c', [(0, 1), (1, 0)])]
  transfers between devices with their start and end apart: 17 -> 18, of which waited for: 8 -> 7; matrix products, arithmetic and copies ran while one was open for 1% -> 2% of each run, Pallas kernels for 5% -> 4%
where the time goes in v5:
time: 140 us; the launch traced here: 139 us
  starting transfers between devices  89.2 us (64%)
  waiting for transfers between devices  27.3 us (20%)
  Pallas kernels  10.7 us (8%)
  local copies, waits for them, and re-layouts  9.3 us (7%)
    all_to_all x1, starting transfers between devices, per_device(): got = lax.all_to_all(by_row, ('x', 'zh', 'c'), 0, 0, tiled=True)  17.3 us
    all_to_all x1, starting transfers between devices, per_device(): lax.all_to_all(piece, COL, 0, 0, tiled=True).reshape(8, 2, 24, LANES)  15.7 us
    ppermute x3, starting transfers between devices, per_device(): parts[t] = lax.ppermute(parts[t], 'zl', [(i, i ^ 2 * t) for i in range(8)])  13.2 us
    ppermute x3, starting transfers between devices, per_device(): rows[t] = lax.ppermute(rows[t], 'x', [(i, (i + t) % 4) for i in range(4)])  10.8 us
    pallas_call x6, Pallas kernels, run(): pl.pallas_call(kernel, out_shape=outs, in_specs=[*[smem()] * len(first),...  10.7 us
    all_to_all x1, waiting for transfers between devices, per_device(): back = lax.all_to_all(packed, ROW, 0, 0, tiled=True)  10.4 us
    ppermute x3, starting transfers between devices, per_device(): lax.ppermute(raws[s], 'y', [(i, (i + s) % 4) for i in range(4)])  10.1 us
    unnamed x35, local copies, waits for them, and re-layouts  7.36 us
  transfers between devices with their start and end apart: 18, of which 7 were waited for; matrix products, arithmetic and copies ran while one was open for 2% of the time, Pallas kernels for 4%

profile of v5, /device:TPU:1, one launch (start us, length us, event | category | flops | bytes accessed | tf_op | source)
XLA Modules:
  0.0 138.6 jit_solution(10147169713142306552)
XLA Ops:
  2.1 15.7 %all-to-all-start = ((f32[16,24,128]{2,1,0:T(8,128)}), f32[16,24,128]{2,1,0:T(8,128)S(1)}, u32[]{:S(2)}, u32[]{:S(2)}) async-start(f32[16,24,128]{2,1,0:T(8,128)} %shard_map.68), calls=%async_computation | async-start | bytes 393216 | tf_op jit(solution)/shard_map/all_to_all | solution.py:236
  18.4 1.3 copy-done
  19.7 1.0 copy-done.2
  22.6 2.1 %shard_map.71 = (f32[6,12,8,128]{3,2,1,0:T(8,128)}, f32[6,12,8,128]{3,2,1,0:T(8,128)}, f32[6,12,8,128]{3,2,1,0:T(8,128)}, f32[6,12,8,128]{3,2,1,0:T(8,128)}, bf1...) custom-call(s32[5]{0:T(128)} %stack.26.place, f32[12,32,192]{2,1,0:T(8,128)S(1)} %bitcast.21, ...), custom_call_target="tpu_custom_call" | custom-call | tf_op jit(solution)/shard_map/pallas_call | solution.py:31
  24.7 4.6 %collective-permute-start.10 = (f32[6,12,8,128]{3,2,1,0:T(8,128)}, f32[6,12,8,128]{3,2,1,0:T(8,128)S(1)}, u32[]{:S(2)}, u32[]{:S(2)}) collective-permute-start(f32[6,12,8,128]{3,2,1,0:T(8,128)} %get-tuple-element.35), channel_id=1, source_target_pairs={{0,384},{128,0},{256,128},{384,256},{1,385},{129,1},{257,129},{385... | collective-permute-start | bytes 884744 | tf_op jit(solution)/shard_map/ppermute | solution.py:247
  29.3 1.9 %collective-permute-start.8 = (f32[6,12,8,128]{3,2,1,0:T(8,128)}, f32[6,12,8,128]{3,2,1,0:T(8,128)S(1)}, u32[]{:S(2)}, u32[]{:S(2)}) collective-permute-start(f32[6,12,8,128]{3,2,1,0:T(8,128)} %get-tuple-element.33), channel_id=1, source_target_pairs={{0,128},{128,256},{256,384},{384,0},{1,129},{129,257},{257,385},{3... | collective-permute-start | bytes 884744 | tf_op jit(solution)/shard_map/ppermute | solution.py:247
  31.2 3.5 %collective-permute-start.9 = (f32[6,12,8,128]{3,2,1,0:T(8,128)}, f32[6,12,8,128]{3,2,1,0:T(8,128)S(1)}, u32[]{:S(2)}, u32[]{:S(2)}) collective-permute-start(f32[6,12,8,128]{3,2,1,0:T(8,128)} %get-tuple-element.34), channel_id=1, source_target_pairs={{0,256},{128,384},{256,0},{384,128},{1,257},{129,385},{257,1},{385... | collective-permute-start | bytes 884744 | tf_op jit(solution)/shard_map/ppermute | solution.py:247
  34.8 1.4 %shard_map.69 = (f32[2,24,8,128]{3,2,1,0:T(8,128)}, f32[2,4,8,128]{3,2,1,0:T(8,128)}, f32[2,24,128]{2,1,0:T(8,128)}, f32[2,24,128]{2,1,0:T(8,128)}) custom-call(s32[5]{0:T(128)} %stack.26.place, f32[8,2,24,128]{3,2,1,0:T(8,128)S(1)} %bitcast.18), custom_call_target="tpu_custom_call" | custom-call | tf_op jit(solution)/shard_map/pallas_call | solution.py:31
  36.2 3.7 %collective-permute-start.6 = (f32[2,4,8,128]{3,2,1,0:T(8,128)}, f32[2,4,8,128]{3,2,1,0:T(8,128)S(1)}, u32[]{:S(2)}, u32[]{:S(2)}) collective-permute-start(f32[2,4,8,128]{3,2,1,0:T(8,128)} %get-tuple-element.31), channel_id=1, source_target_pairs={{0,1},{1,0},{2,3},{3,2},{4,5},{5,4},{6,7},{7,6},{8,9},{9,8},{10,11... | collective-permute-start | bytes 98312 | tf_op jit(solution)/shard_map/ppermute | solution.py:254
  39.9 3.0 %collective-permute-start.7 = (f32[2,4,8,128]{3,2,1,0:T(8,128)}, f32[2,4,8,128]{3,2,1,0:T(8,128)S(1)}, u32[]{:S(2)}, u32[]{:S(2)}) collective-permute-start(f32[2,4,8,128]{3,2,1,0:T(8,128)} %get-tuple-element.31), channel_id=1, source_target_pairs={{1,4},{5,8},{9,12},{4,1},{8,5},{12,9},{3,6},{7,10},{11,14},{6,3},{... | collective-permute-start | bytes 98312 | tf_op jit(solution)/shard_map/ppermute | solution.py:255
  42.9 3.5 %collective-permute-start = (f32[2,24,128]{2,1,0:T(8,128)}, f32[2,24,128]{2,1,0:T(8,128)S(1)}, u32[]{:S(2)}, u32[]{:S(2)}) collective-permute-start(f32[2,24,128]{2,1,0:T(8,128)} %get-tuple-element.24), channel_id=1, source_target_pairs={{0,128},{128,256},{256,384},{1,129},{129,257},{257,385},{2,130},{1... | collective-permute-start | bytes 73736 | tf_op jit(solution)/shard_map/ppermute | solution.py:256
  46.5 1.3 collective-permute-start.1
  47.8 3.5 %collective-permute-done.1.next_row = f32[2,24,128]{2,1,0:T(8,128)S(1)} collective-permute-done((f32[2,24,128]{2,1,0:T(8,128)}, f32[2,24,128]{2,1,0:T(8,128)S(1)}, u32[]{:S(2)}, u32[]{:S(2)}) %collective-permute-start.1) | collective-permute-done | bytes 24608 | tf_op jit(solution)/shard_map/ppermute | solution.py:257
  53.1 1.8 %shard_map.72 = (f32[16,72,128]{2,1,0:T(8,128)}, f32[2,24,128]{2,1,0:T(8,128)}, f32[2,24,128]{2,1,0:T(8,128)}, f32[2,24,128]{2,1,0:T(8,128)}, f32[2,24,128]{2,1,0:T(8,128)}) custom-call(s32[5]{0:T(128)} %stack.26.place, f32[2,24,8,128]{3,2,1,0:T(8,128)S(1)} %copy-done.7, f32[2,24,128]{2,1,0:T(8,128)S(1)} %collective-permute-done.prev_row, ...), custom_call_target="tpu_custom_call" | custom-call | tf_op jit(solution)/shard_map/pallas_call | solution.py:31
  55.0 17.3 %all-to-all-start.1 = ((f32[16,72,128]{2,1,0:T(8,128)}), f32[16,72,128]{2,1,0:T(8,128)S(1)}, u32[]{:S(2)}, u32[]{:S(2)}) async-start(f32[16,72,128]{2,1,0:T(8,128)} %get-tuple-element.36), calls=%async_computation.1 | async-start | bytes 1179648 | tf_op jit(solution)/shard_map/all_to_all | solution.py:264
  72.3 1.5 %shard_map.70 = (f32[2,3,2,24,128]{4,3,2,1,0:T(8,128)}, f32[2,3,2,24,128]{4,3,2,1,0:T(8,128)}, f32[2,3,2,24,128]{4,3,2,1,0:T(8,128)}, f32[2,3,2,24,128]{4,3,2,1,0:T(8,128)}) custom-call(s32[5]{0:T(128)} %stack.26.place, f32[8,2,24,128]{3,2,1,0:T(8,128)S(1)} %bitcast.19, f32[2,24,128]{2,1,0:T(8,128)S(1)} %collective-permute-done.prev_row, ...), custom_call_target="tpu_custom_call" | custom-call | tf_op jit(solution)/shard_map/pallas_call | solution.py:31
  73.8 3.4 %collective-permute-start.2 = (f32[2,3,2,24,128]{4,3,2,1,0:T(8,128)}, f32[2,3,2,24,128]{4,3,2,1,0:T(8,128)S(1)}, u32[]{:S(2)}, u32[]{:S(2)}) collective-permute-start(f32[2,3,2,24,128]{4,3,2,1,0:T(8,128)} %get-tuple-element.27), channel_id=1, source_target_pairs={{0,4},{4,8},{8,12},{12,0},{1,5},{5,9},{9,13},{13,1},{2,6},{6,10},{... | collective-permute-start | bytes 442376 | tf_op jit(solution)/shard_map/ppermute | solution.py:272
  77.3 4.3 %collective-permute-start.3 = (f32[2,3,2,24,128]{4,3,2,1,0:T(8,128)}, f32[2,3,2,24,128]{4,3,2,1,0:T(8,128)S(1)}, u32[]{:S(2)}, u32[]{:S(2)}) collective-permute-start(f32[2,3,2,24,128]{4,3,2,1,0:T(8,128)} %get-tuple-element.28), channel_id=1, source_target_pairs={{0,8},{4,12},{8,0},{12,4},{1,9},{5,13},{9,1},{13,5},{2,10},{6,14},... | collective-permute-start | bytes 442376 | tf_op jit(solution)/shard_map/ppermute | solution.py:272
  81.6 3.1 %collective-permute-start.4 = (f32[2,3,2,24,128]{4,3,2,1,0:T(8,128)}, f32[2,3,2,24,128]{4,3,2,1,0:T(8,128)S(1)}, u32[]{:S(2)}, u32[]{:S(2)}) collective-permute-start(f32[2,3,2,24,128]{4,3,2,1,0:T(8,128)} %get-tuple-element.29), channel_id=1, source_target_pairs={{0,12},{4,0},{8,4},{12,8},{1,13},{5,1},{9,5},{13,9},{2,14},{6,2},{... | collective-permute-start | bytes 442376 | tf_op jit(solution)/shard_map/ppermute | solution.py:272
  85.6 1.3 collective-permute-done.3.refs_2_
  86.8 3.4 %collective-permute-done.4.refs_3_ = f32[2,3,2,24,128]{4,3,2,1,0:T(8,128)S(1)} collective-permute-done((f32[2,3,2,24,128]{4,3,2,1,0:T(8,128)}, f32[2,3,2,24,128]{4,3,2,1,0:T(8,128)S(1)}, u32[]{:S(2)}, u32[]{:S(2)}) %collective-permute-start.4) | collective-permute-done | bytes 147488 | tf_op jit(solution)/shard_map/ppermute | solution.py:272
  90.3 2.7 %collective-permute-start.5 = (f32[4,3,2,24,128]{4,3,2,1,0:T(8,128)S(1)}, f32[4,3,2,24,128]{4,3,2,1,0:T(8,128)S(1)}, u32[]{:S(2)}, u32[]{:S(2)}) collective-permute-start(f32[4,3,2,24,128]{4,3,2,1,0:T(8,128)S(1)} %pad_maximum_fusion), channel_id=1, source_target_pairs={{0,1},{1,0},{2,3},{3,2},{4,5},{5,4},{6,7},{7,6},{8,9},{9,8},{10,11... | collective-permute-start | bytes 884744 | tf_op jit(solution)/shard_map/ppermute | solution.py:273
  93.0 2.0 %collective-permute-start.11 = (f32[2,24,128]{2,1,0:T(8,128)S(1)}, f32[2,24,128]{2,1,0:T(8,128)S(1)}, u32[]{:S(2)}, u32[]{:S(2)}) collective-permute-start(f32[2,24,128]{2,1,0:T(8,128)S(1)} %copy-done.15), channel_id=1, source_target_pairs={{0,32},{16,48},{32,0},{48,16},{64,96},{80,112},{96,64},{112,80},{1... | collective-permute-start | bytes 73736 | tf_op jit(solution)/shard_map/ppermute | solution.py:276
  95.1 2.1 %collective-permute-start.12 = (f32[2,24,128]{2,1,0:T(8,128)S(1)}, f32[2,24,128]{2,1,0:T(8,128)S(1)}, u32[]{:S(2)}, u32[]{:S(2)}) collective-permute-start(f32[2,24,128]{2,1,0:T(8,128)S(1)} %copy-done.14), channel_id=1, source_target_pairs={{0,64},{16,80},{32,96},{48,112},{64,0},{80,16},{96,32},{112,48},{1... | collective-permute-start | bytes 73736 | tf_op jit(solution)/shard_map/ppermute | solution.py:276
  97.1 9.1 %collective-permute-start.13 = (f32[2,24,128]{2,1,0:T(8,128)S(1)}, f32[2,24,128]{2,1,0:T(8,128)S(1)}, u32[]{:S(2)}, u32[]{:S(2)}) collective-permute-start(f32[2,24,128]{2,1,0:T(8,128)S(1)} %copy-done.13), channel_id=1, source_target_pairs={{0,96},{16,112},{32,64},{48,80},{64,32},{80,48},{96,0},{112,16},{1... | collective-permute-start | bytes 73736 | tf_op jit(solution)/shard_map/ppermute | solution.py:276
  106.3 5.0 %collective-permute-done.12.refs_10_ = f32[2,24,128]{2,1,0:T(8,128)S(1)} collective-permute-done((f32[2,24,128]{2,1,0:T(8,128)S(1)}, f32[2,24,128]{2,1,0:T(8,128)S(1)}, u32[]{:S(2)}, u32[]{:S(2)}) %collective-permute-start.12) | collective-permute-done | bytes 24608 | tf_op jit(solution)/shard_map/ppermute | solution.py:276
  112.3 3.1 %shard_map.73 = (f32[32,54,128]{2,1,0:T(8,128)}, f32[24,128]{1,0:T(8,128)}, f32[24,128]{1,0:T(8,128)}) custom-call(s32[5]{0:T(128)} %stack.26.place, f32[2,3,2,24,128]{4,3,2,1,0:T(8,128)S(1)} %copy-done.3, f32[2,3,2,24,128]{4,3,2,1,0:T(8,128)S(1)} %collective-permute-done.2.refs_1_, f32[2,3,2,24,128]{4,3,2,1,0:T(8,128)S(1)} %collective-permute-done.3.refs_2_, ...), custom_call_target="tpu_custom_call" | custom-call | tf_op jit(solution)/shard_map/pallas_call | solution.py:31
  115.4 5.9 %all-to-all-start.2 = ((f32[32,54,128]{2,1,0:T(8,128)}), f32[32,54,128]{2,1,0:T(8,128)S(1)}, u32[]{:S(2)}, u32[]{:S(2)}) async-start(f32[32,54,128]{2,1,0:T(8,128)} %get-tuple-element.43), calls=%async_computation.2 | async-start | bytes 1835008 | tf_op jit(solution)/shard_map/all_to_all | solution.py:287
  121.3 1.9 %collective-permute-start.14 = (f32[24,128]{1,0:T(8,128)S(1)}, f32[24,128]{1,0:T(8,128)S(1)}, u32[]{:S(2)}, u32[]{:S(2)}) collective-permute-start(f32[24,128]{1,0:T(8,128)S(1)} %copy-done.16), channel_id=1, source_target_pairs={{0,16},{16,0},{32,48},{48,32},{64,80},{80,64},{96,112},{112,96},{1... | collective-permute-start | bytes 36872 | tf_op jit(solution)/shard_map/ppermute | solution.py:283
  123.2 2.8 %collective-permute-done.14 = f32[24,128]{1,0:T(8,128)S(1)} collective-permute-done((f32[24,128]{1,0:T(8,128)S(1)}, f32[24,128]{1,0:T(8,128)S(1)}, u32[]{:S(2)}, u32[]{:S(2)}) %collective-permute-start.14) | collective-permute-done | bytes 12320 | tf_op jit(solution)/shard_map/ppermute | solution.py:283
  126.7 10.4 %all-to-all-done.2 = f32[32,54,128]{2,1,0:T(8,128)S(1)} async-done(((f32[32,54,128]{2,1,0:T(8,128)}), f32[32,54,128]{2,1,0:T(8,128)S(1)}, u32[]{:S(2)}, u32[]{:S(2)}) %all-to-all-start.2) | async-done | bytes 884768 | tf_op jit(solution)/shard_map/all_to_all | solution.py:287
  137.5 1.1 maximum_bitcast_fusion
  (61 shorter events, 8.8 us)
Async XLA Ops:
  2.1 32.7 %all-to-all-start = ((f32[16,24,128]{2,1,0:T(8,128)}), f32[16,24,128]{2,1,0:T(8,128)S(1)}, u32[]{:S(2)}, u32[]{:S(2)}) async-start(f32[16,24,128]{2,1,0:T(8,128)} %shard_map.68), calls=%async_computation | async-start | bytes 393216 | tf_op jit(solution)/shard_map/all_to_all | solution.py:236
  18.4 1.3 copy-start
  19.7 1.0 copy-start.2
  20.7 0.9 copy-start.5
  24.7 18.3 %collective-permute-start.10 = (f32[6,12,8,128]{3,2,1,0:T(8,128)}, f32[6,12,8,128]{3,2,1,0:T(8,128)S(1)}, u32[]{:S(2)}, u32[]{:S(2)}) collective-permute-start(f32[6,12,8,128]{3,2,1,0:T(8,128)} %get-tuple-element.35), channel_id=1, source_target_pairs={{0,384},{128,0},{256,128},{384,256},{1,385},{129,1},{257,129},{385... | collective-permute-start | bytes 884744 | tf_op jit(solution)/shard_map/ppermute | solution.py:247
  29.3 17.2 %collective-permute-start.8 = (f32[6,12,8,128]{3,2,1,0:T(8,128)}, f32[6,12,8,128]{3,2,1,0:T(8,128)S(1)}, u32[]{:S(2)}, u32[]{:S(2)}) collective-permute-start(f32[6,12,8,128]{3,2,1,0:T(8,128)} %get-tuple-element.33), channel_id=1, source_target_pairs={{0,128},{128,256},{256,384},{384,0},{1,129},{129,257},{257,385},{3... | collective-permute-start | bytes 884744 | tf_op jit(solution)/shard_map/ppermute | solution.py:247
  31.2 16.5 %collective-permute-start.9 = (f32[6,12,8,128]{3,2,1,0:T(8,128)}, f32[6,12,8,128]{3,2,1,0:T(8,128)S(1)}, u32[]{:S(2)}, u32[]{:S(2)}) collective-permute-start(f32[6,12,8,128]{3,2,1,0:T(8,128)} %get-tuple-element.34), channel_id=1, source_target_pairs={{0,256},{128,384},{256,0},{384,128},{1,257},{129,385},{257,1},{385... | collective-permute-start | bytes 884744 | tf_op jit(solution)/shard_map/ppermute | solution.py:247
  36.2 15.1 %collective-permute-start.6 = (f32[2,4,8,128]{3,2,1,0:T(8,128)}, f32[2,4,8,128]{3,2,1,0:T(8,128)S(1)}, u32[]{:S(2)}, u32[]{:S(2)}) collective-permute-start(f32[2,4,8,128]{3,2,1,0:T(8,128)} %get-tuple-element.31), channel_id=1, source_target_pairs={{0,1},{1,0},{2,3},{3,2},{4,5},{5,4},{6,7},{7,6},{8,9},{9,8},{10,11... | collective-permute-start | bytes 98312 | tf_op jit(solution)/shard_map/ppermute | solution.py:254
  39.9 11.4 %collective-permute-start.7 = (f32[2,4,8,128]{3,2,1,0:T(8,128)}, f32[2,4,8,128]{3,2,1,0:T(8,128)S(1)}, u32[]{:S(2)}, u32[]{:S(2)}) collective-permute-start(f32[2,4,8,128]{3,2,1,0:T(8,128)} %get-tuple-element.31), channel_id=1, source_target_pairs={{1,4},{5,8},{9,12},{4,1},{8,5},{12,9},{3,6},{7,10},{11,14},{6,3},{... | collective-permute-start | bytes 98312 | tf_op jit(solution)/shard_map/ppermute | solution.py:255
  42.9 4.8 %collective-permute-start = (f32[2,24,128]{2,1,0:T(8,128)}, f32[2,24,128]{2,1,0:T(8,128)S(1)}, u32[]{:S(2)}, u32[]{:S(2)}) collective-permute-start(f32[2,24,128]{2,1,0:T(8,128)} %get-tuple-element.24), channel_id=1, source_target_pairs={{0,128},{128,256},{256,384},{1,129},{129,257},{257,385},{2,130},{1... | collective-permute-start | bytes 73736 | tf_op jit(solution)/shard_map/ppermute | solution.py:256
  46.5 4.8 %collective-permute-start.1 = (f32[2,24,128]{2,1,0:T(8,128)}, f32[2,24,128]{2,1,0:T(8,128)S(1)}, u32[]{:S(2)}, u32[]{:S(2)}) collective-permute-start(f32[2,24,128]{2,1,0:T(8,128)} %get-tuple-element.25), channel_id=1, source_target_pairs={{128,0},{256,128},{384,256},{129,1},{257,129},{385,257},{130,2},{2... | collective-permute-start | bytes 73736 | tf_op jit(solution)/shard_map/ppermute | solution.py:257
  51.3 1.0 copy-start.4
  55.0 38.0 %copy-start.15 = (f32[2,24,128]{2,1,0:T(8,128)S(1)}, f32[2,24,128]{2,1,0:T(8,128)}, u32[]{:S(2)}) copy-start(f32[2,24,128]{2,1,0:T(8,128)} %get-tuple-element.40) | copy-start | bytes 73732
  55.0 40.1 %copy-start.14 = (f32[2,24,128]{2,1,0:T(8,128)S(1)}, f32[2,24,128]{2,1,0:T(8,128)}, u32[]{:S(2)}) copy-start(f32[2,24,128]{2,1,0:T(8,128)} %get-tuple-element.41) | copy-start | bytes 73732
  55.0 42.2 %copy-start.13 = (f32[2,24,128]{2,1,0:T(8,128)S(1)}, f32[2,24,128]{2,1,0:T(8,128)}, u32[]{:S(2)}) copy-start(f32[2,24,128]{2,1,0:T(8,128)} %get-tuple-element.42) | copy-start | bytes 73732
  55.0 57.3 %copy-start.1 = (bf16[2,2,256,192]{3,2,1,0:T(8,128)(2,1)S(1)}, bf16[2,2,256,192]{3,2,1,0:T(8,128)(2,1)}, u32[]{:S(2)}) copy-start(bf16[2,2,256,192]{3,2,1,0:T(8,128)(2,1)} %get-tuple-element.38.refs_7_) | copy-start | bytes 1179652
  55.0 57.3 %copy-start.8 = (bf16[2,96,192]{2,1,0:T(8,128)(2,1)S(1)}, bf16[2,96,192]{2,1,0:T(8,128)(2,1)}, u32[]{:S(2)}) copy-start(bf16[2,96,192]{2,1,0:T(8,128)(2,1)} %get-tuple-element.37.refs_6_) | copy-start | bytes 221188
  55.0 57.3 %copy-start.11 = (f32[2,24,128]{2,1,0:T(8,128)S(1)}, f32[2,24,128]{2,1,0:T(8,128)}, u32[]{:S(2)}) copy-start(f32[2,24,128]{2,1,0:T(8,128)} %get-tuple-element.39.refs_8_) | copy-start | bytes 73732
  55.0 57.2 %all-to-all-start.1 = ((f32[16,72,128]{2,1,0:T(8,128)}), f32[16,72,128]{2,1,0:T(8,128)S(1)}, u32[]{:S(2)}, u32[]{:S(2)}) async-start(f32[16,72,128]{2,1,0:T(8,128)} %get-tuple-element.36), calls=%async_computation.1 | async-start | bytes 1179648 | tf_op jit(solution)/shard_map/all_to_all | solution.py:264
  73.8 38.4 %copy-start.3 = (f32[2,3,2,24,128]{4,3,2,1,0:T(8,128)S(1)}, f32[2,3,2,24,128]{4,3,2,1,0:T(8,128)}, u32[]{:S(2)}) copy-start(f32[2,3,2,24,128]{4,3,2,1,0:T(8,128)} %get-tuple-element.26.refs_0_) | copy-start | bytes 442372
  73.8 11.7 %collective-permute-start.2 = (f32[2,3,2,24,128]{4,3,2,1,0:T(8,128)}, f32[2,3,2,24,128]{4,3,2,1,0:T(8,128)S(1)}, u32[]{:S(2)}, u32[]{:S(2)}) collective-permute-start(f32[2,3,2,24,128]{4,3,2,1,0:T(8,128)} %get-tuple-element.27), channel_id=1, source_target_pairs={{0,4},{4,8},{8,12},{12,0},{1,5},{5,9},{9,13},{13,1},{2,6},{6,10},{... | collective-permute-start | bytes 442376 | tf_op jit(solution)/shard_map/ppermute | solution.py:272
  77.3 9.6 %collective-permute-start.3 = (f32[2,3,2,24,128]{4,3,2,1,0:T(8,128)}, f32[2,3,2,24,128]{4,3,2,1,0:T(8,128)S(1)}, u32[]{:S(2)}, u32[]{:S(2)}) collective-permute-start(f32[2,3,2,24,128]{4,3,2,1,0:T(8,128)} %get-tuple-element.28), channel_id=1, source_target_pairs={{0,8},{4,12},{8,0},{12,4},{1,9},{5,13},{9,1},{13,5},{2,10},{6,14},... | collective-permute-start | bytes 442376 | tf_op jit(solution)/shard_map/ppermute | solution.py:272
  81.6 8.7 %collective-permute-start.4 = (f32[2,3,2,24,128]{4,3,2,1,0:T(8,128)}, f32[2,3,2,24,128]{4,3,2,1,0:T(8,128)S(1)}, u32[]{:S(2)}, u32[]{:S(2)}) collective-permute-start(f32[2,3,2,24,128]{4,3,2,1,0:T(8,128)} %get-tuple-element.29), channel_id=1, source_target_pairs={{0,12},{4,0},{8,4},{12,8},{1,13},{5,1},{9,5},{13,9},{2,14},{6,2},{... | collective-permute-start | bytes 442376 | tf_op jit(solution)/shard_map/ppermute | solution.py:272
  90.3 22.0 %collective-permute-start.5 = (f32[4,3,2,24,128]{4,3,2,1,0:T(8,128)S(1)}, f32[4,3,2,24,128]{4,3,2,1,0:T(8,128)S(1)}, u32[]{:S(2)}, u32[]{:S(2)}) collective-permute-start(f32[4,3,2,24,128]{4,3,2,1,0:T(8,128)S(1)} %pad_maximum_fusion), channel_id=1, source_target_pairs={{0,1},{1,0},{2,3},{3,2},{4,5},{5,4},{6,7},{7,6},{8,9},{9,8},{10,11... | collective-permute-start | bytes 884744 | tf_op jit(solution)/shard_map/ppermute | solution.py:273
  93.0 13.2 %collective-permute-start.11 = (f32[2,24,128]{2,1,0:T(8,128)S(1)}, f32[2,24,128]{2,1,0:T(8,128)S(1)}, u32[]{:S(2)}, u32[]{:S(2)}) collective-permute-start(f32[2,24,128]{2,1,0:T(8,128)S(1)} %copy-done.15), channel_id=1, source_target_pairs={{0,32},{16,48},{32,0},{48,16},{64,96},{80,112},{96,64},{112,80},{1... | collective-permute-start | bytes 73736 | tf_op jit(solution)/shard_map/ppermute | solution.py:276
  95.1 16.2 %collective-permute-start.12 = (f32[2,24,128]{2,1,0:T(8,128)S(1)}, f32[2,24,128]{2,1,0:T(8,128)S(1)}, u32[]{:S(2)}, u32[]{:S(2)}) collective-permute-start(f32[2,24,128]{2,1,0:T(8,128)S(1)} %copy-done.14), channel_id=1, source_target_pairs={{0,64},{16,80},{32,96},{48,112},{64,0},{80,16},{96,32},{112,48},{1... | collective-permute-start | bytes 73736 | tf_op jit(solution)/shard_map/ppermute | solution.py:276
  97.1 15.1 %collective-permute-start.13 = (f32[2,24,128]{2,1,0:T(8,128)S(1)}, f32[2,24,128]{2,1,0:T(8,128)S(1)}, u32[]{:S(2)}, u32[]{:S(2)}) collective-permute-start(f32[2,24,128]{2,1,0:T(8,128)S(1)} %copy-done.13), channel_id=1, source_target_pairs={{0,96},{16,112},{32,64},{48,80},{64,32},{80,48},{96,0},{112,16},{1... | collective-permute-start | bytes 73736 | tf_op jit(solution)/shard_map/ppermute | solution.py:276
  115.4 5.9 %copy-start.16 = (f32[24,128]{1,0:T(8,128)S(1)}, f32[24,128]{1,0:T(8,128)}, u32[]{:S(2)}) copy-start(f32[24,128]{1,0:T(8,128)} %get-tuple-element.45) | copy-start | bytes 36868
  115.4 10.6 %copy-start.12 = (f32[24,128]{1,0:T(8,128)S(1)}, f32[24,128]{1,0:T(8,128)}, u32[]{:S(2)}) copy-start(f32[24,128]{1,0:T(8,128)} %get-tuple-element.44) | copy-start | bytes 36868
  115.4 10.7 %copy-start.10 = (f32[12,1,192]{2,1,0:T(1,128)S(1)}, f32[12,1,192]{2,1,0:T(1,128)}, u32[]{:S(2)}) copy-start(f32[12,1,192]{2,1,0:T(1,128)} %row.1) | copy-start | bytes 27652
  115.4 21.6 %all-to-all-start.2 = ((f32[32,54,128]{2,1,0:T(8,128)}), f32[32,54,128]{2,1,0:T(8,128)S(1)}, u32[]{:S(2)}, u32[]{:S(2)}) async-start(f32[32,54,128]{2,1,0:T(8,128)} %get-tuple-element.43), calls=%async_computation.2 | async-start | bytes 1835008 | tf_op jit(solution)/shard_map/all_to_all | solution.py:287
  121.3 4.7 %collective-permute-start.14 = (f32[24,128]{1,0:T(8,128)S(1)}, f32[24,128]{1,0:T(8,128)S(1)}, u32[]{:S(2)}, u32[]{:S(2)}) collective-permute-start(f32[24,128]{1,0:T(8,128)S(1)} %copy-done.16), channel_id=1, source_target_pairs={{0,16},{16,0},{32,48},{48,32},{64,80},{80,64},{96,112},{112,96},{1... | collective-permute-start | bytes 36872 | tf_op jit(solution)/shard_map/ppermute | solution.py:283
  (3 other events, 2.6 us)

commit v6 on v4

--- a/solution.py
+++ b/solution.py
@@ -16,6 +16,10 @@
     return jax.ShapeDtypeStruct(dims, F32)
 
 
+def held(*dims):
+    return pltpu.VMEM(dims, F32)
+
+
 def vmem(n):
     return [pl.BlockSpec(memory_space=pltpu.VMEM)] * n
 
@@ -24,24 +28,42 @@
     return pl.BlockSpec(memory_space=pltpu.SMEM)
 
 
-def call(kernel, outs, scratch=()):
+def call(kernel, outs, scratch=(), pin=True):
     def run(place, *args):
+        if pin:
+            args = [pltpu.with_memory_space_constraint(a, pltpu.VMEM) for a in args]
+        first = [] if place is None else [place]
         return pl.pallas_call(
             kernel,
             out_shape=outs,
-            in_specs=[smem(), *vmem(len(args))],
+            in_specs=[*([smem()] * len(first)), *vmem(len(args))],
             out_specs=tuple(vmem(len(outs))),
             scratch_shapes=list(scratch),
-        )(place, *args)
+        )(*first, *args)
 
     return run
 
 
-def piece_kernel(place, row, out):
+def piece_kernel(row, out):
     values = row[:, 0, :]
     for i in range(16):
         out[i, :12, :] = values[:, :LANES]
         out[i, 12:, :] = jnp.concatenate([values[:, LANES:], jnp.zeros((12, 64), F32)], 1)
+
+
+def split(a):
+    top = a.astype(BF16)
+    return top, (a - top.astype(F32)).astype(BF16)
+
+
+def weights_kernel(place, zk, xk, zw, xw):
+    zrows = [zk[pl.ds(pl.multiple_of(48 * x + 24 * place[1], 8), 24), :] for x in range(4)]
+    zw[0], zw[1] = split(jnp.concatenate(zrows, 0))
+    xt = xk[...].T
+    zeros = jnp.zeros((64, 192), F32)
+    for odd in range(2):
+        cols = [xt[:LANES], zeros, xt[LANES:]] if odd else [xt[:LANES], xt[LANES:], zeros]
+        xw[odd, 0], xw[odd, 1] = split(jnp.concatenate(cols, 0))
 
 
 def pack_kernel(place, image, velocity, *outs):
@@ -138,20 +160,21 @@
         part[...] = total[pl.ds(2 * lax.bitwise_xor(zl // 2, t), 2)]
 
 
-def main_kernel(place, prev, mine, succ, got, zk, xk, *rest):
+def main_kernel(place, prev, mine, succ, got, zw, xw, *rest):
     parts, (out, keep, give, grid, force) = rest[:4], rest[4:]
-    y, zh, odd_row = place[0], place[1], lax.rem(place[3], 2)
+    y, odd_row = place[0], lax.rem(place[3], 2)
     for ref, i in ((keep, odd_row), (give, 1 - odd_row)):
         ref[...] = parts[0][i] + parts[1][i] + parts[2][i] + parts[3][i]
+
     for r, ref in enumerate((prev, mine, succ)):
         grid[r, :8] = jnp.zeros((8, WIDE), F32)
         grid[r, 200:] = jnp.zeros((8, WIDE), F32)
         for x in range(4):
             for h in range(2):
-                for c in range(2):
-                    at = 8 + 48 * x + 24 * h + 12 * c
-                    grid[r, at : at + 12, :LANES] = ref[2 * x + c, h, :12]
-                    grid[r, at : at + 12, LANES:] = ref[2 * x + c, h, 12:]
+                at = 8 + 48 * x + 24 * h
+                first, second = ref[2 * x, h], ref[2 * x + 1, h]
+                grid[r, at : at + 24, :LANES] = jnp.concatenate([first[:12], second[:12]], 0)
+                grid[r, at : at + 24, LANES:] = jnp.concatenate([first[12:], second[12:]], 0)
     here = grid[1, 8:200]
     low_lane = lax.broadcasted_iota(jnp.int32, (192, LANES), 1) < 64
     slopes = (
@@ -167,25 +190,13 @@
             for c in range(3):
                 force[at, (c * 6 + b) * LANES : (c * 6 + b + 1) * LANES] = r * slopes[c][b // 4][at]
 
-    def split(a):
-        top = a.astype(BF16)
-        return top, (a - top.astype(F32)).astype(BF16)
-
-    def times(a, b):
-        (a1, a0), (b1, b0) = a, b
+    def times(a1, a0, b1, b0):
         dot = lambda p, q: jnp.dot(p, q, preferred_element_type=F32)
         return dot(a1, b1) + (dot(a1, b0) + dot(a0, b1))
 
-    zrows = jnp.concatenate(
-        [zk[pl.ds(pl.multiple_of(48 * x + 24 * zh, 8), 24), :] for x in range(4)], 0
-    )
-    smooth = times(split(zrows), split(force[...]))
-
-    xt = xk[...]
-    zeros = jnp.zeros((64, 192), F32)
+    smooth = times(zw[0], zw[1], *split(force[...]))
+
     for odd in range(2):
-        cols = [xt[:LANES], zeros, xt[LANES:]] if odd else [xt[:LANES], xt[LANES:], zeros]
-        weights = split(jnp.concatenate(cols, 0))
         left = []
         for s in (odd, odd + 2):
             for c in range(3):
@@ -199,7 +210,7 @@
                         1,
                     )
                 )
-        update = times(split(jnp.concatenate(left, 0)), weights)
+        update = times(*split(jnp.concatenate(left, 0)), xw[odd, 0], xw[odd, 1])
         for i, s in enumerate((odd, odd + 2)):
             to = 8 * lax.rem(y + 4 - s, 4)
             for c in range(3):
@@ -215,35 +226,43 @@
 def per_device(image, velocity, template, z_kernel, x_kernel):
     place = jnp.stack([lax.axis_index(a) for a in ("y", "zh", "c", "zl")]).astype(jnp.int32)
 
-    (piece,) = call(piece_kernel, (shape(16, 24, LANES),))(place, template)
+    (piece,) = call(piece_kernel, (shape(16, 24, LANES),))(None, template)
     gathered = lax.all_to_all(piece, COL, 0, 0, tiled=True).reshape(8, 2, 24, LANES)
 
-    raws = call(pack_kernel, (shape(6, 12, 8, LANES),) * 4)(place, image[0], velocity[0])
+    raws = call(
+        pack_kernel, (held(6, 12, 8, LANES), *[shape(6, 12, 8, LANES)] * 3), pin=False
+    )(place, image[0], velocity[0])
     raws = [raws[0]] + [
         lax.ppermute(raws[s], "y", [(i, (i + s) % 4) for i in range(4)]) for s in (1, 2, 3)
     ]
 
     tmpl, ends, first, last = call(
         halo_kernel,
-        (shape(2, 24, 8, LANES), shape(2, 4, 8, LANES), shape(2, 24, LANES), shape(2, 24, LANES)),
+        (held(2, 24, 8, LANES), *[shape(2, 4, 8, LANES), shape(2, 24, LANES), shape(2, 24, LANES)]),
     )(place, gathered)
     by_core = lax.ppermute(ends, "c", [(0, 1), (1, 0)])
     by_x = lax.ppermute(ends, ("x", "c"), [(2 * i + 1, 2 * i + 2) for i in range(3)] + [(2 * i + 2, 2 * i + 1) for i in range(3)])
     prev_row = lax.ppermute(last, "y", [(i, i + 1) for i in range(3)])
     next_row = lax.ppermute(first, "y", [(i + 1, i) for i in range(3)])
-    gathered, by_core = lax.optimization_barrier((gathered, by_core))
+
+    gathered, by_x = lax.optimization_barrier((gathered, by_x))
     mine = lax.all_to_all(gathered, ("x", "c"), 0, 0, tiled=True)
 
     by_row, *parts = call(
         residual_kernel,
-        (shape(16, 72, LANES), *[shape(2, 24, LANES)] * 4),
+        (shape(16, 72, LANES), held(2, 24, LANES), *[shape(2, 24, LANES)] * 3),
         (pltpu.VMEM((96, 8, LANES), F32), pltpu.VMEM((8, 24, LANES), F32)),
     )(place, tmpl, prev_row, next_row, by_core, by_x, *raws)
     by_row, mine = lax.optimization_barrier((by_row, mine))
     got = lax.all_to_all(by_row, ("x", "zh", "c"), 0, 0, tiled=True)
+
     along = [(i, i + 1) for i in range(31)]
     prev = lax.ppermute(mine, ROW, along)
     succ = lax.ppermute(mine, ROW, [(j, i) for i, j in along])
+    zw, xw = call(
+        weights_kernel,
+        (pltpu.VMEM((2, 96, 192), BF16), pltpu.VMEM((2, 2, 256, 192), BF16)),
+    )(place, z_kernel, x_kernel)
 
     for t in (1, 2, 3):
         parts[t] = lax.ppermute(parts[t], "zl", [(i, i ^ (2 * t)) for i in range(8)])
@@ -252,7 +271,7 @@
         main_kernel,
         (shape(32, 54, LANES), shape(24, LANES), shape(24, LANES)),
         (pltpu.VMEM((3, 208, WIDE), F32), pltpu.VMEM((192, 18 * LANES), F32)),
-    )(place, prev, mine, succ, got, z_kernel, x_kernel.T, *parts)
+    )(place, prev, mine, succ, got, zw, xw, *parts)
     total = keep + lax.ppermute(give, "zl", [(i, i ^ 1) for i in range(8)])
     summed = jnp.concatenate([total[:12], total[12:, :64]], -1)[:, None]
     new_template = template + summed / 32

time: 138 us -> 137 us (level)
  local copies, waits for them, and re-layouts: 3.9 us -> 1.75 us
  Pallas kernels: 12 us -> 10.5 us
    ppermute x1, starting transfers between devices: 5.94 us -> 1.91 us  [per_device(): by_core = lax.ppermute(ends, 'c', [(0, 1), (1, 0)])]
    ppermute x1, starting transfers between devices: 3.53 us -> 7.04 us  [per_device(): lax.ppermute(ends, ('x', 'c'), [(2 * i + 1, 2 * i + 2) for i in range(3)]...]
    ppermute x3, waiting for transfers between devices: 4.37 us -> 7.34 us  [per_device(): parts[t] = lax.ppermute(parts[t], 'zl', [(i, i ^ 2 * t) for i in range(8)])]
    all_to_all x1, waiting for transfers between devices: 2.71 us -> 0.24 us  [per_device(): got = lax.all_to_all(by_row, ('x', 'zh', 'c'), 0, 0, tiled=True)]
    unnamed x46 -> x19, local copies, waits for them, and re-layouts: 3.49 us -> 1.34 us
    all_to_all x1, starting transfers between devices: 10.5 us -> 12.5 us  [per_device(): got = lax.all_to_all(by_row, ('x', 'zh', 'c'), 0, 0, tiled=True)]
    ppermute x1, waiting for transfers between devices: 0.01 us -> 1.79 us  [per_device(): lax.ppermute(ends, ('x', 'c'), [(2 * i + 1, 2 * i + 2) for i in range(3)]...]
    pallas_call x5 -> x6, Pallas kernels: 12 us -> 10.5 us  [run(): pl.pallas_call(kernel, out_shape=outs, in_specs=[*[smem()] * len(first),...]
where the time goes in v6:
time: 137 us; the launch traced here: 136 us
  starting transfers between devices  94.9 us (69%)
  waiting for transfers between devices  25.8 us (19%)
  Pallas kernels  10.5 us (8%)
  local copies, waits for them, and re-layouts  1.75 us (1%)
  other arithmetic  1.74 us (1%)
    all_to_all x1, starting transfers between devices, per_device(): back = lax.all_to_all(packed, ROW, 0, 0, tiled=True)  17.7 us
    all_to_all x1, starting transfers between devices, per_device(): lax.all_to_all(piece, COL, 0, 0, tiled=True).reshape(8, 2, 24, LANES)  15.8 us
    all_to_all x1, starting transfers between devices, per_device(): got = lax.all_to_all(by_row, ('x', 'zh', 'c'), 0, 0, tiled=True)  12.5 us
    ppermute x3, starting transfers between devices, per_device(): parts[t] = lax.ppermute(parts[t], 'zl', [(i, i ^ 2 * t) for i in range(8)])  11.4 us
    ppermute x3, starting transfers between devices, per_device(): lax.ppermute(raws[s], 'y', [(i, (i + s) % 4) for i in range(4)])  10.7 us
    pallas_call x6, Pallas kernels, run(): pl.pallas_call(kernel, out_shape=outs, in_specs=[*[smem()] * len(first),...  10.5 us
    all_to_all x1, waiting for transfers between devices, per_device(): back = lax.all_to_all(packed, ROW, 0, 0, tiled=True)  10.4 us
    ppermute x3, waiting for transfers between devices, per_device(): parts[t] = lax.ppermute(parts[t], 'zl', [(i, i ^ 2 * t) for i in range(8)])  7.34 us
  transfers between devices with their start and end apart: 17, of which 8 were waited for; matrix products, arithmetic and copies ran while one was open for 1% of the time, Pallas kernels for 5%

profile of v6, /device:TPU:1, one launch (start us, length us, event | category | flops | bytes accessed | tf_op | source)
XLA Modules:
  0.0 135.7 jit_solution(2559915573850961960)
XLA Ops:
  0.6 0.7 copy-done.2
  1.3 0.7 shard_map.68
  2.1 15.8 %all-to-all-start = ((f32[16,24,128]{2,1,0:T(8,128)}), f32[16,24,128]{2,1,0:T(8,128)}, u32[]{:S(2)}, u32[]{:S(2)}) async-start(f32[16,24,128]{2,1,0:T(8,128)} %shard_map.68), calls=%async_computation | async-start | bytes 393216 | tf_op jit(solution)/shard_map/all_to_all | solution.py:230
  18.5 2.5 %shard_map.70 = (f32[6,12,8,128]{3,2,1,0:T(8,128)S(1)}, f32[6,12,8,128]{3,2,1,0:T(8,128)}, f32[6,12,8,128]{3,2,1,0:T(8,128)}, f32[6,12,8,128]{3,2,1,0:T(8,128)}) custom-call(s32[4]{0:T(128)} %pad_add_fusion.place, f32[12,32,192]{2,1,0:T(8,128)} %bitcast.20, f32[3,12,32,192]{3,2,1,0:T(8,128)} %bitcast.19), custom_call_target="tpu_custom_call" | custom-call | tf_op jit(solution)/shard_map/pallas_call | solution.py:36
  21.0 3.2 %collective-permute-start.4 = (f32[6,12,8,128]{3,2,1,0:T(8,128)}, f32[6,12,8,128]{3,2,1,0:T(8,128)S(1)}, u32[]{:S(2)}, u32[]{:S(2)}) collective-permute-start(f32[6,12,8,128]{3,2,1,0:T(8,128)} %get-tuple-element.30), channel_id=1, source_target_pairs={{0,128},{128,256},{256,384},{384,0},{1,129},{129,257},{257,385},{3... | collective-permute-start | bytes 884744 | tf_op jit(solution)/shard_map/ppermute | solution.py:236
  24.2 4.5 %collective-permute-start.5 = (f32[6,12,8,128]{3,2,1,0:T(8,128)}, f32[6,12,8,128]{3,2,1,0:T(8,128)S(1)}, u32[]{:S(2)}, u32[]{:S(2)}) collective-permute-start(f32[6,12,8,128]{3,2,1,0:T(8,128)} %get-tuple-element.31), channel_id=1, source_target_pairs={{0,256},{128,384},{256,0},{384,128},{1,257},{129,385},{257,1},{385... | collective-permute-start | bytes 884744 | tf_op jit(solution)/shard_map/ppermute | solution.py:236
  28.7 3.0 %collective-permute-start.6 = (f32[6,12,8,128]{3,2,1,0:T(8,128)}, f32[6,12,8,128]{3,2,1,0:T(8,128)S(1)}, u32[]{:S(2)}, u32[]{:S(2)}) collective-permute-start(f32[6,12,8,128]{3,2,1,0:T(8,128)} %get-tuple-element.32), channel_id=1, source_target_pairs={{0,384},{128,0},{256,128},{384,256},{1,385},{129,1},{257,129},{385... | collective-permute-start | bytes 884744 | tf_op jit(solution)/shard_map/ppermute | solution.py:236
  31.7 0.9 all-to-all-done
  32.6 1.6 %shard_map.69 = (f32[2,24,8,128]{3,2,1,0:T(8,128)S(1)}, f32[2,4,8,128]{3,2,1,0:T(8,128)}, f32[2,24,128]{2,1,0:T(8,128)}, f32[2,24,128]{2,1,0:T(8,128)}) custom-call(s32[4]{0:T(128)} %pad_add_fusion.place, f32[8,2,24,128]{3,2,1,0:T(8,128)} %bitcast.4.gathered), custom_call_target="tpu_custom_call" | custom-call | tf_op jit(solution)/shard_map/pallas_call | solution.py:36
  34.2 7.0 %collective-permute-start.3 = (f32[2,4,8,128]{3,2,1,0:T(8,128)}, f32[2,4,8,128]{3,2,1,0:T(8,128)S(1)}, u32[]{:S(2)}, u32[]{:S(2)}) collective-permute-start(f32[2,4,8,128]{3,2,1,0:T(8,128)} %get-tuple-element.27), channel_id=1, source_target_pairs={{1,4},{5,8},{9,12},{4,1},{8,5},{12,9},{3,6},{7,10},{11,14},{6,3},{... | collective-permute-start | bytes 98312 | tf_op jit(solution)/shard_map/ppermute | solution.py:244
  41.2 1.8 %collective-permute-done.3.by_x = f32[2,4,8,128]{3,2,1,0:T(8,128)S(1)} collective-permute-done((f32[2,4,8,128]{3,2,1,0:T(8,128)}, f32[2,4,8,128]{3,2,1,0:T(8,128)S(1)}, u32[]{:S(2)}, u32[]{:S(2)}) %collective-permute-start.3) | collective-permute-done | bytes 32800 | tf_op jit(solution)/shard_map/ppermute | solution.py:244
  43.0 4.9 %all-to-all-start.1 = ((f32[8,2,24,128]{3,2,1,0:T(8,128)}), f32[8,2,24,128]{3,2,1,0:T(8,128)S(1)}, u32[]{:S(2)}, u32[]{:S(2)}) async-start(f32[8,2,24,128]{3,2,1,0:T(8,128)} %bitcast.4.gathered), calls=%async_computation.1 | async-start | bytes 393216 | tf_op jit(solution)/shard_map/all_to_all | solution.py:249
  48.0 1.9 %collective-permute-start.2 = (f32[2,4,8,128]{3,2,1,0:T(8,128)}, f32[2,4,8,128]{3,2,1,0:T(8,128)S(1)}, u32[]{:S(2)}, u32[]{:S(2)}) collective-permute-start(f32[2,4,8,128]{3,2,1,0:T(8,128)} %get-tuple-element.27), channel_id=1, source_target_pairs={{0,1},{1,0},{2,3},{3,2},{4,5},{5,4},{6,7},{7,6},{8,9},{9,8},{10,11... | collective-permute-start | bytes 98312 | tf_op jit(solution)/shard_map/ppermute | solution.py:243
  49.9 3.2 %collective-permute-start = (f32[2,24,128]{2,1,0:T(8,128)}, f32[2,24,128]{2,1,0:T(8,128)S(1)}, u32[]{:S(2)}, u32[]{:S(2)}) collective-permute-start(f32[2,24,128]{2,1,0:T(8,128)} %get-tuple-element.25), channel_id=1, source_target_pairs={{0,128},{128,256},{256,384},{1,129},{129,257},{257,385},{2,130},{1... | collective-permute-start | bytes 73736 | tf_op jit(solution)/shard_map/ppermute | solution.py:245
  53.1 1.3 collective-permute-start.1
  54.4 3.4 %collective-permute-done.1.next_row = f32[2,24,128]{2,1,0:T(8,128)S(1)} collective-permute-done((f32[2,24,128]{2,1,0:T(8,128)}, f32[2,24,128]{2,1,0:T(8,128)S(1)}, u32[]{:S(2)}, u32[]{:S(2)}) %collective-permute-start.1) | collective-permute-done | bytes 24608 | tf_op jit(solution)/shard_map/ppermute | solution.py:246
  57.9 2.0 %shard_map.71 = (f32[16,72,128]{2,1,0:T(8,128)}, f32[2,24,128]{2,1,0:T(8,128)S(1)}, f32[2,24,128]{2,1,0:T(8,128)}, f32[2,24,128]{2,1,0:T(8,128)}, f32[2,24,128]{2,1,0:T(8,128)}) custom-call(s32[4]{0:T(128)} %pad_add_fusion.place, f32[2,24,8,128]{3,2,1,0:T(8,128)S(1)} %get-tuple-element.24.tmpl, f32[2,24,128]{2,1,0:T(8,128)S(1)} %collective-permute-done.prev_row, ...), custom_call_target="tpu_custom_call" | custom-call | tf_op jit(solution)/shard_map/pallas_call | solution.py:36
  59.9 12.5 %all-to-all-start.2 = ((f32[16,72,128]{2,1,0:T(8,128)}), f32[16,72,128]{2,1,0:T(8,128)S(1)}, u32[]{:S(2)}, u32[]{:S(2)}) async-start(f32[16,72,128]{2,1,0:T(8,128)} %get-tuple-element.36), calls=%async_computation.2 | async-start | bytes 1179648 | tf_op jit(solution)/shard_map/all_to_all | solution.py:257
  72.4 3.5 %collective-permute-start.7 = (f32[8,2,24,128]{3,2,1,0:T(8,128)S(1)}, f32[8,2,24,128]{3,2,1,0:T(8,128)S(1)}, u32[]{:S(2)}, u32[]{:S(2)}) collective-permute-start(f32[8,2,24,128]{3,2,1,0:T(8,128)S(1)} %all-to-all-done.1.mine), channel_id=1, source_target_pairs={{0,1},{1,4},{4,5},{5,8},{8,9},{9,12},{12,13},{13,128},{128,129},{1... | collective-permute-start | bytes 589832 | tf_op jit(solution)/shard_map/ppermute | solution.py:260
  75.9 1.9 %collective-permute-start.8 = (f32[8,2,24,128]{3,2,1,0:T(8,128)S(1)}, f32[8,2,24,128]{3,2,1,0:T(8,128)S(1)}, u32[]{:S(2)}, u32[]{:S(2)}) collective-permute-start(f32[8,2,24,128]{3,2,1,0:T(8,128)S(1)} %all-to-all-done.1.mine), channel_id=1, source_target_pairs={{1,0},{4,1},{5,4},{8,5},{9,8},{12,9},{13,12},{128,13},{129,128},{1... | collective-permute-start | bytes 589832 | tf_op jit(solution)/shard_map/ppermute | solution.py:261
  77.8 2.4 %collective-permute-start.10 = (f32[2,24,128]{2,1,0:T(8,128)S(1)}, f32[2,24,128]{2,1,0:T(8,128)S(1)}, u32[]{:S(2)}, u32[]{:S(2)}) collective-permute-start(f32[2,24,128]{2,1,0:T(8,128)S(1)} %copy-done.7), channel_id=1, source_target_pairs={{0,64},{16,80},{32,96},{48,112},{64,0},{80,16},{96,32},{112,48},{1... | collective-permute-start | bytes 73736 | tf_op jit(solution)/shard_map/ppermute | solution.py:268
  80.3 6.8 %collective-permute-start.11 = (f32[2,24,128]{2,1,0:T(8,128)S(1)}, f32[2,24,128]{2,1,0:T(8,128)S(1)}, u32[]{:S(2)}, u32[]{:S(2)}) collective-permute-start(f32[2,24,128]{2,1,0:T(8,128)S(1)} %copy-done.6), channel_id=1, source_target_pairs={{0,96},{16,112},{32,64},{48,80},{64,32},{80,48},{96,0},{112,16},{1... | collective-permute-start | bytes 73736 | tf_op jit(solution)/shard_map/ppermute | solution.py:268
  87.1 2.2 %collective-permute-start.9 = (f32[2,24,128]{2,1,0:T(8,128)S(1)}, f32[2,24,128]{2,1,0:T(8,128)S(1)}, u32[]{:S(2)}, u32[]{:S(2)}) collective-permute-start(f32[2,24,128]{2,1,0:T(8,128)S(1)} %copy-done.5), channel_id=1, source_target_pairs={{0,32},{16,48},{32,0},{48,16},{64,96},{80,112},{96,64},{112,80},{1... | collective-permute-start | bytes 73736 | tf_op jit(solution)/shard_map/ppermute | solution.py:268
  89.3 0.8 shard_map.72
  90.1 2.8 %collective-permute-done.10.rest_2_ = f32[2,24,128]{2,1,0:T(8,128)S(1)} collective-permute-done((f32[2,24,128]{2,1,0:T(8,128)S(1)}, f32[2,24,128]{2,1,0:T(8,128)S(1)}, u32[]{:S(2)}, u32[]{:S(2)}) %collective-permute-start.10) | collective-permute-done | bytes 24608 | tf_op jit(solution)/shard_map/ppermute | solution.py:268
  92.9 4.5 %collective-permute-done.9.rest_1_ = f32[2,24,128]{2,1,0:T(8,128)S(1)} collective-permute-done((f32[2,24,128]{2,1,0:T(8,128)S(1)}, f32[2,24,128]{2,1,0:T(8,128)S(1)}, u32[]{:S(2)}, u32[]{:S(2)}) %collective-permute-start.9) | collective-permute-done | bytes 24608 | tf_op jit(solution)/shard_map/ppermute | solution.py:268
  97.7 3.0 %shard_map.73 = (f32[32,54,128]{2,1,0:T(8,128)}, f32[24,128]{1,0:T(8,128)}, f32[24,128]{1,0:T(8,128)}) custom-call(s32[4]{0:T(128)} %pad_add_fusion.place, f32[8,2,24,128]{3,2,1,0:T(8,128)S(1)} %collective-permute-done.7.prev, f32[8,2,24,128]{3,2,1,0:T(8,128)S(1)} %all-to-all-done.1.mine, f32[8,2,24,128]{3,2,1,0:T(8,128)S(1)} %collective-permute-done.8.succ, ...), custom_call_target="tpu_custom_call" | custom-call | tf_op jit(solution)/shard_map/pallas_call | solution.py:36
  100.7 17.7 %all-to-all-start.3 = ((f32[32,54,128]{2,1,0:T(8,128)}), f32[32,54,128]{2,1,0:T(8,128)S(1)}, u32[]{:S(2)}, u32[]{:S(2)}) async-start(f32[32,54,128]{2,1,0:T(8,128)} %get-tuple-element.43), calls=%async_computation.3 | async-start | bytes 1835008 | tf_op jit(solution)/shard_map/all_to_all | solution.py:279
  118.4 3.0 %collective-permute-start.12 = (f32[24,128]{1,0:T(8,128)S(1)}, f32[24,128]{1,0:T(8,128)S(1)}, u32[]{:S(2)}, u32[]{:S(2)}) collective-permute-start(f32[24,128]{1,0:T(8,128)S(1)} %copy-done.8), channel_id=1, source_target_pairs={{0,16},{16,0},{32,48},{48,32},{64,80},{80,64},{96,112},{112,96},{1... | collective-permute-start | bytes 36872 | tf_op jit(solution)/shard_map/ppermute | solution.py:275
  121.5 1.7 %collective-permute-done.12 = f32[24,128]{1,0:T(8,128)S(1)} collective-permute-done((f32[24,128]{1,0:T(8,128)S(1)}, f32[24,128]{1,0:T(8,128)S(1)}, u32[]{:S(2)}, u32[]{:S(2)}) %collective-permute-start.12) | collective-permute-done | bytes 12320 | tf_op jit(solution)/shard_map/ppermute | solution.py:275
  123.8 10.4 %all-to-all-done.3 = f32[32,54,128]{2,1,0:T(8,128)S(1)} async-done(((f32[32,54,128]{2,1,0:T(8,128)}), f32[32,54,128]{2,1,0:T(8,128)S(1)}, u32[]{:S(2)}, u32[]{:S(2)}) %all-to-all-start.3) | async-done | bytes 884768 | tf_op jit(solution)/shard_map/all_to_all | solution.py:279
  134.6 1.1 maximum_bitcast_fusion
  (38 shorter events, 1.9 us)
Async XLA Ops:
  0.6 0.7 copy-start.2
  2.1 30.5 %all-to-all-start = ((f32[16,24,128]{2,1,0:T(8,128)}), f32[16,24,128]{2,1,0:T(8,128)}, u32[]{:S(2)}, u32[]{:S(2)}) async-start(f32[16,24,128]{2,1,0:T(8,128)} %shard_map.68), calls=%async_computation | async-start | bytes 393216 | tf_op jit(solution)/shard_map/all_to_all | solution.py:230
  21.0 32.1 %collective-permute-start.4 = (f32[6,12,8,128]{3,2,1,0:T(8,128)}, f32[6,12,8,128]{3,2,1,0:T(8,128)S(1)}, u32[]{:S(2)}, u32[]{:S(2)}) collective-permute-start(f32[6,12,8,128]{3,2,1,0:T(8,128)} %get-tuple-element.30), channel_id=1, source_target_pairs={{0,128},{128,256},{256,384},{384,0},{1,129},{129,257},{257,385},{3... | collective-permute-start | bytes 884744 | tf_op jit(solution)/shard_map/ppermute | solution.py:236
  24.2 30.2 %collective-permute-start.5 = (f32[6,12,8,128]{3,2,1,0:T(8,128)}, f32[6,12,8,128]{3,2,1,0:T(8,128)S(1)}, u32[]{:S(2)}, u32[]{:S(2)}) collective-permute-start(f32[6,12,8,128]{3,2,1,0:T(8,128)} %get-tuple-element.31), channel_id=1, source_target_pairs={{0,256},{128,384},{256,0},{384,128},{1,257},{129,385},{257,1},{385... | collective-permute-start | bytes 884744 | tf_op jit(solution)/shard_map/ppermute | solution.py:236
  28.7 25.7 %collective-permute-start.6 = (f32[6,12,8,128]{3,2,1,0:T(8,128)}, f32[6,12,8,128]{3,2,1,0:T(8,128)S(1)}, u32[]{:S(2)}, u32[]{:S(2)}) collective-permute-start(f32[6,12,8,128]{3,2,1,0:T(8,128)} %get-tuple-element.32), channel_id=1, source_target_pairs={{0,384},{128,0},{256,128},{384,256},{1,385},{129,1},{257,129},{385... | collective-permute-start | bytes 884744 | tf_op jit(solution)/shard_map/ppermute | solution.py:236
  34.2 8.8 %collective-permute-start.3 = (f32[2,4,8,128]{3,2,1,0:T(8,128)}, f32[2,4,8,128]{3,2,1,0:T(8,128)S(1)}, u32[]{:S(2)}, u32[]{:S(2)}) collective-permute-start(f32[2,4,8,128]{3,2,1,0:T(8,128)} %get-tuple-element.27), channel_id=1, source_target_pairs={{1,4},{5,8},{9,12},{4,1},{8,5},{12,9},{3,6},{7,10},{11,14},{6,3},{... | collective-permute-start | bytes 98312 | tf_op jit(solution)/shard_map/ppermute | solution.py:244
  43.0 16.8 %all-to-all-start.1 = ((f32[8,2,24,128]{3,2,1,0:T(8,128)}), f32[8,2,24,128]{3,2,1,0:T(8,128)S(1)}, u32[]{:S(2)}, u32[]{:S(2)}) async-start(f32[8,2,24,128]{3,2,1,0:T(8,128)} %bitcast.4.gathered), calls=%async_computation.1 | async-start | bytes 393216 | tf_op jit(solution)/shard_map/all_to_all | solution.py:249
  48.0 9.9 %collective-permute-start.2 = (f32[2,4,8,128]{3,2,1,0:T(8,128)}, f32[2,4,8,128]{3,2,1,0:T(8,128)S(1)}, u32[]{:S(2)}, u32[]{:S(2)}) collective-permute-start(f32[2,4,8,128]{3,2,1,0:T(8,128)} %get-tuple-element.27), channel_id=1, source_target_pairs={{0,1},{1,0},{2,3},{3,2},{4,5},{5,4},{6,7},{7,6},{8,9},{9,8},{10,11... | collective-permute-start | bytes 98312 | tf_op jit(solution)/shard_map/ppermute | solution.py:243
  49.9 4.5 %collective-permute-start = (f32[2,24,128]{2,1,0:T(8,128)}, f32[2,24,128]{2,1,0:T(8,128)S(1)}, u32[]{:S(2)}, u32[]{:S(2)}) collective-permute-start(f32[2,24,128]{2,1,0:T(8,128)} %get-tuple-element.25), channel_id=1, source_target_pairs={{0,128},{128,256},{256,384},{1,129},{129,257},{257,385},{2,130},{1... | collective-permute-start | bytes 73736 | tf_op jit(solution)/shard_map/ppermute | solution.py:245
  53.1 4.8 %collective-permute-start.1 = (f32[2,24,128]{2,1,0:T(8,128)}, f32[2,24,128]{2,1,0:T(8,128)S(1)}, u32[]{:S(2)}, u32[]{:S(2)}) collective-permute-start(f32[2,24,128]{2,1,0:T(8,128)} %get-tuple-element.26), channel_id=1, source_target_pairs={{128,0},{256,128},{384,256},{129,1},{257,129},{385,257},{130,2},{2... | collective-permute-start | bytes 73736 | tf_op jit(solution)/shard_map/ppermute | solution.py:246
  57.9 31.4 %copy-start = (f32[192,192]{1,0:T(8,128)S(1)}, f32[192,192]{1,0:T(8,128)}, u32[]{:S(2)}) copy-start(f32[192,192]{1,0:T(8,128)} %zk.1) | copy-start | bytes 442372
  57.9 31.4 %copy-start.1 = (f32[192,192]{1,0:T(8,128)S(1)}, f32[192,192]{1,0:T(8,128)}, u32[]{:S(2)}) copy-start(f32[192,192]{1,0:T(8,128)} %xk.1) | copy-start | bytes 442372
  59.8 18.0 %copy-start.7 = (f32[2,24,128]{2,1,0:T(8,128)S(1)}, f32[2,24,128]{2,1,0:T(8,128)}, u32[]{:S(2)}) copy-start(f32[2,24,128]{2,1,0:T(8,128)} %get-tuple-element.41) | copy-start | bytes 73732
  59.8 20.4 %copy-start.6 = (f32[2,24,128]{2,1,0:T(8,128)S(1)}, f32[2,24,128]{2,1,0:T(8,128)}, u32[]{:S(2)}) copy-start(f32[2,24,128]{2,1,0:T(8,128)} %get-tuple-element.42) | copy-start | bytes 73732
  59.9 27.2 %copy-start.5 = (f32[2,24,128]{2,1,0:T(8,128)S(1)}, f32[2,24,128]{2,1,0:T(8,128)}, u32[]{:S(2)}) copy-start(f32[2,24,128]{2,1,0:T(8,128)} %get-tuple-element.40) | copy-start | bytes 73732
  59.9 37.8 %all-to-all-start.2 = ((f32[16,72,128]{2,1,0:T(8,128)}), f32[16,72,128]{2,1,0:T(8,128)S(1)}, u32[]{:S(2)}, u32[]{:S(2)}) async-start(f32[16,72,128]{2,1,0:T(8,128)} %get-tuple-element.36), calls=%async_computation.2 | async-start | bytes 1179648 | tf_op jit(solution)/shard_map/all_to_all | solution.py:257
  72.4 25.1 %collective-permute-start.7 = (f32[8,2,24,128]{3,2,1,0:T(8,128)S(1)}, f32[8,2,24,128]{3,2,1,0:T(8,128)S(1)}, u32[]{:S(2)}, u32[]{:S(2)}) collective-permute-start(f32[8,2,24,128]{3,2,1,0:T(8,128)S(1)} %all-to-all-done.1.mine), channel_id=1, source_target_pairs={{0,1},{1,4},{4,5},{5,8},{8,9},{9,12},{12,13},{13,128},{128,129},{1... | collective-permute-start | bytes 589832 | tf_op jit(solution)/shard_map/ppermute | solution.py:260
  75.9 21.5 %collective-permute-start.8 = (f32[8,2,24,128]{3,2,1,0:T(8,128)S(1)}, f32[8,2,24,128]{3,2,1,0:T(8,128)S(1)}, u32[]{:S(2)}, u32[]{:S(2)}) collective-permute-start(f32[8,2,24,128]{3,2,1,0:T(8,128)S(1)} %all-to-all-done.1.mine), channel_id=1, source_target_pairs={{1,0},{4,1},{5,4},{8,5},{9,8},{12,9},{13,12},{128,13},{129,128},{1... | collective-permute-start | bytes 589832 | tf_op jit(solution)/shard_map/ppermute | solution.py:261
  77.8 15.1 %collective-permute-start.10 = (f32[2,24,128]{2,1,0:T(8,128)S(1)}, f32[2,24,128]{2,1,0:T(8,128)S(1)}, u32[]{:S(2)}, u32[]{:S(2)}) collective-permute-start(f32[2,24,128]{2,1,0:T(8,128)S(1)} %copy-done.7), channel_id=1, source_target_pairs={{0,64},{16,80},{32,96},{48,112},{64,0},{80,16},{96,32},{112,48},{1... | collective-permute-start | bytes 73736 | tf_op jit(solution)/shard_map/ppermute | solution.py:268
  80.3 12.7 %collective-permute-start.11 = (f32[2,24,128]{2,1,0:T(8,128)S(1)}, f32[2,24,128]{2,1,0:T(8,128)S(1)}, u32[]{:S(2)}, u32[]{:S(2)}) collective-permute-start(f32[2,24,128]{2,1,0:T(8,128)S(1)} %copy-done.6), channel_id=1, source_target_pairs={{0,96},{16,112},{32,64},{48,80},{64,32},{80,48},{96,0},{112,16},{1... | collective-permute-start | bytes 73736 | tf_op jit(solution)/shard_map/ppermute | solution.py:268
  87.1 10.4 %collective-permute-start.9 = (f32[2,24,128]{2,1,0:T(8,128)S(1)}, f32[2,24,128]{2,1,0:T(8,128)S(1)}, u32[]{:S(2)}, u32[]{:S(2)}) collective-permute-start(f32[2,24,128]{2,1,0:T(8,128)S(1)} %copy-done.5), channel_id=1, source_target_pairs={{0,32},{16,48},{32,0},{48,16},{64,96},{80,112},{96,64},{112,80},{1... | collective-permute-start | bytes 73736 | tf_op jit(solution)/shard_map/ppermute | solution.py:268
  100.7 17.8 %copy-start.8 = (f32[24,128]{1,0:T(8,128)S(1)}, f32[24,128]{1,0:T(8,128)}, u32[]{:S(2)}) copy-start(f32[24,128]{1,0:T(8,128)} %get-tuple-element.45) | copy-start | bytes 36868
  100.7 22.5 %copy-start.4 = (f32[24,128]{1,0:T(8,128)S(1)}, f32[24,128]{1,0:T(8,128)}, u32[]{:S(2)}) copy-start(f32[24,128]{1,0:T(8,128)} %get-tuple-element.44) | copy-start | bytes 36868
  100.7 22.5 %copy-start.3 = (f32[12,1,192]{2,1,0:T(1,128)S(1)}, f32[12,1,192]{2,1,0:T(1,128)}, u32[]{:S(2)}) copy-start(f32[12,1,192]{2,1,0:T(1,128)} %row.1) | copy-start | bytes 27652
  100.7 33.5 %all-to-all-start.3 = ((f32[32,54,128]{2,1,0:T(8,128)}), f32[32,54,128]{2,1,0:T(8,128)S(1)}, u32[]{:S(2)}, u32[]{:S(2)}) async-start(f32[32,54,128]{2,1,0:T(8,128)} %get-tuple-element.43), calls=%async_computation.3 | async-start | bytes 1835008 | tf_op jit(solution)/shard_map/all_to_all | solution.py:279
  118.4 4.7 %collective-permute-start.12 = (f32[24,128]{1,0:T(8,128)S(1)}, f32[24,128]{1,0:T(8,128)S(1)}, u32[]{:S(2)}, u32[]{:S(2)}) collective-permute-start(f32[24,128]{1,0:T(8,128)S(1)} %copy-done.8), channel_id=1, source_target_pairs={{0,16},{16,0},{32,48},{48,32},{64,80},{80,64},{96,112},{112,96},{1... | collective-permute-start | bytes 36872 | tf_op jit(solution)/shard_map/ppermute | solution.py:275

commit v7 on v6

--- a/solution.py
+++ b/solution.py
@@ -161,10 +161,8 @@
 
 
 def main_kernel(place, prev, mine, succ, got, zw, xw, *rest):
-    parts, (out, keep, give, grid, force) = rest[:4], rest[4:]
-    y, odd_row = place[0], lax.rem(place[3], 2)
-    for ref, i in ((keep, odd_row), (give, 1 - odd_row)):
-        ref[...] = parts[0][i] + parts[1][i] + parts[2][i] + parts[3][i]
+    out, grid, force = rest
+    y = place[0]
 
     for r, ref in enumerate((prev, mine, succ)):
         grid[r, :8] = jnp.zeros((8, WIDE), F32)
@@ -223,6 +221,17 @@
                     )
 
 
+def unpack_kernel(packed, out):
+    for k in range(4):
+        rows = slice(8 * k, 8 * k + 8)
+        block = jnp.swapaxes(packed[rows], 0, 1)
+        for c in range(3):
+            out[c, :, rows, :LANES] = block[12 * c : 12 * c + 12]
+            high = block[36 + 6 * c : 42 + 6 * c]
+            out[c, :6, rows, LANES:] = high[..., :64]
+            out[c, 6:, rows, LANES:] = high[..., 64:]
+
+
 def per_device(image, velocity, template, z_kernel, x_kernel):
     place = jnp.stack([lax.axis_index(a) for a in ("y", "zh", "c", "zl")]).astype(jnp.int32)
 
@@ -245,7 +254,6 @@
     prev_row = lax.ppermute(last, "y", [(i, i + 1) for i in range(3)])
     next_row = lax.ppermute(first, "y", [(i + 1, i) for i in range(3)])
 
-    gathered, by_x = lax.optimization_barrier((gathered, by_x))
     mine = lax.all_to_all(gathered, ("x", "c"), 0, 0, tiled=True)
 
     by_row, *parts = call(
@@ -264,23 +272,22 @@
         (pltpu.VMEM((2, 96, 192), BF16), pltpu.VMEM((2, 2, 256, 192), BF16)),
     )(place, z_kernel, x_kernel)
 
+    packed, = call(
+        main_kernel,
+        (shape(32, 54, LANES),),
+        (pltpu.VMEM((3, 208, WIDE), F32), pltpu.VMEM((192, 18 * LANES), F32)),
+    )(place, prev, mine, succ, got, zw, xw)
     for t in (1, 2, 3):
         parts[t] = lax.ppermute(parts[t], "zl", [(i, i ^ (2 * t)) for i in range(8)])
-
-    packed, keep, give = call(
-        main_kernel,
-        (shape(32, 54, LANES), shape(24, LANES), shape(24, LANES)),
-        (pltpu.VMEM((3, 208, WIDE), F32), pltpu.VMEM((192, 18 * LANES), F32)),
-    )(place, prev, mine, succ, got, zw, xw, *parts)
+    two, odd = sum(parts), lax.axis_index("zl") & 1
+    keep = lax.dynamic_index_in_dim(two, odd, 0, False)
+    give = lax.dynamic_index_in_dim(two, 1 - odd, 0, False)
     total = keep + lax.ppermute(give, "zl", [(i, i ^ 1) for i in range(8)])
     summed = jnp.concatenate([total[:12], total[12:, :64]], -1)[:, None]
     new_template = template + summed / 32
 
     back = lax.all_to_all(packed, ROW, 0, 0, tiled=True)
-    low = back[:, :36].reshape(32, 3, 12, LANES)
-    high = back[:, 36:].reshape(32, 3, 6, LANES)
-    high = jnp.concatenate([high[..., :64], high[..., 64:]], 2)
-    out = jnp.concatenate([low, high], -1).transpose(1, 2, 0, 3)
+    (out,) = call(unpack_kernel, (shape(3, 12, 32, 192),))(None, back)
     return out[None], new_template
 
 

time: 137 us -> 132 us (0.964)
  the two profiles are of different devices: /device:TPU:1 before, /device:TPU:33 now
where the time goes in v7:
time: 132 us; the launch traced here: 131 us
  starting transfers between devices  78.2 us (59%)
  waiting for transfers between devices  38.3 us (29%)
  Pallas kernels  11.7 us (9%)
    all_to_all x1, waiting for transfers between devices, per_device(): got = lax.all_to_all(by_row, ('x', 'zh', 'c'), 0, 0, tiled=True)  21.6 us
    all_to_all x1, starting transfers between devices, per_device(): lax.all_to_all(piece, COL, 0, 0, tiled=True).reshape(8, 2, 24, LANES)  14.7 us
    pallas_call x7, Pallas kernels, run(): pl.pallas_call(kernel, out_shape=outs, in_specs=[*[smem()] * len(first),...  11.7 us
    ppermute x3, starting transfers between devices, per_device(): parts[t] = lax.ppermute(parts[t], 'zl', [(i, i ^ 2 * t) for i in range(8)])  11.4 us
    ppermute x3, starting transfers between devices, per_device(): lax.ppermute(raws[s], 'y', [(i, (i + s) % 4) for i in range(4)])  10.7 us
    all_to_all x1, waiting for transfers between devices, per_device(): back = lax.all_to_all(packed, ROW, 0, 0, tiled=True)  10.4 us
    all_to_all x1, starting transfers between devices, per_device(): mine = lax.all_to_all(gathered, ('x', 'c'), 0, 0, tiled=True)  9.81 us
    all_to_all x1, starting transfers between devices, per_device(): got = lax.all_to_all(by_row, ('x', 'zh', 'c'), 0, 0, tiled=True)  9.68 us
  transfers between devices with their start and end apart: 17, of which 4 were waited for; matrix products, arithmetic and copies ran while one was open for 1% of the time, Pallas kernels for 8%

profile of v7, /device:TPU:33, one launch (start us, length us, event | category | flops | bytes accessed | tf_op | source)
XLA Modules:
  0.0 131.2 jit_solution(15978126744367736781)
XLA Ops:
  0.6 0.7 copy-done.2
  1.3 0.7 shard_map.68
  2.0 14.7 %all-to-all-start = ((f32[16,24,128]{2,1,0:T(8,128)}), f32[16,24,128]{2,1,0:T(8,128)}, u32[]{:S(2)}, u32[]{:S(2)}) async-start(f32[16,24,128]{2,1,0:T(8,128)} %shard_map.68), calls=%async_computation | async-start | bytes 393216 | tf_op jit(solution)/shard_map/all_to_all | solution.py:239
  16.7 0.6 pad_add_fusion.place
  17.3 2.5 %shard_map.70 = (f32[6,12,8,128]{3,2,1,0:T(8,128)S(1)}, f32[6,12,8,128]{3,2,1,0:T(8,128)}, f32[6,12,8,128]{3,2,1,0:T(8,128)}, f32[6,12,8,128]{3,2,1,0:T(8,128)}) custom-call(s32[4]{0:T(128)} %pad_add_fusion.place, f32[12,32,192]{2,1,0:T(8,128)} %bitcast.16, f32[3,12,32,192]{3,2,1,0:T(8,128)} %bitcast.14), custom_call_target="tpu_custom_call" | custom-call | tf_op jit(solution)/shard_map/pallas_call | solution.py:36
  19.8 3.2 %collective-permute-start.4 = (f32[6,12,8,128]{3,2,1,0:T(8,128)}, f32[6,12,8,128]{3,2,1,0:T(8,128)S(1)}, u32[]{:S(2)}, u32[]{:S(2)}) collective-permute-start(f32[6,12,8,128]{3,2,1,0:T(8,128)} %get-tuple-element.24), channel_id=1, source_target_pairs={{0,128},{128,256},{256,384},{384,0},{1,129},{129,257},{257,385},{3... | collective-permute-start | bytes 884744 | tf_op jit(solution)/shard_map/ppermute | solution.py:245
  23.0 4.5 %collective-permute-start.5 = (f32[6,12,8,128]{3,2,1,0:T(8,128)}, f32[6,12,8,128]{3,2,1,0:T(8,128)S(1)}, u32[]{:S(2)}, u32[]{:S(2)}) collective-permute-start(f32[6,12,8,128]{3,2,1,0:T(8,128)} %get-tuple-element.25), channel_id=1, source_target_pairs={{0,256},{128,384},{256,0},{384,128},{1,257},{129,385},{257,1},{385... | collective-permute-start | bytes 884744 | tf_op jit(solution)/shard_map/ppermute | solution.py:245
  27.6 3.0 %collective-permute-start.6 = (f32[6,12,8,128]{3,2,1,0:T(8,128)}, f32[6,12,8,128]{3,2,1,0:T(8,128)S(1)}, u32[]{:S(2)}, u32[]{:S(2)}) collective-permute-start(f32[6,12,8,128]{3,2,1,0:T(8,128)} %get-tuple-element.26), channel_id=1, source_target_pairs={{0,384},{128,0},{256,128},{384,256},{1,385},{129,1},{257,129},{385... | collective-permute-start | bytes 884744 | tf_op jit(solution)/shard_map/ppermute | solution.py:245
  30.6 9.8 %all-to-all-start.1 = ((f32[8,2,24,128]{3,2,1,0:T(8,128)}), f32[8,2,24,128]{3,2,1,0:T(8,128)S(1)}, u32[]{:S(2)}, u32[]{:S(2)}) async-start(f32[8,2,24,128]{3,2,1,0:T(8,128)} %bitcast.4.gathered), calls=%async_computation.1 | async-start | bytes 393216 | tf_op jit(solution)/shard_map/all_to_all | solution.py:257
  40.4 1.6 %shard_map.69 = (f32[2,24,8,128]{3,2,1,0:T(8,128)S(1)}, f32[2,4,8,128]{3,2,1,0:T(8,128)}, f32[2,24,128]{2,1,0:T(8,128)}, f32[2,24,128]{2,1,0:T(8,128)}) custom-call(s32[4]{0:T(128)} %pad_add_fusion.place, f32[8,2,24,128]{3,2,1,0:T(8,128)} %bitcast.4.gathered), custom_call_target="tpu_custom_call" | custom-call | tf_op jit(solution)/shard_map/pallas_call | solution.py:36
  42.0 1.9 %collective-permute-start.2 = (f32[2,4,8,128]{3,2,1,0:T(8,128)}, f32[2,4,8,128]{3,2,1,0:T(8,128)S(1)}, u32[]{:S(2)}, u32[]{:S(2)}) collective-permute-start(f32[2,4,8,128]{3,2,1,0:T(8,128)} %get-tuple-element.22), channel_id=1, source_target_pairs={{0,1},{1,0},{2,3},{3,2},{4,5},{5,4},{6,7},{7,6},{8,9},{9,8},{10,11... | collective-permute-start | bytes 98312 | tf_op jit(solution)/shard_map/ppermute | solution.py:252
  43.9 3.7 %collective-permute-start.3 = (f32[2,4,8,128]{3,2,1,0:T(8,128)}, f32[2,4,8,128]{3,2,1,0:T(8,128)S(1)}, u32[]{:S(2)}, u32[]{:S(2)}) collective-permute-start(f32[2,4,8,128]{3,2,1,0:T(8,128)} %get-tuple-element.22), channel_id=1, source_target_pairs={{1,4},{5,8},{9,12},{4,1},{8,5},{12,9},{3,6},{7,10},{11,14},{6,3},{... | collective-permute-start | bytes 98312 | tf_op jit(solution)/shard_map/ppermute | solution.py:253
  47.6 3.2 %collective-permute-start = (f32[2,24,128]{2,1,0:T(8,128)}, f32[2,24,128]{2,1,0:T(8,128)S(1)}, u32[]{:S(2)}, u32[]{:S(2)}) collective-permute-start(f32[2,24,128]{2,1,0:T(8,128)} %get-tuple-element.20), channel_id=1, source_target_pairs={{0,128},{128,256},{256,384},{1,129},{129,257},{257,385},{2,130},{1... | collective-permute-start | bytes 73736 | tf_op jit(solution)/shard_map/ppermute | solution.py:254
  50.8 1.3 collective-permute-start.1
  52.1 3.5 %collective-permute-done.1.next_row = f32[2,24,128]{2,1,0:T(8,128)S(1)} collective-permute-done((f32[2,24,128]{2,1,0:T(8,128)}, f32[2,24,128]{2,1,0:T(8,128)S(1)}, u32[]{:S(2)}, u32[]{:S(2)}) %collective-permute-start.1) | collective-permute-done | bytes 24608 | tf_op jit(solution)/shard_map/ppermute | solution.py:255
  55.6 0.0 copy-start.1
  55.6 2.0 %shard_map.71 = (f32[16,72,128]{2,1,0:T(8,128)}, f32[2,24,128]{2,1,0:T(8,128)S(1)}, f32[2,24,128]{2,1,0:T(8,128)}, f32[2,24,128]{2,1,0:T(8,128)}, f32[2,24,128]{2,1,0:T(8,128)}) custom-call(s32[4]{0:T(128)} %pad_add_fusion.place, f32[2,24,8,128]{3,2,1,0:T(8,128)S(1)} %get-tuple-element.19.tmpl, f32[2,24,128]{2,1,0:T(8,128)S(1)} %collective-permute-done.prev_row, ...), custom_call_target="tpu_custom_call" | custom-call | tf_op jit(solution)/shard_map/pallas_call | solution.py:36
  57.6 9.7 %all-to-all-start.2 = ((f32[16,72,128]{2,1,0:T(8,128)}), f32[16,72,128]{2,1,0:T(8,128)S(1)}, u32[]{:S(2)}, u32[]{:S(2)}) async-start(f32[16,72,128]{2,1,0:T(8,128)} %get-tuple-element.29), calls=%async_computation.2 | async-start | bytes 1179648 | tf_op jit(solution)/shard_map/all_to_all | solution.py:265
  67.3 3.5 %collective-permute-start.7 = (f32[8,2,24,128]{3,2,1,0:T(8,128)S(1)}, f32[8,2,24,128]{3,2,1,0:T(8,128)S(1)}, u32[]{:S(2)}, u32[]{:S(2)}) collective-permute-start(f32[8,2,24,128]{3,2,1,0:T(8,128)S(1)} %all-to-all-done.1.mine), channel_id=1, source_target_pairs={{0,1},{1,4},{4,5},{5,8},{8,9},{9,12},{12,13},{13,128},{128,129},{1... | collective-permute-start | bytes 589832 | tf_op jit(solution)/shard_map/ppermute | solution.py:268
  70.8 1.9 %collective-permute-start.8 = (f32[8,2,24,128]{3,2,1,0:T(8,128)S(1)}, f32[8,2,24,128]{3,2,1,0:T(8,128)S(1)}, u32[]{:S(2)}, u32[]{:S(2)}) collective-permute-start(f32[8,2,24,128]{3,2,1,0:T(8,128)S(1)} %all-to-all-done.1.mine), channel_id=1, source_target_pairs={{1,0},{4,1},{5,4},{8,5},{9,8},{12,9},{13,12},{128,13},{129,128},{1... | collective-permute-start | bytes 589832 | tf_op jit(solution)/shard_map/ppermute | solution.py:269
  72.8 3.4 %collective-permute-start.10 = (f32[2,24,128]{2,1,0:T(8,128)S(1)}, f32[2,24,128]{2,1,0:T(8,128)S(1)}, u32[]{:S(2)}, u32[]{:S(2)}) collective-permute-start(f32[2,24,128]{2,1,0:T(8,128)S(1)} %copy-done.6), channel_id=1, source_target_pairs={{0,64},{16,80},{32,96},{48,112},{64,0},{80,16},{96,32},{112,48},{1... | collective-permute-start | bytes 73736 | tf_op jit(solution)/shard_map/ppermute | solution.py:281
  76.2 5.8 %collective-permute-start.11 = (f32[2,24,128]{2,1,0:T(8,128)S(1)}, f32[2,24,128]{2,1,0:T(8,128)S(1)}, u32[]{:S(2)}, u32[]{:S(2)}) collective-permute-start(f32[2,24,128]{2,1,0:T(8,128)S(1)} %copy-done.5), channel_id=1, source_target_pairs={{0,96},{16,112},{32,64},{48,80},{64,32},{80,48},{96,0},{112,16},{1... | collective-permute-start | bytes 73736 | tf_op jit(solution)/shard_map/ppermute | solution.py:281
  82.0 2.2 %collective-permute-start.9 = (f32[2,24,128]{2,1,0:T(8,128)S(1)}, f32[2,24,128]{2,1,0:T(8,128)S(1)}, u32[]{:S(2)}, u32[]{:S(2)}) collective-permute-start(f32[2,24,128]{2,1,0:T(8,128)S(1)} %copy-done.4), channel_id=1, source_target_pairs={{0,32},{16,48},{32,0},{48,16},{64,96},{80,112},{96,64},{112,80},{1... | collective-permute-start | bytes 73736 | tf_op jit(solution)/shard_map/ppermute | solution.py:281
  84.2 0.8 shard_map.72
  85.0 21.6 %all-to-all-done.2.got = f32[16,72,128]{2,1,0:T(8,128)S(1)} async-done(((f32[16,72,128]{2,1,0:T(8,128)}), f32[16,72,128]{2,1,0:T(8,128)S(1)}, u32[]{:S(2)}, u32[]{:S(2)}) %all-to-all-start.2) | async-done | bytes 589856 | tf_op jit(solution)/shard_map/all_to_all | solution.py:265
  106.6 3.0 %shard_map.73 = f32[32,54,128]{2,1,0:T(8,128)} custom-call(s32[4]{0:T(128)} %pad_add_fusion.place, f32[8,2,24,128]{3,2,1,0:T(8,128)S(1)} %collective-permute-done.7.prev, f32[8,2,24,128]{3,2,1,0:T(8,128)S(1)} %all-to-all-done.1.mine, f32[8,2,24,128]{3,2,1,0:T(8,128)S(1)} %collective-permute-done.8.succ, f32[16,72,128]{2,1,0:T(8,128)S(1)} %all-to-all-done.2.got, ...), custom_call_target="tpu_custom_call" | custom-call | tf_op jit(solution)/shard_map/pallas_call | solution.py:36
  109.6 4.5 %all-to-all-start.3 = ((f32[32,54,128]{2,1,0:T(8,128)}), f32[32,54,128]{2,1,0:T(8,128)S(1)}, u32[]{:S(2)}, u32[]{:S(2)}) async-start(f32[32,54,128]{2,1,0:T(8,128)} %shard_map.73), calls=%async_computation.3 | async-start | bytes 1835008 | tf_op jit(solution)/shard_map/all_to_all | solution.py:289
  114.2 1.9 %collective-permute-start.12 = (f32[24,128]{1,0:T(8,128)S(1)}, f32[24,128]{1,0:T(8,128)S(1)}, u32[]{:S(2)}, u32[]{:S(2)}) collective-permute-start(f32[24,128]{1,0:T(8,128)S(1)} %dynamic-slice_bitcast_fusion), channel_id=1, source_target_pairs={{0,16},{16,0},{32,48},{48,32},{64,80},{80,64},{96,112},{112,96},{1... | collective-permute-start | bytes 36872 | tf_op jit(solution)/shard_map/ppermute | solution.py:285
  116.1 2.8 %collective-permute-done.12 = f32[24,128]{1,0:T(8,128)S(1)} collective-permute-done((f32[24,128]{1,0:T(8,128)S(1)}, f32[24,128]{1,0:T(8,128)S(1)}, u32[]{:S(2)}, u32[]{:S(2)}) %collective-permute-start.12) | collective-permute-done | bytes 12320 | tf_op jit(solution)/shard_map/ppermute | solution.py:285
  119.0 0.6 fusion
  119.6 10.4 %all-to-all-done.3.packed = f32[32,54,128]{2,1,0:T(8,128)S(1)} async-done(((f32[32,54,128]{2,1,0:T(8,128)}), f32[32,54,128]{2,1,0:T(8,128)S(1)}, u32[]{:S(2)}, u32[]{:S(2)}) %all-to-all-start.3) | async-done | bytes 884768 | tf_op jit(solution)/shard_map/all_to_all | solution.py:289
  130.0 1.2 shard_map.74
  (32 shorter events, 0.1 us)
Async XLA Ops:
  0.6 0.7 copy-start.2
  2.0 28.5 %all-to-all-start = ((f32[16,24,128]{2,1,0:T(8,128)}), f32[16,24,128]{2,1,0:T(8,128)}, u32[]{:S(2)}, u32[]{:S(2)}) async-start(f32[16,24,128]{2,1,0:T(8,128)} %shard_map.68), calls=%async_computation | async-start | bytes 393216 | tf_op jit(solution)/shard_map/all_to_all | solution.py:239
  19.8 27.7 %collective-permute-start.4 = (f32[6,12,8,128]{3,2,1,0:T(8,128)}, f32[6,12,8,128]{3,2,1,0:T(8,128)S(1)}, u32[]{:S(2)}, u32[]{:S(2)}) collective-permute-start(f32[6,12,8,128]{3,2,1,0:T(8,128)} %get-tuple-element.24), channel_id=1, source_target_pairs={{0,128},{128,256},{256,384},{384,0},{1,129},{129,257},{257,385},{3... | collective-permute-start | bytes 884744 | tf_op jit(solution)/shard_map/ppermute | solution.py:245
  23.0 27.8 %collective-permute-start.5 = (f32[6,12,8,128]{3,2,1,0:T(8,128)}, f32[6,12,8,128]{3,2,1,0:T(8,128)S(1)}, u32[]{:S(2)}, u32[]{:S(2)}) collective-permute-start(f32[6,12,8,128]{3,2,1,0:T(8,128)} %get-tuple-element.25), channel_id=1, source_target_pairs={{0,256},{128,384},{256,0},{384,128},{1,257},{129,385},{257,1},{385... | collective-permute-start | bytes 884744 | tf_op jit(solution)/shard_map/ppermute | solution.py:245
  27.6 24.5 %collective-permute-start.6 = (f32[6,12,8,128]{3,2,1,0:T(8,128)}, f32[6,12,8,128]{3,2,1,0:T(8,128)S(1)}, u32[]{:S(2)}, u32[]{:S(2)}) collective-permute-start(f32[6,12,8,128]{3,2,1,0:T(8,128)} %get-tuple-element.26), channel_id=1, source_target_pairs={{0,384},{128,0},{256,128},{384,256},{1,385},{129,1},{257,129},{385... | collective-permute-start | bytes 884744 | tf_op jit(solution)/shard_map/ppermute | solution.py:245
  30.6 27.0 %all-to-all-start.1 = ((f32[8,2,24,128]{3,2,1,0:T(8,128)}), f32[8,2,24,128]{3,2,1,0:T(8,128)S(1)}, u32[]{:S(2)}, u32[]{:S(2)}) async-start(f32[8,2,24,128]{3,2,1,0:T(8,128)} %bitcast.4.gathered), calls=%async_computation.1 | async-start | bytes 393216 | tf_op jit(solution)/shard_map/all_to_all | solution.py:257
  42.0 13.6 %collective-permute-start.2 = (f32[2,4,8,128]{3,2,1,0:T(8,128)}, f32[2,4,8,128]{3,2,1,0:T(8,128)S(1)}, u32[]{:S(2)}, u32[]{:S(2)}) collective-permute-start(f32[2,4,8,128]{3,2,1,0:T(8,128)} %get-tuple-element.22), channel_id=1, source_target_pairs={{0,1},{1,0},{2,3},{3,2},{4,5},{5,4},{6,7},{7,6},{8,9},{9,8},{10,11... | collective-permute-start | bytes 98312 | tf_op jit(solution)/shard_map/ppermute | solution.py:252
  43.9 11.7 %collective-permute-start.3 = (f32[2,4,8,128]{3,2,1,0:T(8,128)}, f32[2,4,8,128]{3,2,1,0:T(8,128)S(1)}, u32[]{:S(2)}, u32[]{:S(2)}) collective-permute-start(f32[2,4,8,128]{3,2,1,0:T(8,128)} %get-tuple-element.22), channel_id=1, source_target_pairs={{1,4},{5,8},{9,12},{4,1},{8,5},{12,9},{3,6},{7,10},{11,14},{6,3},{... | collective-permute-start | bytes 98312 | tf_op jit(solution)/shard_map/ppermute | solution.py:253
  47.6 4.5 %collective-permute-start = (f32[2,24,128]{2,1,0:T(8,128)}, f32[2,24,128]{2,1,0:T(8,128)S(1)}, u32[]{:S(2)}, u32[]{:S(2)}) collective-permute-start(f32[2,24,128]{2,1,0:T(8,128)} %get-tuple-element.20), channel_id=1, source_target_pairs={{0,128},{128,256},{256,384},{1,129},{129,257},{257,385},{2,130},{1... | collective-permute-start | bytes 73736 | tf_op jit(solution)/shard_map/ppermute | solution.py:254
  50.8 4.8 %collective-permute-start.1 = (f32[2,24,128]{2,1,0:T(8,128)}, f32[2,24,128]{2,1,0:T(8,128)S(1)}, u32[]{:S(2)}, u32[]{:S(2)}) collective-permute-start(f32[2,24,128]{2,1,0:T(8,128)} %get-tuple-element.21), channel_id=1, source_target_pairs={{128,0},{256,128},{384,256},{129,1},{257,129},{385,257},{130,2},{2... | collective-permute-start | bytes 73736 | tf_op jit(solution)/shard_map/ppermute | solution.py:255
  55.6 28.6 %copy-start = (f32[192,192]{1,0:T(8,128)S(1)}, f32[192,192]{1,0:T(8,128)}, u32[]{:S(2)}) copy-start(f32[192,192]{1,0:T(8,128)} %zk.1) | copy-start | bytes 442372
  55.6 28.6 %copy-start.1 = (f32[192,192]{1,0:T(8,128)S(1)}, f32[192,192]{1,0:T(8,128)}, u32[]{:S(2)}) copy-start(f32[192,192]{1,0:T(8,128)} %xk.1) | copy-start | bytes 442372
  57.6 15.2 %copy-start.6 = (f32[2,24,128]{2,1,0:T(8,128)S(1)}, f32[2,24,128]{2,1,0:T(8,128)}, u32[]{:S(2)}) copy-start(f32[2,24,128]{2,1,0:T(8,128)} %get-tuple-element.34) | copy-start | bytes 73732
  57.6 18.6 %copy-start.5 = (f32[2,24,128]{2,1,0:T(8,128)S(1)}, f32[2,24,128]{2,1,0:T(8,128)}, u32[]{:S(2)}) copy-start(f32[2,24,128]{2,1,0:T(8,128)} %get-tuple-element.35) | copy-start | bytes 73732
  57.6 24.4 %copy-start.4 = (f32[2,24,128]{2,1,0:T(8,128)S(1)}, f32[2,24,128]{2,1,0:T(8,128)}, u32[]{:S(2)}) copy-start(f32[2,24,128]{2,1,0:T(8,128)} %get-tuple-element.33) | copy-start | bytes 73732
  57.6 49.0 %all-to-all-start.2 = ((f32[16,72,128]{2,1,0:T(8,128)}), f32[16,72,128]{2,1,0:T(8,128)S(1)}, u32[]{:S(2)}, u32[]{:S(2)}) async-start(f32[16,72,128]{2,1,0:T(8,128)} %get-tuple-element.29), calls=%async_computation.2 | async-start | bytes 1179648 | tf_op jit(solution)/shard_map/all_to_all | solution.py:265
  67.3 17.7 %collective-permute-start.7 = (f32[8,2,24,128]{3,2,1,0:T(8,128)S(1)}, f32[8,2,24,128]{3,2,1,0:T(8,128)S(1)}, u32[]{:S(2)}, u32[]{:S(2)}) collective-permute-start(f32[8,2,24,128]{3,2,1,0:T(8,128)S(1)} %all-to-all-done.1.mine), channel_id=1, source_target_pairs={{0,1},{1,4},{4,5},{5,8},{8,9},{9,12},{12,13},{13,128},{128,129},{1... | collective-permute-start | bytes 589832 | tf_op jit(solution)/shard_map/ppermute | solution.py:268
  70.8 14.2 %collective-permute-start.8 = (f32[8,2,24,128]{3,2,1,0:T(8,128)S(1)}, f32[8,2,24,128]{3,2,1,0:T(8,128)S(1)}, u32[]{:S(2)}, u32[]{:S(2)}) collective-permute-start(f32[8,2,24,128]{3,2,1,0:T(8,128)S(1)} %all-to-all-done.1.mine), channel_id=1, source_target_pairs={{1,0},{4,1},{5,4},{8,5},{9,8},{12,9},{13,12},{128,13},{129,128},{1... | collective-permute-start | bytes 589832 | tf_op jit(solution)/shard_map/ppermute | solution.py:269
  72.8 41.4 %collective-permute-start.10 = (f32[2,24,128]{2,1,0:T(8,128)S(1)}, f32[2,24,128]{2,1,0:T(8,128)S(1)}, u32[]{:S(2)}, u32[]{:S(2)}) collective-permute-start(f32[2,24,128]{2,1,0:T(8,128)S(1)} %copy-done.6), channel_id=1, source_target_pairs={{0,64},{16,80},{32,96},{48,112},{64,0},{80,16},{96,32},{112,48},{1... | collective-permute-start | bytes 73736 | tf_op jit(solution)/shard_map/ppermute | solution.py:281
  76.2 38.0 %collective-permute-start.11 = (f32[2,24,128]{2,1,0:T(8,128)S(1)}, f32[2,24,128]{2,1,0:T(8,128)S(1)}, u32[]{:S(2)}, u32[]{:S(2)}) collective-permute-start(f32[2,24,128]{2,1,0:T(8,128)S(1)} %copy-done.5), channel_id=1, source_target_pairs={{0,96},{16,112},{32,64},{48,80},{64,32},{80,48},{96,0},{112,16},{1... | collective-permute-start | bytes 73736 | tf_op jit(solution)/shard_map/ppermute | solution.py:281
  82.0 32.2 %collective-permute-start.9 = (f32[2,24,128]{2,1,0:T(8,128)S(1)}, f32[2,24,128]{2,1,0:T(8,128)S(1)}, u32[]{:S(2)}, u32[]{:S(2)}) collective-permute-start(f32[2,24,128]{2,1,0:T(8,128)S(1)} %copy-done.4), channel_id=1, source_target_pairs={{0,32},{16,48},{32,0},{48,16},{64,96},{80,112},{96,64},{112,80},{1... | collective-permute-start | bytes 73736 | tf_op jit(solution)/shard_map/ppermute | solution.py:281
  109.6 9.4 %copy-start.3 = (f32[12,1,192]{2,1,0:T(1,128)S(1)}, f32[12,1,192]{2,1,0:T(1,128)}, u32[]{:S(2)}) copy-start(f32[12,1,192]{2,1,0:T(1,128)} %row.1) | copy-start | bytes 27652
  109.6 20.4 %all-to-all-start.3 = ((f32[32,54,128]{2,1,0:T(8,128)}), f32[32,54,128]{2,1,0:T(8,128)S(1)}, u32[]{:S(2)}, u32[]{:S(2)}) async-start(f32[32,54,128]{2,1,0:T(8,128)} %shard_map.73), calls=%async_computation.3 | async-start | bytes 1835008 | tf_op jit(solution)/shard_map/all_to_all | solution.py:289
  114.2 4.7 %collective-permute-start.12 = (f32[24,128]{1,0:T(8,128)S(1)}, f32[24,128]{1,0:T(8,128)S(1)}, u32[]{:S(2)}, u32[]{:S(2)}) collective-permute-start(f32[24,128]{1,0:T(8,128)S(1)} %dynamic-slice_bitcast_fusion), channel_id=1, source_target_pairs={{0,16},{16,0},{32,48},{48,32},{64,80},{80,64},{96,112},{112,96},{1... | collective-permute-start | bytes 36872 | tf_op jit(solution)/shard_map/ppermute | solution.py:285

commit v8 on v7

--- a/solution.py
+++ b/solution.py
@@ -79,38 +79,33 @@
             out[4 + k] = jnp.concatenate([first[:, rows, LANES:], second[:, rows, LANES:]], -1)
 
 
-def halo_kernel(place, gathered, tmpl, ends, first, last):
+def spread_kernel(place, gathered, tmpl, out):
+    zh, c = place[1], place[2]
     for h in range(2):
         for k in range(3):
-            block = jnp.swapaxes(gathered[:, h, 8 * k : 8 * k + 8], 0, 1)
-            tmpl[h, 8 * k : 8 * k + 8] = block
-            for i, p in enumerate((0, 11, 12, 23)):
-                if p // 8 == k:
-                    ends[h, i] = block[p % 8]
-        first[h] = gathered[0, h]
-        last[h] = gathered[7, h]
-
-
-def residual_kernel(place, tmpl, prev_row, next_row, by_core, by_x, *rest):
+            tmpl[h, 8 * k : 8 * k + 8] = jnp.swapaxes(gathered[:, h, 8 * k : 8 * k + 8], 0, 1)
+    near, far = 11 * (1 - c), 11 * c
+    ends = [tmpl[zh, near], tmpl[zh, 12 + near], tmpl[1 - zh, far], tmpl[1 - zh, 12 + far]]
+    for i in range(8):
+        out[i, :24] = gathered[i, 0]
+        out[i, 24:48] = gathered[i, 1]
+        for k, end in enumerate(ends):
+            out[i, 48 + 8 * k : 56 + 8 * k] = end
+
+
+def residual_kernel(place, tmpl, prev_row, next_row, mixed, *rest):
     raws, out, parts, (rows, total) = rest[:4], rest[4], rest[5:9], rest[9:]
-    zh, c, zl = place[1], place[2], place[3]
+    zh, c, zl, x = place[1], place[2], place[3], place[4]
     low, high = tmpl[zh, :12], tmpl[zh, 12:]
     here = jnp.concatenate([low, high], -1)
 
-    at_x = jnp.logical_and(c == 0, zh == 0)
-    z_from = jnp.where(c == 0, 1 - zh, zh)
-    before = jnp.where(
-        at_x,
-        jnp.concatenate([by_x[1, 1], by_x[1, 3]], -1),
-        jnp.concatenate([by_core[z_from, 1], by_core[z_from, 3]], -1),
-    )
-    at_x = jnp.logical_and(c == 1, zh == 1)
-    z_from = jnp.where(c == 0, zh, 1 - zh)
-    after = jnp.where(
-        at_x,
-        jnp.concatenate([by_x[0, 0], by_x[0, 2]], -1),
-        jnp.concatenate([by_core[z_from, 0], by_core[z_from, 2]], -1),
-    )
+    step = jnp.where(c == 0, zh - 1, zh)
+    inside = jnp.logical_and(x + step >= 0, x + step < 4)
+    chip = jnp.clip(x + step, 0, 3)
+    near = jnp.concatenate([mixed[2 * x + 1 - c, 48:56], mixed[2 * x + 1 - c, 56:64]], -1)
+    far = jnp.concatenate([mixed[2 * chip + 1 - c, 64:72], mixed[2 * chip + 1 - c, 72:80]], -1)
+    far = jnp.where(inside, far, 0.0)
+    before, after = jnp.where(c == 0, far, near), jnp.where(c == 0, near, far)
     up = jnp.concatenate([here[1:], after[None]], 0)
     down = jnp.concatenate([before[None], here[:-1]], 0)
     slope_z = (up - down) * 0.5
@@ -170,7 +165,7 @@
         for x in range(4):
             for h in range(2):
                 at = 8 + 48 * x + 24 * h
-                first, second = ref[2 * x, h], ref[2 * x + 1, h]
+                first, second = (ref[2 * x + c, 24 * h : 24 * h + 24] for c in range(2))
                 grid[r, at : at + 24, :LANES] = jnp.concatenate([first[:12], second[:12]], 0)
                 grid[r, at : at + 24, LANES:] = jnp.concatenate([first[12:], second[12:]], 0)
     here = grid[1, 8:200]
@@ -233,7 +228,7 @@
 
 
 def per_device(image, velocity, template, z_kernel, x_kernel):
-    place = jnp.stack([lax.axis_index(a) for a in ("y", "zh", "c", "zl")]).astype(jnp.int32)
+    place = jnp.stack([lax.axis_index(a) for a in ("y", "zh", "c", "zl", "x")]).astype(jnp.int32)
 
     (piece,) = call(piece_kernel, (shape(16, 24, LANES),))(None, template)
     gathered = lax.all_to_all(piece, COL, 0, 0, tiled=True).reshape(8, 2, 24, LANES)
@@ -241,32 +236,25 @@
     raws = call(
         pack_kernel, (held(6, 12, 8, LANES), *[shape(6, 12, 8, LANES)] * 3), pin=False
     )(place, image[0], velocity[0])
-    raws = [raws[0]] + [
-        lax.ppermute(raws[s], "y", [(i, (i + s) % 4) for i in range(4)]) for s in (1, 2, 3)
-    ]
-
-    tmpl, ends, first, last = call(
-        halo_kernel,
-        (held(2, 24, 8, LANES), *[shape(2, 4, 8, LANES), shape(2, 24, LANES), shape(2, 24, LANES)]),
-    )(place, gathered)
-    by_core = lax.ppermute(ends, "c", [(0, 1), (1, 0)])
-    by_x = lax.ppermute(ends, ("x", "c"), [(2 * i + 1, 2 * i + 2) for i in range(3)] + [(2 * i + 2, 2 * i + 1) for i in range(3)])
-    prev_row = lax.ppermute(last, "y", [(i, i + 1) for i in range(3)])
-    next_row = lax.ppermute(first, "y", [(i + 1, i) for i in range(3)])
-
-    mine = lax.all_to_all(gathered, ("x", "c"), 0, 0, tiled=True)
+    raws = list(raws)
+    for s in (2, 1, 3):
+        raws[s] = lax.ppermute(raws[s], "y", [(i, (i + s) % 4) for i in range(4)])
+
+    prev_row = lax.ppermute(gathered[7], "y", [(i, i + 1) for i in range(3)])
+    next_row = lax.ppermute(gathered[0], "y", [(i + 1, i) for i in range(3)])
+    tmpl, mixed = call(spread_kernel, (held(2, 24, 8, LANES), shape(8, 80, LANES)))(place, gathered)
+    mixed = lax.all_to_all(mixed, ("x", "c"), 0, 0, tiled=True)
 
     by_row, *parts = call(
         residual_kernel,
         (shape(16, 72, LANES), held(2, 24, LANES), *[shape(2, 24, LANES)] * 3),
         (pltpu.VMEM((96, 8, LANES), F32), pltpu.VMEM((8, 24, LANES), F32)),
-    )(place, tmpl, prev_row, next_row, by_core, by_x, *raws)
-    by_row, mine = lax.optimization_barrier((by_row, mine))
+    )(place, tmpl, prev_row, next_row, mixed, *raws)
     got = lax.all_to_all(by_row, ("x", "zh", "c"), 0, 0, tiled=True)
 
     along = [(i, i + 1) for i in range(31)]
-    prev = lax.ppermute(mine, ROW, along)
-    succ = lax.ppermute(mine, ROW, [(j, i) for i, j in along])
+    prev = lax.ppermute(mixed, ROW, along)
+    succ = lax.ppermute(mixed, ROW, [(j, i) for i, j in along])
     zw, xw = call(
         weights_kernel,
         (pltpu.VMEM((2, 96, 192), BF16), pltpu.VMEM((2, 2, 256, 192), BF16)),
@@ -276,7 +264,7 @@
         main_kernel,
         (shape(32, 54, LANES),),
         (pltpu.VMEM((3, 208, WIDE), F32), pltpu.VMEM((192, 18 * LANES), F32)),
-    )(place, prev, mine, succ, got, zw, xw)
+    )(place, prev, mixed, succ, got, zw, xw)
     for t in (1, 2, 3):
         parts[t] = lax.ppermute(parts[t], "zl", [(i, i ^ (2 * t)) for i in range(8)])
     two, odd = sum(parts), lax.axis_index("zl") & 1

time: 132 us -> 127 us (0.962)
  starting transfers between devices: 78.2 us -> 75.4 us
  waiting for transfers between devices: 38.3 us -> 36.4 us
    ppermute x9 -> x7, starting transfers between devices: 26.2 us -> 20.6 us  [the longest x3 10.7 us: per_device(): raws[s] = lax.ppermute(raws[s], 'y', [(i, (i + s) % 4) for i in range(4)])]
    ppermute x3, starting transfers between devices: 11.4 us -> 13.2 us  [per_device(): parts[t] = lax.ppermute(parts[t], 'zl', [(i, i ^ 2 * t) for i in range(8)])]
    all_to_all x1, waiting for transfers between devices: 21.6 us -> 19.9 us  [per_device(): got = lax.all_to_all(by_row, ('x', 'zh', 'c'), 0, 0, tiled=True)]
    ppermute x9 -> x7, waiting for transfers between devices: 3.48 us -> 3.32 us  [the longest x1 3.3 us: per_device(): next_row = lax.ppermute(gathered[0], 'y', [(i + 1, i) for i in range(3)])]
  transfers between devices with their start and end apart: 17 -> 15, of which waited for: 4 -> 4; matrix products, arithmetic and copies ran while one was open for 1% -> 1% of each run, Pallas kernels for 8% -> 6%
where the time goes in v8:
time: 127 us; the launch traced here: 126 us
  starting transfers between devices  75.4 us (59%)
  waiting for transfers between devices  36.4 us (29%)
  Pallas kernels  11.6 us (9%)
  local copies, waits for them, and re-layouts  1.33 us (1%)
    all_to_all x1, waiting for transfers between devices, per_device(): got = lax.all_to_all(by_row, ('x', 'zh', 'c'), 0, 0, tiled=True)  19.9 us
    all_to_all x1, starting transfers between devices, per_device(): lax.all_to_all(piece, COL, 0, 0, tiled=True).reshape(8, 2, 24, LANES)  14.7 us
    ppermute x3, starting transfers between devices, per_device(): parts[t] = lax.ppermute(parts[t], 'zl', [(i, i ^ 2 * t) for i in range(8)])  13.2 us
    pallas_call x7, Pallas kernels, run(): pl.pallas_call(kernel, out_shape=outs, in_specs=[*[smem()] * len(first),...  11.6 us
    all_to_all x1, starting transfers between devices, per_device(): got = lax.all_to_all(by_row, ('x', 'zh', 'c'), 0, 0, tiled=True)  10.8 us
    ppermute x3, starting transfers between devices, per_device(): raws[s] = lax.ppermute(raws[s], 'y', [(i, (i + s) % 4) for i in range(4)])  10.7 us
    all_to_all x1, waiting for transfers between devices, per_device(): back = lax.all_to_all(packed, ROW, 0, 0, tiled=True)  10.4 us
    all_to_all x1, starting transfers between devices, per_device(): mixed = lax.all_to_all(mixed, ('x', 'c'), 0, 0, tiled=True)  9.74 us
  transfers between devices with their start and end apart: 15, of which 4 were waited for; matrix products, arithmetic and copies ran while one was open for 1% of the time, Pallas kernels for 6%

profile of v8, /device:TPU:33, one launch (start us, length us, event | category | flops | bytes accessed | tf_op | source)
XLA Modules:
  0.0 126.3 jit_solution(2205845871676154494)
XLA Ops:
  0.6 0.0 copy-start.2
  0.6 0.7 copy-done.2
  1.3 0.7 shard_map.68
  2.0 14.7 %all-to-all-start = ((f32[16,24,128]{2,1,0:T(8,128)}), f32[16,24,128]{2,1,0:T(8,128)S(1)}, u32[]{:S(2)}, u32[]{:S(2)}) async-start(f32[16,24,128]{2,1,0:T(8,128)} %shard_map.68), calls=%async_computation | async-start | bytes 393216 | tf_op jit(solution)/shard_map/all_to_all | solution.py:234
  16.7 0.6 stack.23.place
  17.3 2.5 %shard_map.70 = (f32[6,12,8,128]{3,2,1,0:T(8,128)S(1)}, f32[6,12,8,128]{3,2,1,0:T(8,128)}, f32[6,12,8,128]{3,2,1,0:T(8,128)}, f32[6,12,8,128]{3,2,1,0:T(8,128)}) custom-call(s32[5]{0:T(128)} %stack.23.place, f32[12,32,192]{2,1,0:T(8,128)} %bitcast.18, f32[3,12,32,192]{3,2,1,0:T(8,128)} %bitcast.16), custom_call_target="tpu_custom_call" | custom-call | tf_op jit(solution)/shard_map/pallas_call | solution.py:36
  19.8 3.2 %collective-permute-start.4 = (f32[6,12,8,128]{3,2,1,0:T(8,128)}, f32[6,12,8,128]{3,2,1,0:T(8,128)S(1)}, u32[]{:S(2)}, u32[]{:S(2)}) collective-permute-start(f32[6,12,8,128]{3,2,1,0:T(8,128)} %get-tuple-element.18), channel_id=1, source_target_pairs={{0,128},{128,256},{256,384},{384,0},{1,129},{129,257},{257,385},{3... | collective-permute-start | bytes 884744 | tf_op jit(solution)/shard_map/ppermute | solution.py:241
  23.0 4.5 %collective-permute-start.5 = (f32[6,12,8,128]{3,2,1,0:T(8,128)}, f32[6,12,8,128]{3,2,1,0:T(8,128)S(1)}, u32[]{:S(2)}, u32[]{:S(2)}) collective-permute-start(f32[6,12,8,128]{3,2,1,0:T(8,128)} %get-tuple-element.19), channel_id=1, source_target_pairs={{0,256},{128,384},{256,0},{384,128},{1,257},{129,385},{257,1},{385... | collective-permute-start | bytes 884744 | tf_op jit(solution)/shard_map/ppermute | solution.py:241
  27.5 3.0 %collective-permute-start.6 = (f32[6,12,8,128]{3,2,1,0:T(8,128)}, f32[6,12,8,128]{3,2,1,0:T(8,128)S(1)}, u32[]{:S(2)}, u32[]{:S(2)}) collective-permute-start(f32[6,12,8,128]{3,2,1,0:T(8,128)} %get-tuple-element.20), channel_id=1, source_target_pairs={{0,384},{128,0},{256,128},{384,256},{1,385},{129,1},{257,129},{385... | collective-permute-start | bytes 884744 | tf_op jit(solution)/shard_map/ppermute | solution.py:241
  30.5 1.4 %shard_map.69 = (f32[2,24,8,128]{3,2,1,0:T(8,128)S(1)}, f32[8,80,128]{2,1,0:T(8,128)}) custom-call(s32[5]{0:T(128)} %stack.23.place, f32[8,2,24,128]{3,2,1,0:T(8,128)S(1)} %bitcast.15), custom_call_target="tpu_custom_call" | custom-call | tf_op jit(solution)/shard_map/pallas_call | solution.py:36
  31.9 9.7 %all-to-all-start.1 = ((f32[8,80,128]{2,1,0:T(8,128)}), f32[8,80,128]{2,1,0:T(8,128)S(1)}, u32[]{:S(2)}, u32[]{:S(2)}) async-start(f32[8,80,128]{2,1,0:T(8,128)} %get-tuple-element.15), calls=%async_computation.1 | async-start | bytes 655360 | tf_op jit(solution)/shard_map/all_to_all | solution.py:246
  41.7 3.2 %collective-permute-start.2 = (f32[2,24,128]{2,1,0:T(8,128)S(1)}, f32[2,24,128]{2,1,0:T(8,128)S(1)}, u32[]{:S(2)}, u32[]{:S(2)}) collective-permute-start(f32[2,24,128]{2,1,0:T(8,128)S(1)} %get-tuple-element.29), channel_id=1, source_target_pairs={{0,128},{128,256},{256,384},{1,129},{129,257},{257,385},{2,130},{1... | collective-permute-start | bytes 73736 | tf_op jit(solution)/shard_map/ppermute | solution.py:243
  44.9 1.3 %collective-permute-start.3 = (f32[2,24,128]{2,1,0:T(8,128)S(1)}, f32[2,24,128]{2,1,0:T(8,128)S(1)}, u32[]{:S(2)}, u32[]{:S(2)}) collective-permute-start(f32[2,24,128]{2,1,0:T(8,128)S(1)} %get-tuple-element.28), channel_id=1, source_target_pairs={{128,0},{256,128},{384,256},{129,1},{257,129},{385,257},{130,2},{2... | collective-permute-start | bytes 73736 | tf_op jit(solution)/shard_map/ppermute | solution.py:244
  46.2 0.0 collective-permute-done.4.rest_1_
  46.2 0.0 collective-permute-done.6.rest_3_
  46.2 3.3 %collective-permute-done.3.next_row = f32[2,24,128]{2,1,0:T(8,128)S(1)} collective-permute-done((f32[2,24,128]{2,1,0:T(8,128)S(1)}, f32[2,24,128]{2,1,0:T(8,128)S(1)}, u32[]{:S(2)}, u32[]{:S(2)}) %collective-permute-start.3) | collective-permute-done | bytes 24608 | tf_op jit(solution)/shard_map/ppermute | solution.py:244
  49.6 2.0 %shard_map.71 = (f32[16,72,128]{2,1,0:T(8,128)}, f32[2,24,128]{2,1,0:T(8,128)S(1)}, f32[2,24,128]{2,1,0:T(8,128)}, f32[2,24,128]{2,1,0:T(8,128)}, f32[2,24,128]{2,1,0:T(8,128)}) custom-call(s32[5]{0:T(128)} %stack.23.place, f32[2,24,8,128]{3,2,1,0:T(8,128)S(1)} %get-tuple-element.16.tmpl, f32[2,24,128]{2,1,0:T(8,128)S(1)} %collective-permute-done.2.prev_row, ...), custom_call_target="tpu_custom_call" | custom-call | tf_op jit(solution)/shard_map/pallas_call | solution.py:36
  51.5 10.8 %all-to-all-start.2 = ((f32[16,72,128]{2,1,0:T(8,128)}), f32[16,72,128]{2,1,0:T(8,128)S(1)}, u32[]{:S(2)}, u32[]{:S(2)}) async-start(f32[16,72,128]{2,1,0:T(8,128)} %get-tuple-element.21), calls=%async_computation.2 | async-start | bytes 1179648 | tf_op jit(solution)/shard_map/all_to_all | solution.py:253
  62.3 3.5 %collective-permute-start = (f32[8,80,128]{2,1,0:T(8,128)S(1)}, f32[8,80,128]{2,1,0:T(8,128)S(1)}, u32[]{:S(2)}, u32[]{:S(2)}) collective-permute-start(f32[8,80,128]{2,1,0:T(8,128)S(1)} %all-to-all-done.1.mixed.mine), channel_id=1, source_target_pairs={{0,1},{1,4},{4,5},{5,8},{8,9},{9,12},{12,13},{13,128},{128,129},{1... | collective-permute-start | bytes 983048 | tf_op jit(solution)/shard_map/ppermute | solution.py:256
  65.8 1.9 %collective-permute-start.1 = (f32[8,80,128]{2,1,0:T(8,128)S(1)}, f32[8,80,128]{2,1,0:T(8,128)S(1)}, u32[]{:S(2)}, u32[]{:S(2)}) collective-permute-start(f32[8,80,128]{2,1,0:T(8,128)S(1)} %all-to-all-done.1.mixed.mine), channel_id=1, source_target_pairs={{1,0},{4,1},{5,4},{8,5},{9,8},{12,9},{13,12},{128,13},{129,128},{1... | collective-permute-start | bytes 983048 | tf_op jit(solution)/shard_map/ppermute | solution.py:257
  67.8 2.2 %collective-permute-start.7 = (f32[2,24,128]{2,1,0:T(8,128)S(1)}, f32[2,24,128]{2,1,0:T(8,128)S(1)}, u32[]{:S(2)}, u32[]{:S(2)}) collective-permute-start(f32[2,24,128]{2,1,0:T(8,128)S(1)} %copy-done.6), channel_id=1, source_target_pairs={{0,32},{16,48},{32,0},{48,16},{64,96},{80,112},{96,64},{112,80},{1... | collective-permute-start | bytes 73736 | tf_op jit(solution)/shard_map/ppermute | solution.py:269
  70.0 3.3 %collective-permute-start.8 = (f32[2,24,128]{2,1,0:T(8,128)S(1)}, f32[2,24,128]{2,1,0:T(8,128)S(1)}, u32[]{:S(2)}, u32[]{:S(2)}) collective-permute-start(f32[2,24,128]{2,1,0:T(8,128)S(1)} %copy-done.5), channel_id=1, source_target_pairs={{0,64},{16,80},{32,96},{48,112},{64,0},{80,16},{96,32},{112,48},{1... | collective-permute-start | bytes 73736 | tf_op jit(solution)/shard_map/ppermute | solution.py:269
  73.2 7.7 %collective-permute-start.9 = (f32[2,24,128]{2,1,0:T(8,128)S(1)}, f32[2,24,128]{2,1,0:T(8,128)S(1)}, u32[]{:S(2)}, u32[]{:S(2)}) collective-permute-start(f32[2,24,128]{2,1,0:T(8,128)S(1)} %copy-done.4), channel_id=1, source_target_pairs={{0,96},{16,112},{32,64},{48,80},{64,32},{80,48},{96,0},{112,16},{1... | collective-permute-start | bytes 73736 | tf_op jit(solution)/shard_map/ppermute | solution.py:269
  81.0 0.8 shard_map.72
  81.8 19.9 %all-to-all-done.2.got = f32[16,72,128]{2,1,0:T(8,128)S(1)} async-done(((f32[16,72,128]{2,1,0:T(8,128)}), f32[16,72,128]{2,1,0:T(8,128)S(1)}, u32[]{:S(2)}, u32[]{:S(2)}) %all-to-all-start.2) | async-done | bytes 589856 | tf_op jit(solution)/shard_map/all_to_all | solution.py:253
  101.7 3.0 %shard_map.73 = f32[32,54,128]{2,1,0:T(8,128)} custom-call(s32[5]{0:T(128)} %stack.23.place, f32[8,80,128]{2,1,0:T(8,128)S(1)} %collective-permute-done.prev, f32[8,80,128]{2,1,0:T(8,128)S(1)} %all-to-all-done.1.mixed.mine, f32[8,80,128]{2,1,0:T(8,128)S(1)} %collective-permute-done.1.succ, f32[16,72,128]{2,1,0:T(8,128)S(1)} %all-to-all-done.2.got, ...), custom_call_target="tpu_custom_call" | custom-call | tf_op jit(solution)/shard_map/pallas_call | solution.py:36
  104.7 4.5 %all-to-all-start.3 = ((f32[32,54,128]{2,1,0:T(8,128)}), f32[32,54,128]{2,1,0:T(8,128)S(1)}, u32[]{:S(2)}, u32[]{:S(2)}) async-start(f32[32,54,128]{2,1,0:T(8,128)} %shard_map.73), calls=%async_computation.3 | async-start | bytes 1835008 | tf_op jit(solution)/shard_map/all_to_all | solution.py:277
  109.3 1.9 %collective-permute-start.10 = (f32[24,128]{1,0:T(8,128)S(1)}, f32[24,128]{1,0:T(8,128)S(1)}, u32[]{:S(2)}, u32[]{:S(2)}) collective-permute-start(f32[24,128]{1,0:T(8,128)S(1)} %dynamic-slice_bitcast_fusion), channel_id=1, source_target_pairs={{0,16},{16,0},{32,48},{48,32},{64,80},{80,64},{96,112},{112,96},{1... | collective-permute-start | bytes 36872 | tf_op jit(solution)/shard_map/ppermute | solution.py:273
  111.2 2.8 %collective-permute-done.10 = f32[24,128]{1,0:T(8,128)S(1)} collective-permute-done((f32[24,128]{1,0:T(8,128)S(1)}, f32[24,128]{1,0:T(8,128)S(1)}, u32[]{:S(2)}, u32[]{:S(2)}) %collective-permute-start.10) | collective-permute-done | bytes 12320 | tf_op jit(solution)/shard_map/ppermute | solution.py:273
  114.1 0.6 fusion
  114.7 10.4 %all-to-all-done.3.packed = f32[32,54,128]{2,1,0:T(8,128)S(1)} async-done(((f32[32,54,128]{2,1,0:T(8,128)}), f32[32,54,128]{2,1,0:T(8,128)S(1)}, u32[]{:S(2)}, u32[]{:S(2)}) %all-to-all-start.3) | async-done | bytes 884768 | tf_op jit(solution)/shard_map/all_to_all | solution.py:277
  125.1 1.2 shard_map.74
  (29 shorter events, 0.1 us)
Async XLA Ops:
  0.6 0.7 copy-start.2
  2.0 28.5 %all-to-all-start = ((f32[16,24,128]{2,1,0:T(8,128)}), f32[16,24,128]{2,1,0:T(8,128)S(1)}, u32[]{:S(2)}, u32[]{:S(2)}) async-start(f32[16,24,128]{2,1,0:T(8,128)} %shard_map.68), calls=%async_computation | async-start | bytes 393216 | tf_op jit(solution)/shard_map/all_to_all | solution.py:234
  19.8 26.4 %collective-permute-start.4 = (f32[6,12,8,128]{3,2,1,0:T(8,128)}, f32[6,12,8,128]{3,2,1,0:T(8,128)S(1)}, u32[]{:S(2)}, u32[]{:S(2)}) collective-permute-start(f32[6,12,8,128]{3,2,1,0:T(8,128)} %get-tuple-element.18), channel_id=1, source_target_pairs={{0,128},{128,256},{256,384},{384,0},{1,129},{129,257},{257,385},{3... | collective-permute-start | bytes 884744 | tf_op jit(solution)/shard_map/ppermute | solution.py:241
  23.0 23.2 %collective-permute-start.5 = (f32[6,12,8,128]{3,2,1,0:T(8,128)}, f32[6,12,8,128]{3,2,1,0:T(8,128)S(1)}, u32[]{:S(2)}, u32[]{:S(2)}) collective-permute-start(f32[6,12,8,128]{3,2,1,0:T(8,128)} %get-tuple-element.19), channel_id=1, source_target_pairs={{0,256},{128,384},{256,0},{384,128},{1,257},{129,385},{257,1},{385... | collective-permute-start | bytes 884744 | tf_op jit(solution)/shard_map/ppermute | solution.py:241
  27.5 18.7 %collective-permute-start.6 = (f32[6,12,8,128]{3,2,1,0:T(8,128)}, f32[6,12,8,128]{3,2,1,0:T(8,128)S(1)}, u32[]{:S(2)}, u32[]{:S(2)}) collective-permute-start(f32[6,12,8,128]{3,2,1,0:T(8,128)} %get-tuple-element.20), channel_id=1, source_target_pairs={{0,384},{128,0},{256,128},{384,256},{1,385},{129,1},{257,129},{385... | collective-permute-start | bytes 884744 | tf_op jit(solution)/shard_map/ppermute | solution.py:241
  31.9 17.6 %all-to-all-start.1 = ((f32[8,80,128]{2,1,0:T(8,128)}), f32[8,80,128]{2,1,0:T(8,128)S(1)}, u32[]{:S(2)}, u32[]{:S(2)}) async-start(f32[8,80,128]{2,1,0:T(8,128)} %get-tuple-element.15), calls=%async_computation.1 | async-start | bytes 655360 | tf_op jit(solution)/shard_map/all_to_all | solution.py:246
  41.7 4.5 %collective-permute-start.2 = (f32[2,24,128]{2,1,0:T(8,128)S(1)}, f32[2,24,128]{2,1,0:T(8,128)S(1)}, u32[]{:S(2)}, u32[]{:S(2)}) collective-permute-start(f32[2,24,128]{2,1,0:T(8,128)S(1)} %get-tuple-element.29), channel_id=1, source_target_pairs={{0,128},{128,256},{256,384},{1,129},{129,257},{257,385},{2,130},{1... | collective-permute-start | bytes 73736 | tf_op jit(solution)/shard_map/ppermute | solution.py:243
  44.9 4.6 %collective-permute-start.3 = (f32[2,24,128]{2,1,0:T(8,128)S(1)}, f32[2,24,128]{2,1,0:T(8,128)S(1)}, u32[]{:S(2)}, u32[]{:S(2)}) collective-permute-start(f32[2,24,128]{2,1,0:T(8,128)S(1)} %get-tuple-element.28), channel_id=1, source_target_pairs={{128,0},{256,128},{384,256},{129,1},{257,129},{385,257},{130,2},{2... | collective-permute-start | bytes 73736 | tf_op jit(solution)/shard_map/ppermute | solution.py:244
  49.5 31.4 %copy-start = (f32[192,192]{1,0:T(8,128)S(1)}, f32[192,192]{1,0:T(8,128)}, u32[]{:S(2)}) copy-start(f32[192,192]{1,0:T(8,128)} %zk.1) | copy-start | bytes 442372
  49.6 31.4 %copy-start.1 = (f32[192,192]{1,0:T(8,128)S(1)}, f32[192,192]{1,0:T(8,128)}, u32[]{:S(2)}) copy-start(f32[192,192]{1,0:T(8,128)} %xk.1) | copy-start | bytes 442372
  51.5 16.2 %copy-start.6 = (f32[2,24,128]{2,1,0:T(8,128)S(1)}, f32[2,24,128]{2,1,0:T(8,128)}, u32[]{:S(2)}) copy-start(f32[2,24,128]{2,1,0:T(8,128)} %get-tuple-element.25) | copy-start | bytes 73732
  51.5 18.5 %copy-start.5 = (f32[2,24,128]{2,1,0:T(8,128)S(1)}, f32[2,24,128]{2,1,0:T(8,128)}, u32[]{:S(2)}) copy-start(f32[2,24,128]{2,1,0:T(8,128)} %get-tuple-element.26) | copy-start | bytes 73732
  51.5 21.7 %copy-start.4 = (f32[2,24,128]{2,1,0:T(8,128)S(1)}, f32[2,24,128]{2,1,0:T(8,128)}, u32[]{:S(2)}) copy-start(f32[2,24,128]{2,1,0:T(8,128)} %get-tuple-element.27) | copy-start | bytes 73732
  51.5 50.2 %all-to-all-start.2 = ((f32[16,72,128]{2,1,0:T(8,128)}), f32[16,72,128]{2,1,0:T(8,128)S(1)}, u32[]{:S(2)}, u32[]{:S(2)}) async-start(f32[16,72,128]{2,1,0:T(8,128)} %get-tuple-element.21), calls=%async_computation.2 | async-start | bytes 1179648 | tf_op jit(solution)/shard_map/all_to_all | solution.py:253
  62.3 19.5 %collective-permute-start = (f32[8,80,128]{2,1,0:T(8,128)S(1)}, f32[8,80,128]{2,1,0:T(8,128)S(1)}, u32[]{:S(2)}, u32[]{:S(2)}) collective-permute-start(f32[8,80,128]{2,1,0:T(8,128)S(1)} %all-to-all-done.1.mixed.mine), channel_id=1, source_target_pairs={{0,1},{1,4},{4,5},{5,8},{8,9},{9,12},{12,13},{13,128},{128,129},{1... | collective-permute-start | bytes 983048 | tf_op jit(solution)/shard_map/ppermute | solution.py:256
  65.8 16.0 %collective-permute-start.1 = (f32[8,80,128]{2,1,0:T(8,128)S(1)}, f32[8,80,128]{2,1,0:T(8,128)S(1)}, u32[]{:S(2)}, u32[]{:S(2)}) collective-permute-start(f32[8,80,128]{2,1,0:T(8,128)S(1)} %all-to-all-done.1.mixed.mine), channel_id=1, source_target_pairs={{1,0},{4,1},{5,4},{8,5},{9,8},{12,9},{13,12},{128,13},{129,128},{1... | collective-permute-start | bytes 983048 | tf_op jit(solution)/shard_map/ppermute | solution.py:257
  67.8 41.4 %collective-permute-start.7 = (f32[2,24,128]{2,1,0:T(8,128)S(1)}, f32[2,24,128]{2,1,0:T(8,128)S(1)}, u32[]{:S(2)}, u32[]{:S(2)}) collective-permute-start(f32[2,24,128]{2,1,0:T(8,128)S(1)} %copy-done.6), channel_id=1, source_target_pairs={{0,32},{16,48},{32,0},{48,16},{64,96},{80,112},{96,64},{112,80},{1... | collective-permute-start | bytes 73736 | tf_op jit(solution)/shard_map/ppermute | solution.py:269
  70.0 39.2 %collective-permute-start.8 = (f32[2,24,128]{2,1,0:T(8,128)S(1)}, f32[2,24,128]{2,1,0:T(8,128)S(1)}, u32[]{:S(2)}, u32[]{:S(2)}) collective-permute-start(f32[2,24,128]{2,1,0:T(8,128)S(1)} %copy-done.5), channel_id=1, source_target_pairs={{0,64},{16,80},{32,96},{48,112},{64,0},{80,16},{96,32},{112,48},{1... | collective-permute-start | bytes 73736 | tf_op jit(solution)/shard_map/ppermute | solution.py:269
  73.2 36.0 %collective-permute-start.9 = (f32[2,24,128]{2,1,0:T(8,128)S(1)}, f32[2,24,128]{2,1,0:T(8,128)S(1)}, u32[]{:S(2)}, u32[]{:S(2)}) collective-permute-start(f32[2,24,128]{2,1,0:T(8,128)S(1)} %copy-done.4), channel_id=1, source_target_pairs={{0,96},{16,112},{32,64},{48,80},{64,32},{80,48},{96,0},{112,16},{1... | collective-permute-start | bytes 73736 | tf_op jit(solution)/shard_map/ppermute | solution.py:269
  104.7 9.4 %copy-start.3 = (f32[12,1,192]{2,1,0:T(1,128)S(1)}, f32[12,1,192]{2,1,0:T(1,128)}, u32[]{:S(2)}) copy-start(f32[12,1,192]{2,1,0:T(1,128)} %row.1) | copy-start | bytes 27652
  104.7 20.4 %all-to-all-start.3 = ((f32[32,54,128]{2,1,0:T(8,128)}), f32[32,54,128]{2,1,0:T(8,128)S(1)}, u32[]{:S(2)}, u32[]{:S(2)}) async-start(f32[32,54,128]{2,1,0:T(8,128)} %shard_map.73), calls=%async_computation.3 | async-start | bytes 1835008 | tf_op jit(solution)/shard_map/all_to_all | solution.py:277
  109.3 4.7 %collective-permute-start.10 = (f32[24,128]{1,0:T(8,128)S(1)}, f32[24,128]{1,0:T(8,128)S(1)}, u32[]{:S(2)}, u32[]{:S(2)}) collective-permute-start(f32[24,128]{1,0:T(8,128)S(1)} %dynamic-slice_bitcast_fusion), channel_id=1, source_target_pairs={{0,16},{16,0},{32,48},{48,32},{64,80},{80,64},{96,112},{112,96},{1... | collective-permute-start | bytes 36872 | tf_op jit(solution)/shard_map/ppermute | solution.py:273

commit v9 on v8

--- a/solution.py
+++ b/solution.py
@@ -155,10 +155,7 @@
         part[...] = total[pl.ds(2 * lax.bitwise_xor(zl // 2, t), 2)]
 
 
-def main_kernel(place, prev, mine, succ, got, zw, xw, *rest):
-    out, grid, force = rest
-    y = place[0]
-
+def slopes_kernel(prev, mine, succ, out, grid):
     for r, ref in enumerate((prev, mine, succ)):
         grid[r, :8] = jnp.zeros((8, WIDE), F32)
         grid[r, 200:] = jnp.zeros((8, WIDE), F32)
@@ -175,13 +172,21 @@
         (grid[2, 8:200] - grid[0, 8:200]) * 0.5,
         (pltpu.roll(here, WIDE - 1, 1) - pltpu.roll(here, 1, 1)) * 0.5,
     )
-    slopes = [(a[:, :LANES], jnp.where(low_lane, a[:, LANES:], pltpu.roll(a[:, LANES:], 64, 1))) for a in slopes]
+    for c, a in enumerate(slopes):
+        high = a[:, LANES:]
+        out[c, :, :LANES] = a[:, :LANES]
+        out[c, :, LANES:] = jnp.where(low_lane, high, pltpu.roll(high, 64, 1))
+
+
+def main_kernel(place, slopes, got, zw, xw, out, force):
+    y = place[0]
     for k in range(8):
         at = slice(24 * k, 24 * k + 24)
         for b in range(6):
             r = jnp.concatenate([got[2 * k, 12 * b : 12 * b + 12], got[2 * k + 1, 12 * b : 12 * b + 12]], 0)
             for c in range(3):
-                force[at, (c * 6 + b) * LANES : (c * 6 + b + 1) * LANES] = r * slopes[c][b // 4][at]
+                half = slice(0, LANES) if b < 4 else slice(LANES, WIDE)
+                force[at, (c * 6 + b) * LANES : (c * 6 + b + 1) * LANES] = r * slopes[c, at, half]
 
     def times(a1, a0, b1, b0):
         dot = lambda p, q: jnp.dot(p, q, preferred_element_type=F32)
@@ -260,11 +265,14 @@
         (pltpu.VMEM((2, 96, 192), BF16), pltpu.VMEM((2, 2, 256, 192), BF16)),
     )(place, z_kernel, x_kernel)
 
-    packed, = call(
-        main_kernel,
-        (shape(32, 54, LANES),),
-        (pltpu.VMEM((3, 208, WIDE), F32), pltpu.VMEM((192, 18 * LANES), F32)),
-    )(place, prev, mixed, succ, got, zw, xw)
+    (slopes,) = call(slopes_kernel, (held(3, 192, WIDE),), (pltpu.VMEM((3, 208, WIDE), F32),))(
+        None, prev, mixed, succ
+    )
+    slopes, *parts[1:] = lax.optimization_barrier((slopes, *parts[1:]))
+    (packed,) = call(main_kernel, (shape(32, 54, LANES),), (pltpu.VMEM((192, 18 * LANES), F32),))(
+        place, slopes, got, zw, xw
+    )
+
     for t in (1, 2, 3):
         parts[t] = lax.ppermute(parts[t], "zl", [(i, i ^ (2 * t)) for i in range(8)])
     two, odd = sum(parts), lax.axis_index("zl") & 1

time: 127 us -> 127 us (level)
    all_to_all x1, waiting for transfers between devices: 19.9 us -> 13.2 us  [per_device(): got = lax.all_to_all(by_row, ('x', 'zh', 'c'), 0, 0, tiled=True)]
    ppermute x1, waiting for transfers between devices: 0.01 us -> 4.4 us  [per_device(): succ = lax.ppermute(mixed, ROW, [(j, i) for i, j in along])]
    ppermute x1, waiting for transfers between devices: 0.01 us -> 2.07 us  [per_device(): prev = lax.ppermute(mixed, ROW, along)]
    pallas_call x7 -> x8, Pallas kernels: 11.6 us -> 11.6 us  [run(): pl.pallas_call(kernel, out_shape=outs, in_specs=[*[smem()] * len(first),...]
  transfers between devices with their start and end apart: 15 -> 15, of which waited for: 4 -> 6; matrix products, arithmetic and copies ran while one was open for 1% -> 1% of each run, Pallas kernels for 6% -> 6%
where the time goes in v9:
time: 127 us; the launch traced here: 126 us
  starting transfers between devices  75.4 us (59%)
  waiting for transfers between devices  36.1 us (28%)
  Pallas kernels  11.6 us (9%)
  local copies, waits for them, and re-layouts  1.34 us (1%)
    all_to_all x1, starting transfers between devices, per_device(): lax.all_to_all(piece, COL, 0, 0, tiled=True).reshape(8, 2, 24, LANES)  14.7 us
    ppermute x3, starting transfers between devices, per_device(): parts[t] = lax.ppermute(parts[t], 'zl', [(i, i ^ 2 * t) for i in range(8)])  13.2 us
    all_to_all x1, waiting for transfers between devices, per_device(): got = lax.all_to_all(by_row, ('x', 'zh', 'c'), 0, 0, tiled=True)  13.2 us
    pallas_call x8, Pallas kernels, run(): pl.pallas_call(kernel, out_shape=outs, in_specs=[*[smem()] * len(first),...  11.6 us
    all_to_all x1, starting transfers between devices, per_device(): got = lax.all_to_all(by_row, ('x', 'zh', 'c'), 0, 0, tiled=True)  10.8 us
    ppermute x3, starting transfers between devices, per_device(): raws[s] = lax.ppermute(raws[s], 'y', [(i, (i + s) % 4) for i in range(4)])  10.7 us
    all_to_all x1, waiting for transfers between devices, per_device(): back = lax.all_to_all(packed, ROW, 0, 0, tiled=True)  10.4 us
    all_to_all x1, starting transfers between devices, per_device(): mixed = lax.all_to_all(mixed, ('x', 'c'), 0, 0, tiled=True)  9.74 us
  transfers between devices with their start and end apart: 15, of which 6 were waited for; matrix products, arithmetic and copies ran while one was open for 1% of the time, Pallas kernels for 6%

profile of v9, /device:TPU:33, one launch (start us, length us, event | category | flops | bytes accessed | tf_op | source)
XLA Modules:
  0.0 126.1 jit_solution(3166856161220225039)
XLA Ops:
  0.6 0.7 copy-done.2
  1.3 0.7 shard_map.68
  2.0 14.7 %all-to-all-start = ((f32[16,24,128]{2,1,0:T(8,128)}), f32[16,24,128]{2,1,0:T(8,128)S(1)}, u32[]{:S(2)}, u32[]{:S(2)}) async-start(f32[16,24,128]{2,1,0:T(8,128)} %shard_map.68), calls=%async_computation | async-start | bytes 393216 | tf_op jit(solution)/shard_map/all_to_all | solution.py:239
  16.7 0.6 stack.23.place
  17.3 2.5 %shard_map.71 = (f32[6,12,8,128]{3,2,1,0:T(8,128)S(1)}, f32[6,12,8,128]{3,2,1,0:T(8,128)}, f32[6,12,8,128]{3,2,1,0:T(8,128)}, f32[6,12,8,128]{3,2,1,0:T(8,128)}) custom-call(s32[5]{0:T(128)} %stack.23.place, f32[12,32,192]{2,1,0:T(8,128)} %bitcast.18, f32[3,12,32,192]{3,2,1,0:T(8,128)} %bitcast.16), custom_call_target="tpu_custom_call" | custom-call | tf_op jit(solution)/shard_map/pallas_call | solution.py:36
  19.8 3.2 %collective-permute-start.4 = (f32[6,12,8,128]{3,2,1,0:T(8,128)}, f32[6,12,8,128]{3,2,1,0:T(8,128)S(1)}, u32[]{:S(2)}, u32[]{:S(2)}) collective-permute-start(f32[6,12,8,128]{3,2,1,0:T(8,128)} %get-tuple-element.22), channel_id=1, source_target_pairs={{0,128},{128,256},{256,384},{384,0},{1,129},{129,257},{257,385},{3... | collective-permute-start | bytes 884744 | tf_op jit(solution)/shard_map/ppermute | solution.py:246
  23.0 4.5 %collective-permute-start.5 = (f32[6,12,8,128]{3,2,1,0:T(8,128)}, f32[6,12,8,128]{3,2,1,0:T(8,128)S(1)}, u32[]{:S(2)}, u32[]{:S(2)}) collective-permute-start(f32[6,12,8,128]{3,2,1,0:T(8,128)} %get-tuple-element.23), channel_id=1, source_target_pairs={{0,256},{128,384},{256,0},{384,128},{1,257},{129,385},{257,1},{385... | collective-permute-start | bytes 884744 | tf_op jit(solution)/shard_map/ppermute | solution.py:246
  27.5 3.0 %collective-permute-start.6 = (f32[6,12,8,128]{3,2,1,0:T(8,128)}, f32[6,12,8,128]{3,2,1,0:T(8,128)S(1)}, u32[]{:S(2)}, u32[]{:S(2)}) collective-permute-start(f32[6,12,8,128]{3,2,1,0:T(8,128)} %get-tuple-element.24), channel_id=1, source_target_pairs={{0,384},{128,0},{256,128},{384,256},{1,385},{129,1},{257,129},{385... | collective-permute-start | bytes 884744 | tf_op jit(solution)/shard_map/ppermute | solution.py:246
  30.5 1.4 %shard_map.69 = (f32[2,24,8,128]{3,2,1,0:T(8,128)S(1)}, f32[8,80,128]{2,1,0:T(8,128)}) custom-call(s32[5]{0:T(128)} %stack.23.place, f32[8,2,24,128]{3,2,1,0:T(8,128)S(1)} %bitcast.15), custom_call_target="tpu_custom_call" | custom-call | tf_op jit(solution)/shard_map/pallas_call | solution.py:36
  31.9 9.7 %all-to-all-start.1 = ((f32[8,80,128]{2,1,0:T(8,128)}), f32[8,80,128]{2,1,0:T(8,128)S(1)}, u32[]{:S(2)}, u32[]{:S(2)}) async-start(f32[8,80,128]{2,1,0:T(8,128)} %get-tuple-element.19), calls=%async_computation.1 | async-start | bytes 655360 | tf_op jit(solution)/shard_map/all_to_all | solution.py:251
  41.7 3.2 %collective-permute-start.2 = (f32[2,24,128]{2,1,0:T(8,128)S(1)}, f32[2,24,128]{2,1,0:T(8,128)S(1)}, u32[]{:S(2)}, u32[]{:S(2)}) collective-permute-start(f32[2,24,128]{2,1,0:T(8,128)S(1)} %get-tuple-element.37), channel_id=1, source_target_pairs={{0,128},{128,256},{256,384},{1,129},{129,257},{257,385},{2,130},{1... | collective-permute-start | bytes 73736 | tf_op jit(solution)/shard_map/ppermute | solution.py:248
  44.9 1.3 %collective-permute-start.3 = (f32[2,24,128]{2,1,0:T(8,128)S(1)}, f32[2,24,128]{2,1,0:T(8,128)S(1)}, u32[]{:S(2)}, u32[]{:S(2)}) collective-permute-start(f32[2,24,128]{2,1,0:T(8,128)S(1)} %get-tuple-element.36), channel_id=1, source_target_pairs={{128,0},{256,128},{384,256},{129,1},{257,129},{385,257},{130,2},{2... | collective-permute-start | bytes 73736 | tf_op jit(solution)/shard_map/ppermute | solution.py:249
  46.2 3.3 %collective-permute-done.3.next_row = f32[2,24,128]{2,1,0:T(8,128)S(1)} collective-permute-done((f32[2,24,128]{2,1,0:T(8,128)S(1)}, f32[2,24,128]{2,1,0:T(8,128)S(1)}, u32[]{:S(2)}, u32[]{:S(2)}) %collective-permute-start.3) | collective-permute-done | bytes 24608 | tf_op jit(solution)/shard_map/ppermute | solution.py:249
  49.5 1.8 %shard_map.72 = (f32[16,72,128]{2,1,0:T(8,128)}, f32[2,24,128]{2,1,0:T(8,128)S(1)}, f32[2,24,128]{2,1,0:T(8,128)}, f32[2,24,128]{2,1,0:T(8,128)}, f32[2,24,128]{2,1,0:T(8,128)}) custom-call(s32[5]{0:T(128)} %stack.23.place, f32[2,24,8,128]{3,2,1,0:T(8,128)S(1)} %get-tuple-element.20.tmpl, f32[2,24,128]{2,1,0:T(8,128)S(1)} %collective-permute-done.2.prev_row, ...), custom_call_target="tpu_custom_call" | custom-call | tf_op jit(solution)/shard_map/pallas_call | solution.py:36
  51.4 10.8 %all-to-all-start.2 = ((f32[16,72,128]{2,1,0:T(8,128)}), f32[16,72,128]{2,1,0:T(8,128)S(1)}, u32[]{:S(2)}, u32[]{:S(2)}) async-start(f32[16,72,128]{2,1,0:T(8,128)} %get-tuple-element.29), calls=%async_computation.2 | async-start | bytes 1179648 | tf_op jit(solution)/shard_map/all_to_all | solution.py:258
  62.2 3.5 %collective-permute-start = (f32[8,80,128]{2,1,0:T(8,128)S(1)}, f32[8,80,128]{2,1,0:T(8,128)S(1)}, u32[]{:S(2)}, u32[]{:S(2)}) collective-permute-start(f32[8,80,128]{2,1,0:T(8,128)S(1)} %all-to-all-done.1.mine.mixed), channel_id=1, source_target_pairs={{0,1},{1,4},{4,5},{5,8},{8,9},{9,12},{12,13},{13,128},{128,129},{1... | collective-permute-start | bytes 983048 | tf_op jit(solution)/shard_map/ppermute | solution.py:261
  65.7 1.9 %collective-permute-start.1 = (f32[8,80,128]{2,1,0:T(8,128)S(1)}, f32[8,80,128]{2,1,0:T(8,128)S(1)}, u32[]{:S(2)}, u32[]{:S(2)}) collective-permute-start(f32[8,80,128]{2,1,0:T(8,128)S(1)} %all-to-all-done.1.mine.mixed), channel_id=1, source_target_pairs={{1,0},{4,1},{5,4},{8,5},{9,8},{12,9},{13,12},{128,13},{129,128},{1... | collective-permute-start | bytes 983048 | tf_op jit(solution)/shard_map/ppermute | solution.py:262
  67.6 2.1 %collective-permute-done.prev = f32[8,80,128]{2,1,0:T(8,128)S(1)} collective-permute-done((f32[8,80,128]{2,1,0:T(8,128)S(1)}, f32[8,80,128]{2,1,0:T(8,128)S(1)}, u32[]{:S(2)}, u32[]{:S(2)}) %collective-permute-start) | collective-permute-done | bytes 327712 | tf_op jit(solution)/shard_map/ppermute | solution.py:261
  69.7 4.4 %collective-permute-done.1.succ = f32[8,80,128]{2,1,0:T(8,128)S(1)} collective-permute-done((f32[8,80,128]{2,1,0:T(8,128)S(1)}, f32[8,80,128]{2,1,0:T(8,128)S(1)}, u32[]{:S(2)}, u32[]{:S(2)}) %collective-permute-start.1) | collective-permute-done | bytes 327712 | tf_op jit(solution)/shard_map/ppermute | solution.py:262
  74.1 0.2 shard_map.70.slopes
  74.4 2.5 %collective-permute-start.7 = (f32[2,24,128]{2,1,0:T(8,128)S(1)}, f32[2,24,128]{2,1,0:T(8,128)S(1)}, u32[]{:S(2)}, u32[]{:S(2)}) collective-permute-start(f32[2,24,128]{2,1,0:T(8,128)S(1)} %copy-done.6), channel_id=1, source_target_pairs={{0,32},{16,48},{32,0},{48,16},{64,96},{80,112},{96,64},{112,80},{1... | collective-permute-start | bytes 73736 | tf_op jit(solution)/shard_map/ppermute | solution.py:277
  76.9 3.3 %collective-permute-start.8 = (f32[2,24,128]{2,1,0:T(8,128)S(1)}, f32[2,24,128]{2,1,0:T(8,128)S(1)}, u32[]{:S(2)}, u32[]{:S(2)}) collective-permute-start(f32[2,24,128]{2,1,0:T(8,128)S(1)} %copy-done.5), channel_id=1, source_target_pairs={{0,64},{16,80},{32,96},{48,112},{64,0},{80,16},{96,32},{112,48},{1... | collective-permute-start | bytes 73736 | tf_op jit(solution)/shard_map/ppermute | solution.py:277
  80.1 7.4 %collective-permute-start.9 = (f32[2,24,128]{2,1,0:T(8,128)S(1)}, f32[2,24,128]{2,1,0:T(8,128)S(1)}, u32[]{:S(2)}, u32[]{:S(2)}) collective-permute-start(f32[2,24,128]{2,1,0:T(8,128)S(1)} %copy-done.4), channel_id=1, source_target_pairs={{0,96},{16,112},{32,64},{48,80},{64,32},{80,48},{96,0},{112,16},{1... | collective-permute-start | bytes 73736 | tf_op jit(solution)/shard_map/ppermute | solution.py:277
  87.6 0.8 shard_map.73
  88.4 13.2 %all-to-all-done.2.got = f32[16,72,128]{2,1,0:T(8,128)S(1)} async-done(((f32[16,72,128]{2,1,0:T(8,128)}), f32[16,72,128]{2,1,0:T(8,128)S(1)}, u32[]{:S(2)}, u32[]{:S(2)}) %all-to-all-start.2) | async-done | bytes 589856 | tf_op jit(solution)/shard_map/all_to_all | solution.py:258
  101.6 2.9 %shard_map.74 = f32[32,54,128]{2,1,0:T(8,128)} custom-call(s32[5]{0:T(128)} %stack.23.place, f32[3,192,256]{2,1,0:T(8,128)S(1)} %shard_map.70.slopes, f32[16,72,128]{2,1,0:T(8,128)S(1)} %all-to-all-done.2.got, bf16[2,96,192]{2,1,0:T(8,128)(2,1)S(1)} %get-tuple-element.30.zw, bf16[2,2,256,192]{3,2,1,0:T(8,128)(2,1)S(1)} %get-tuple-element.31.xw), custom_call_target="tpu_custom_call" | custom-call | tf_op jit(solution)/shard_map/pallas_call | solution.py:36
  104.5 4.5 %all-to-all-start.3 = ((f32[32,54,128]{2,1,0:T(8,128)}), f32[32,54,128]{2,1,0:T(8,128)S(1)}, u32[]{:S(2)}, u32[]{:S(2)}) async-start(f32[32,54,128]{2,1,0:T(8,128)} %shard_map.74), calls=%async_computation.3 | async-start | bytes 1835008 | tf_op jit(solution)/shard_map/all_to_all | solution.py:285
  109.1 1.9 %collective-permute-start.10 = (f32[24,128]{1,0:T(8,128)S(1)}, f32[24,128]{1,0:T(8,128)S(1)}, u32[]{:S(2)}, u32[]{:S(2)}) collective-permute-start(f32[24,128]{1,0:T(8,128)S(1)} %dynamic-slice_bitcast_fusion), channel_id=1, source_target_pairs={{0,16},{16,0},{32,48},{48,32},{64,80},{80,64},{96,112},{112,96},{1... | collective-permute-start | bytes 36872 | tf_op jit(solution)/shard_map/ppermute | solution.py:281
  111.0 2.8 %collective-permute-done.10 = f32[24,128]{1,0:T(8,128)S(1)} collective-permute-done((f32[24,128]{1,0:T(8,128)S(1)}, f32[24,128]{1,0:T(8,128)S(1)}, u32[]{:S(2)}, u32[]{:S(2)}) %collective-permute-start.10) | collective-permute-done | bytes 12320 | tf_op jit(solution)/shard_map/ppermute | solution.py:281
  113.9 0.6 fusion
  114.5 10.4 %all-to-all-done.3.packed = f32[32,54,128]{2,1,0:T(8,128)S(1)} async-done(((f32[32,54,128]{2,1,0:T(8,128)}), f32[32,54,128]{2,1,0:T(8,128)S(1)}, u32[]{:S(2)}, u32[]{:S(2)}) %all-to-all-start.3) | async-done | bytes 884768 | tf_op jit(solution)/shard_map/all_to_all | solution.py:285
  124.9 1.2 shard_map.75
  (30 shorter events, 0.1 us)
Async XLA Ops:
  0.6 0.7 copy-start.2
  2.0 28.5 %all-to-all-start = ((f32[16,24,128]{2,1,0:T(8,128)}), f32[16,24,128]{2,1,0:T(8,128)S(1)}, u32[]{:S(2)}, u32[]{:S(2)}) async-start(f32[16,24,128]{2,1,0:T(8,128)} %shard_map.68), calls=%async_computation | async-start | bytes 393216 | tf_op jit(solution)/shard_map/all_to_all | solution.py:239
  19.8 26.4 %collective-permute-start.4 = (f32[6,12,8,128]{3,2,1,0:T(8,128)}, f32[6,12,8,128]{3,2,1,0:T(8,128)S(1)}, u32[]{:S(2)}, u32[]{:S(2)}) collective-permute-start(f32[6,12,8,128]{3,2,1,0:T(8,128)} %get-tuple-element.22), channel_id=1, source_target_pairs={{0,128},{128,256},{256,384},{384,0},{1,129},{129,257},{257,385},{3... | collective-permute-start | bytes 884744 | tf_op jit(solution)/shard_map/ppermute | solution.py:246
  23.0 23.2 %collective-permute-start.5 = (f32[6,12,8,128]{3,2,1,0:T(8,128)}, f32[6,12,8,128]{3,2,1,0:T(8,128)S(1)}, u32[]{:S(2)}, u32[]{:S(2)}) collective-permute-start(f32[6,12,8,128]{3,2,1,0:T(8,128)} %get-tuple-element.23), channel_id=1, source_target_pairs={{0,256},{128,384},{256,0},{384,128},{1,257},{129,385},{257,1},{385... | collective-permute-start | bytes 884744 | tf_op jit(solution)/shard_map/ppermute | solution.py:246
  27.5 18.7 %collective-permute-start.6 = (f32[6,12,8,128]{3,2,1,0:T(8,128)}, f32[6,12,8,128]{3,2,1,0:T(8,128)S(1)}, u32[]{:S(2)}, u32[]{:S(2)}) collective-permute-start(f32[6,12,8,128]{3,2,1,0:T(8,128)} %get-tuple-element.24), channel_id=1, source_target_pairs={{0,384},{128,0},{256,128},{384,256},{1,385},{129,1},{257,129},{385... | collective-permute-start | bytes 884744 | tf_op jit(solution)/shard_map/ppermute | solution.py:246
  31.9 17.6 %all-to-all-start.1 = ((f32[8,80,128]{2,1,0:T(8,128)}), f32[8,80,128]{2,1,0:T(8,128)S(1)}, u32[]{:S(2)}, u32[]{:S(2)}) async-start(f32[8,80,128]{2,1,0:T(8,128)} %get-tuple-element.19), calls=%async_computation.1 | async-start | bytes 655360 | tf_op jit(solution)/shard_map/all_to_all | solution.py:251
  41.7 4.5 %collective-permute-start.2 = (f32[2,24,128]{2,1,0:T(8,128)S(1)}, f32[2,24,128]{2,1,0:T(8,128)S(1)}, u32[]{:S(2)}, u32[]{:S(2)}) collective-permute-start(f32[2,24,128]{2,1,0:T(8,128)S(1)} %get-tuple-element.37), channel_id=1, source_target_pairs={{0,128},{128,256},{256,384},{1,129},{129,257},{257,385},{2,130},{1... | collective-permute-start | bytes 73736 | tf_op jit(solution)/shard_map/ppermute | solution.py:248
  44.9 4.6 %collective-permute-start.3 = (f32[2,24,128]{2,1,0:T(8,128)S(1)}, f32[2,24,128]{2,1,0:T(8,128)S(1)}, u32[]{:S(2)}, u32[]{:S(2)}) collective-permute-start(f32[2,24,128]{2,1,0:T(8,128)S(1)} %get-tuple-element.36), channel_id=1, source_target_pairs={{128,0},{256,128},{384,256},{129,1},{257,129},{385,257},{130,2},{2... | collective-permute-start | bytes 73736 | tf_op jit(solution)/shard_map/ppermute | solution.py:249
  51.4 23.0 %copy-start.6 = (f32[2,24,128]{2,1,0:T(8,128)S(1)}, f32[2,24,128]{2,1,0:T(8,128)}, u32[]{:S(2)}) copy-start(f32[2,24,128]{2,1,0:T(8,128)} %get-tuple-element.33) | copy-start | bytes 73732
  51.4 25.5 %copy-start.5 = (f32[2,24,128]{2,1,0:T(8,128)S(1)}, f32[2,24,128]{2,1,0:T(8,128)}, u32[]{:S(2)}) copy-start(f32[2,24,128]{2,1,0:T(8,128)} %get-tuple-element.34) | copy-start | bytes 73732
  51.4 28.8 %copy-start.4 = (f32[2,24,128]{2,1,0:T(8,128)S(1)}, f32[2,24,128]{2,1,0:T(8,128)}, u32[]{:S(2)}) copy-start(f32[2,24,128]{2,1,0:T(8,128)} %get-tuple-element.35) | copy-start | bytes 73732
  51.4 36.2 %copy-start = (f32[192,192]{1,0:T(8,128)S(1)}, f32[192,192]{1,0:T(8,128)}, u32[]{:S(2)}) copy-start(f32[192,192]{1,0:T(8,128)} %zk.1) | copy-start | bytes 442372
  51.4 36.2 %copy-start.1 = (f32[192,192]{1,0:T(8,128)S(1)}, f32[192,192]{1,0:T(8,128)}, u32[]{:S(2)}) copy-start(f32[192,192]{1,0:T(8,128)} %xk.1) | copy-start | bytes 442372
  51.4 50.2 %all-to-all-start.2 = ((f32[16,72,128]{2,1,0:T(8,128)}), f32[16,72,128]{2,1,0:T(8,128)S(1)}, u32[]{:S(2)}, u32[]{:S(2)}) async-start(f32[16,72,128]{2,1,0:T(8,128)} %get-tuple-element.29), calls=%async_computation.2 | async-start | bytes 1179648 | tf_op jit(solution)/shard_map/all_to_all | solution.py:258
  62.2 7.5 %collective-permute-start = (f32[8,80,128]{2,1,0:T(8,128)S(1)}, f32[8,80,128]{2,1,0:T(8,128)S(1)}, u32[]{:S(2)}, u32[]{:S(2)}) collective-permute-start(f32[8,80,128]{2,1,0:T(8,128)S(1)} %all-to-all-done.1.mine.mixed), channel_id=1, source_target_pairs={{0,1},{1,4},{4,5},{5,8},{8,9},{9,12},{12,13},{13,128},{128,129},{1... | collective-permute-start | bytes 983048 | tf_op jit(solution)/shard_map/ppermute | solution.py:261
  65.7 8.4 %collective-permute-start.1 = (f32[8,80,128]{2,1,0:T(8,128)S(1)}, f32[8,80,128]{2,1,0:T(8,128)S(1)}, u32[]{:S(2)}, u32[]{:S(2)}) collective-permute-start(f32[8,80,128]{2,1,0:T(8,128)S(1)} %all-to-all-done.1.mine.mixed), channel_id=1, source_target_pairs={{1,0},{4,1},{5,4},{8,5},{9,8},{12,9},{13,12},{128,13},{129,128},{1... | collective-permute-start | bytes 983048 | tf_op jit(solution)/shard_map/ppermute | solution.py:262
  74.4 34.7 %collective-permute-start.7 = (f32[2,24,128]{2,1,0:T(8,128)S(1)}, f32[2,24,128]{2,1,0:T(8,128)S(1)}, u32[]{:S(2)}, u32[]{:S(2)}) collective-permute-start(f32[2,24,128]{2,1,0:T(8,128)S(1)} %copy-done.6), channel_id=1, source_target_pairs={{0,32},{16,48},{32,0},{48,16},{64,96},{80,112},{96,64},{112,80},{1... | collective-permute-start | bytes 73736 | tf_op jit(solution)/shard_map/ppermute | solution.py:277
  76.9 32.2 %collective-permute-start.8 = (f32[2,24,128]{2,1,0:T(8,128)S(1)}, f32[2,24,128]{2,1,0:T(8,128)S(1)}, u32[]{:S(2)}, u32[]{:S(2)}) collective-permute-start(f32[2,24,128]{2,1,0:T(8,128)S(1)} %copy-done.5), channel_id=1, source_target_pairs={{0,64},{16,80},{32,96},{48,112},{64,0},{80,16},{96,32},{112,48},{1... | collective-permute-start | bytes 73736 | tf_op jit(solution)/shard_map/ppermute | solution.py:277
  80.1 28.9 %collective-permute-start.9 = (f32[2,24,128]{2,1,0:T(8,128)S(1)}, f32[2,24,128]{2,1,0:T(8,128)S(1)}, u32[]{:S(2)}, u32[]{:S(2)}) collective-permute-start(f32[2,24,128]{2,1,0:T(8,128)S(1)} %copy-done.4), channel_id=1, source_target_pairs={{0,96},{16,112},{32,64},{48,80},{64,32},{80,48},{96,0},{112,16},{1... | collective-permute-start | bytes 73736 | tf_op jit(solution)/shard_map/ppermute | solution.py:277
  104.5 9.4 %copy-start.3 = (f32[12,1,192]{2,1,0:T(1,128)S(1)}, f32[12,1,192]{2,1,0:T(1,128)}, u32[]{:S(2)}) copy-start(f32[12,1,192]{2,1,0:T(1,128)} %row.1) | copy-start | bytes 27652
  104.5 20.4 %all-to-all-start.3 = ((f32[32,54,128]{2,1,0:T(8,128)}), f32[32,54,128]{2,1,0:T(8,128)S(1)}, u32[]{:S(2)}, u32[]{:S(2)}) async-start(f32[32,54,128]{2,1,0:T(8,128)} %shard_map.74), calls=%async_computation.3 | async-start | bytes 1835008 | tf_op jit(solution)/shard_map/all_to_all | solution.py:285
  109.1 4.7 %collective-permute-start.10 = (f32[24,128]{1,0:T(8,128)S(1)}, f32[24,128]{1,0:T(8,128)S(1)}, u32[]{:S(2)}, u32[]{:S(2)}) collective-permute-start(f32[24,128]{1,0:T(8,128)S(1)} %dynamic-slice_bitcast_fusion), channel_id=1, source_target_pairs={{0,16},{16,0},{32,48},{48,32},{64,80},{80,64},{96,112},{112,96},{1... | collective-permute-start | bytes 36872 | tf_op jit(solution)/shard_map/ppermute | solution.py:281

commit v10 on v9

--- a/solution.py
+++ b/solution.py
@@ -79,18 +79,30 @@
             out[4 + k] = jnp.concatenate([first[:, rows, LANES:], second[:, rows, LANES:]], -1)
 
 
-def spread_kernel(place, gathered, tmpl, out):
-    zh, c = place[1], place[2]
+def rows_kernel(gathered, tmpl):
     for h in range(2):
         for k in range(3):
             tmpl[h, 8 * k : 8 * k + 8] = jnp.swapaxes(gathered[:, h, 8 * k : 8 * k + 8], 0, 1)
-    near, far = 11 * (1 - c), 11 * c
-    ends = [tmpl[zh, near], tmpl[zh, 12 + near], tmpl[1 - zh, far], tmpl[1 - zh, 12 + far]]
+
+
+def spread_kernel(place, gathered, out):
+    zh, c = place[1], place[2]
+
+    def plane(h, p):
+        return jnp.concatenate([gathered[i, h, p : p + 1] for i in range(8)], 0)
+
+    def end(last, h, high):
+        at = 12 * high
+        first_half = jnp.where(last == 1, plane(0, at + 11), plane(0, at))
+        second_half = jnp.where(last == 1, plane(1, at + 11), plane(1, at))
+        return jnp.where(h == 0, first_half, second_half)
+
+    ends = [end(1 - c, zh, 0), end(1 - c, zh, 1), end(c, 1 - zh, 0), end(c, 1 - zh, 1)]
     for i in range(8):
         out[i, :24] = gathered[i, 0]
         out[i, 24:48] = gathered[i, 1]
-        for k, end in enumerate(ends):
-            out[i, 48 + 8 * k : 56 + 8 * k] = end
+        for k, e in enumerate(ends):
+            out[i, 48 + 8 * k : 56 + 8 * k] = e
 
 
 def residual_kernel(place, tmpl, prev_row, next_row, mixed, *rest):
@@ -247,7 +259,8 @@
 
     prev_row = lax.ppermute(gathered[7], "y", [(i, i + 1) for i in range(3)])
     next_row = lax.ppermute(gathered[0], "y", [(i + 1, i) for i in range(3)])
-    tmpl, mixed = call(spread_kernel, (held(2, 24, 8, LANES), shape(8, 80, LANES)))(place, gathered)
+    (mixed,) = call(spread_kernel, (shape(8, 80, LANES),))(place, gathered)
+    (tmpl,) = call(rows_kernel, (held(2, 24, 8, LANES),))(None, gathered)
     mixed = lax.all_to_all(mixed, ("x", "c"), 0, 0, tiled=True)
 
     by_row, *parts = call(

time: 127 us -> 127 us (level)
    pallas_call x8 -> x9, Pallas kernels: 11.6 us -> 11.7 us  [run(): pl.pallas_call(kernel, out_shape=outs, in_specs=[*[smem()] * len(first),...]
where the time goes in v10:
time: 127 us; the launch traced here: 126 us
  starting transfers between devices  75.4 us (59%)
  waiting for transfers between devices  36.1 us (28%)
  Pallas kernels  11.7 us (9%)
  local copies, waits for them, and re-layouts  1.44 us (1%)
    all_to_all x1, starting transfers between devices, per_device(): lax.all_to_all(piece, COL, 0, 0, tiled=True).reshape(8, 2, 24, LANES)  14.7 us
    ppermute x3, starting transfers between devices, per_device(): parts[t] = lax.ppermute(parts[t], 'zl', [(i, i ^ 2 * t) for i in range(8)])  13.2 us
    all_to_all x1, waiting for transfers between devices, per_device(): got = lax.all_to_all(by_row, ('x', 'zh', 'c'), 0, 0, tiled=True)  13.2 us
    pallas_call x9, Pallas kernels, run(): pl.pallas_call(kernel, out_shape=outs, in_specs=[*[smem()] * len(first),...  11.7 us
    all_to_all x1, starting transfers between devices, per_device(): got = lax.all_to_all(by_row, ('x', 'zh', 'c'), 0, 0, tiled=True)  10.9 us
    ppermute x3, starting transfers between devices, per_device(): raws[s] = lax.ppermute(raws[s], 'y', [(i, (i + s) % 4) for i in range(4)])  10.7 us
    all_to_all x1, waiting for transfers between devices, per_device(): back = lax.all_to_all(packed, ROW, 0, 0, tiled=True)  10.4 us
    all_to_all x1, starting transfers between devices, per_device(): mixed = lax.all_to_all(mixed, ('x', 'c'), 0, 0, tiled=True)  9.66 us
  transfers between devices with their start and end apart: 15, of which 6 were waited for; matrix products, arithmetic and copies ran while one was open for 1% of the time, Pallas kernels for 6%

profile of v10, /device:TPU:33, one launch (start us, length us, event | category | flops | bytes accessed | tf_op | source)
XLA Modules:
  0.0 126.1 jit_solution(13612192923698169408)
XLA Ops:
  0.6 0.7 copy-done.2
  1.3 0.7 shard_map.68
  2.0 14.7 %all-to-all-start = ((f32[16,24,128]{2,1,0:T(8,128)}), f32[16,24,128]{2,1,0:T(8,128)S(1)}, u32[]{:S(2)}, u32[]{:S(2)}) async-start(f32[16,24,128]{2,1,0:T(8,128)} %shard_map.68), calls=%async_computation | async-start | bytes 393216 | tf_op jit(solution)/shard_map/all_to_all | solution.py:251
  16.7 0.7 stack.23.place
  17.4 2.5 %shard_map.72 = (f32[6,12,8,128]{3,2,1,0:T(8,128)S(1)}, f32[6,12,8,128]{3,2,1,0:T(8,128)}, f32[6,12,8,128]{3,2,1,0:T(8,128)}, f32[6,12,8,128]{3,2,1,0:T(8,128)}) custom-call(s32[5]{0:T(128)} %stack.23.place, f32[12,32,192]{2,1,0:T(8,128)} %bitcast.19, f32[3,12,32,192]{3,2,1,0:T(8,128)} %bitcast.17), custom_call_target="tpu_custom_call" | custom-call | tf_op jit(solution)/shard_map/pallas_call | solution.py:36
  19.9 3.2 %collective-permute-start.4 = (f32[6,12,8,128]{3,2,1,0:T(8,128)}, f32[6,12,8,128]{3,2,1,0:T(8,128)S(1)}, u32[]{:S(2)}, u32[]{:S(2)}) collective-permute-start(f32[6,12,8,128]{3,2,1,0:T(8,128)} %get-tuple-element.18), channel_id=1, source_target_pairs={{0,128},{128,256},{256,384},{384,0},{1,129},{129,257},{257,385},{3... | collective-permute-start | bytes 884744 | tf_op jit(solution)/shard_map/ppermute | solution.py:258
  23.1 4.5 %collective-permute-start.5 = (f32[6,12,8,128]{3,2,1,0:T(8,128)}, f32[6,12,8,128]{3,2,1,0:T(8,128)S(1)}, u32[]{:S(2)}, u32[]{:S(2)}) collective-permute-start(f32[6,12,8,128]{3,2,1,0:T(8,128)} %get-tuple-element.19), channel_id=1, source_target_pairs={{0,256},{128,384},{256,0},{384,128},{1,257},{129,385},{257,1},{385... | collective-permute-start | bytes 884744 | tf_op jit(solution)/shard_map/ppermute | solution.py:258
  27.6 3.0 %collective-permute-start.6 = (f32[6,12,8,128]{3,2,1,0:T(8,128)}, f32[6,12,8,128]{3,2,1,0:T(8,128)S(1)}, u32[]{:S(2)}, u32[]{:S(2)}) collective-permute-start(f32[6,12,8,128]{3,2,1,0:T(8,128)} %get-tuple-element.20), channel_id=1, source_target_pairs={{0,384},{128,0},{256,128},{384,256},{1,385},{129,1},{257,129},{385... | collective-permute-start | bytes 884744 | tf_op jit(solution)/shard_map/ppermute | solution.py:258
  30.6 1.4 %shard_map.69 = f32[8,80,128]{2,1,0:T(8,128)} custom-call(s32[5]{0:T(128)} %stack.23.place, f32[8,2,24,128]{3,2,1,0:T(8,128)S(1)} %bitcast.15), custom_call_target="tpu_custom_call" | custom-call | tf_op jit(solution)/shard_map/pallas_call | solution.py:36
  32.0 9.7 %all-to-all-start.1 = ((f32[8,80,128]{2,1,0:T(8,128)}), f32[8,80,128]{2,1,0:T(8,128)S(1)}, u32[]{:S(2)}, u32[]{:S(2)}) async-start(f32[8,80,128]{2,1,0:T(8,128)} %shard_map.69), calls=%async_computation.1 | async-start | bytes 655360 | tf_op jit(solution)/shard_map/all_to_all | solution.py:264
  41.7 3.2 %collective-permute-start.2 = (f32[2,24,128]{2,1,0:T(8,128)S(1)}, f32[2,24,128]{2,1,0:T(8,128)S(1)}, u32[]{:S(2)}, u32[]{:S(2)}) collective-permute-start(f32[2,24,128]{2,1,0:T(8,128)S(1)} %get-tuple-element.33), channel_id=1, source_target_pairs={{0,128},{128,256},{256,384},{1,129},{129,257},{257,385},{2,130},{1... | collective-permute-start | bytes 73736 | tf_op jit(solution)/shard_map/ppermute | solution.py:260
  44.9 1.3 %collective-permute-start.3 = (f32[2,24,128]{2,1,0:T(8,128)S(1)}, f32[2,24,128]{2,1,0:T(8,128)S(1)}, u32[]{:S(2)}, u32[]{:S(2)}) collective-permute-start(f32[2,24,128]{2,1,0:T(8,128)S(1)} %get-tuple-element.32), channel_id=1, source_target_pairs={{128,0},{256,128},{384,256},{129,1},{257,129},{385,257},{130,2},{2... | collective-permute-start | bytes 73736 | tf_op jit(solution)/shard_map/ppermute | solution.py:261
  46.3 3.3 %collective-permute-done.3.next_row = f32[2,24,128]{2,1,0:T(8,128)S(1)} collective-permute-done((f32[2,24,128]{2,1,0:T(8,128)S(1)}, f32[2,24,128]{2,1,0:T(8,128)S(1)}, u32[]{:S(2)}, u32[]{:S(2)}) %collective-permute-start.3) | collective-permute-done | bytes 24608 | tf_op jit(solution)/shard_map/ppermute | solution.py:261
  49.5 1.8 %shard_map.73 = (f32[16,72,128]{2,1,0:T(8,128)}, f32[2,24,128]{2,1,0:T(8,128)S(1)}, f32[2,24,128]{2,1,0:T(8,128)}, f32[2,24,128]{2,1,0:T(8,128)}, f32[2,24,128]{2,1,0:T(8,128)}) custom-call(s32[5]{0:T(128)} %stack.23.place, f32[2,24,8,128]{3,2,1,0:T(8,128)S(1)} %shard_map.71.tmpl, f32[2,24,128]{2,1,0:T(8,128)S(1)} %collective-permute-done.2.prev_row, ...), custom_call_target="tpu_custom_call" | custom-call | tf_op jit(solution)/shard_map/pallas_call | solution.py:36
  51.4 10.9 %all-to-all-start.2 = ((f32[16,72,128]{2,1,0:T(8,128)}), f32[16,72,128]{2,1,0:T(8,128)S(1)}, u32[]{:S(2)}, u32[]{:S(2)}) async-start(f32[16,72,128]{2,1,0:T(8,128)} %get-tuple-element.25), calls=%async_computation.2 | async-start | bytes 1179648 | tf_op jit(solution)/shard_map/all_to_all | solution.py:271
  62.2 3.5 %collective-permute-start = (f32[8,80,128]{2,1,0:T(8,128)S(1)}, f32[8,80,128]{2,1,0:T(8,128)S(1)}, u32[]{:S(2)}, u32[]{:S(2)}) collective-permute-start(f32[8,80,128]{2,1,0:T(8,128)S(1)} %all-to-all-done.1.mine.mixed), channel_id=1, source_target_pairs={{0,1},{1,4},{4,5},{5,8},{8,9},{9,12},{12,13},{13,128},{128,129},{1... | collective-permute-start | bytes 983048 | tf_op jit(solution)/shard_map/ppermute | solution.py:274
  65.8 1.9 %collective-permute-start.1 = (f32[8,80,128]{2,1,0:T(8,128)S(1)}, f32[8,80,128]{2,1,0:T(8,128)S(1)}, u32[]{:S(2)}, u32[]{:S(2)}) collective-permute-start(f32[8,80,128]{2,1,0:T(8,128)S(1)} %all-to-all-done.1.mine.mixed), channel_id=1, source_target_pairs={{1,0},{4,1},{5,4},{8,5},{9,8},{12,9},{13,12},{128,13},{129,128},{1... | collective-permute-start | bytes 983048 | tf_op jit(solution)/shard_map/ppermute | solution.py:275
  67.7 2.1 %collective-permute-done.prev = f32[8,80,128]{2,1,0:T(8,128)S(1)} collective-permute-done((f32[8,80,128]{2,1,0:T(8,128)S(1)}, f32[8,80,128]{2,1,0:T(8,128)S(1)}, u32[]{:S(2)}, u32[]{:S(2)}) %collective-permute-start) | collective-permute-done | bytes 327712 | tf_op jit(solution)/shard_map/ppermute | solution.py:274
  69.8 4.4 %collective-permute-done.1.succ = f32[8,80,128]{2,1,0:T(8,128)S(1)} collective-permute-done((f32[8,80,128]{2,1,0:T(8,128)S(1)}, f32[8,80,128]{2,1,0:T(8,128)S(1)}, u32[]{:S(2)}, u32[]{:S(2)}) %collective-permute-start.1) | collective-permute-done | bytes 327712 | tf_op jit(solution)/shard_map/ppermute | solution.py:275
  74.2 0.2 shard_map.70.slopes
  74.4 2.5 %collective-permute-start.7 = (f32[2,24,128]{2,1,0:T(8,128)S(1)}, f32[2,24,128]{2,1,0:T(8,128)S(1)}, u32[]{:S(2)}, u32[]{:S(2)}) collective-permute-start(f32[2,24,128]{2,1,0:T(8,128)S(1)} %copy-done.6), channel_id=1, source_target_pairs={{0,32},{16,48},{32,0},{48,16},{64,96},{80,112},{96,64},{112,80},{1... | collective-permute-start | bytes 73736 | tf_op jit(solution)/shard_map/ppermute | solution.py:290
  76.9 3.2 %collective-permute-start.8 = (f32[2,24,128]{2,1,0:T(8,128)S(1)}, f32[2,24,128]{2,1,0:T(8,128)S(1)}, u32[]{:S(2)}, u32[]{:S(2)}) collective-permute-start(f32[2,24,128]{2,1,0:T(8,128)S(1)} %copy-done.5), channel_id=1, source_target_pairs={{0,64},{16,80},{32,96},{48,112},{64,0},{80,16},{96,32},{112,48},{1... | collective-permute-start | bytes 73736 | tf_op jit(solution)/shard_map/ppermute | solution.py:290
  80.1 7.5 %collective-permute-start.9 = (f32[2,24,128]{2,1,0:T(8,128)S(1)}, f32[2,24,128]{2,1,0:T(8,128)S(1)}, u32[]{:S(2)}, u32[]{:S(2)}) collective-permute-start(f32[2,24,128]{2,1,0:T(8,128)S(1)} %copy-done.4), channel_id=1, source_target_pairs={{0,96},{16,112},{32,64},{48,80},{64,32},{80,48},{96,0},{112,16},{1... | collective-permute-start | bytes 73736 | tf_op jit(solution)/shard_map/ppermute | solution.py:290
  87.7 0.8 shard_map.74
  88.5 13.2 %all-to-all-done.2.got = f32[16,72,128]{2,1,0:T(8,128)S(1)} async-done(((f32[16,72,128]{2,1,0:T(8,128)}), f32[16,72,128]{2,1,0:T(8,128)S(1)}, u32[]{:S(2)}, u32[]{:S(2)}) %all-to-all-start.2) | async-done | bytes 589856 | tf_op jit(solution)/shard_map/all_to_all | solution.py:271
  101.6 2.9 %shard_map.75 = f32[32,54,128]{2,1,0:T(8,128)} custom-call(s32[5]{0:T(128)} %stack.23.place, f32[3,192,256]{2,1,0:T(8,128)S(1)} %shard_map.70.slopes, f32[16,72,128]{2,1,0:T(8,128)S(1)} %all-to-all-done.2.got, bf16[2,96,192]{2,1,0:T(8,128)(2,1)S(1)} %get-tuple-element.26.zw, bf16[2,2,256,192]{3,2,1,0:T(8,128)(2,1)S(1)} %get-tuple-element.27.xw), custom_call_target="tpu_custom_call" | custom-call | tf_op jit(solution)/shard_map/pallas_call | solution.py:36
  104.6 4.5 %all-to-all-start.3 = ((f32[32,54,128]{2,1,0:T(8,128)}), f32[32,54,128]{2,1,0:T(8,128)S(1)}, u32[]{:S(2)}, u32[]{:S(2)}) async-start(f32[32,54,128]{2,1,0:T(8,128)} %shard_map.75), calls=%async_computation.3 | async-start | bytes 1835008 | tf_op jit(solution)/shard_map/all_to_all | solution.py:298
  109.2 1.9 %collective-permute-start.10 = (f32[24,128]{1,0:T(8,128)S(1)}, f32[24,128]{1,0:T(8,128)S(1)}, u32[]{:S(2)}, u32[]{:S(2)}) collective-permute-start(f32[24,128]{1,0:T(8,128)S(1)} %dynamic-slice_bitcast_fusion), channel_id=1, source_target_pairs={{0,16},{16,0},{32,48},{48,32},{64,80},{80,64},{96,112},{112,96},{1... | collective-permute-start | bytes 36872 | tf_op jit(solution)/shard_map/ppermute | solution.py:294
  111.1 2.8 %collective-permute-done.10 = f32[24,128]{1,0:T(8,128)S(1)} collective-permute-done((f32[24,128]{1,0:T(8,128)S(1)}, f32[24,128]{1,0:T(8,128)S(1)}, u32[]{:S(2)}, u32[]{:S(2)}) %collective-permute-start.10) | collective-permute-done | bytes 12320 | tf_op jit(solution)/shard_map/ppermute | solution.py:294
  113.9 0.6 fusion
  114.6 10.4 %all-to-all-done.3.packed = f32[32,54,128]{2,1,0:T(8,128)S(1)} async-done(((f32[32,54,128]{2,1,0:T(8,128)}), f32[32,54,128]{2,1,0:T(8,128)S(1)}, u32[]{:S(2)}, u32[]{:S(2)}) %all-to-all-start.3) | async-done | bytes 884768 | tf_op jit(solution)/shard_map/all_to_all | solution.py:298
  125.0 1.2 shard_map.76
  (31 shorter events, 0.2 us)
Async XLA Ops:
  0.6 0.7 copy-start.2
  2.0 28.5 %all-to-all-start = ((f32[16,24,128]{2,1,0:T(8,128)}), f32[16,24,128]{2,1,0:T(8,128)S(1)}, u32[]{:S(2)}, u32[]{:S(2)}) async-start(f32[16,24,128]{2,1,0:T(8,128)} %shard_map.68), calls=%async_computation | async-start | bytes 393216 | tf_op jit(solution)/shard_map/all_to_all | solution.py:251
  19.9 26.4 %collective-permute-start.4 = (f32[6,12,8,128]{3,2,1,0:T(8,128)}, f32[6,12,8,128]{3,2,1,0:T(8,128)S(1)}, u32[]{:S(2)}, u32[]{:S(2)}) collective-permute-start(f32[6,12,8,128]{3,2,1,0:T(8,128)} %get-tuple-element.18), channel_id=1, source_target_pairs={{0,128},{128,256},{256,384},{384,0},{1,129},{129,257},{257,385},{3... | collective-permute-start | bytes 884744 | tf_op jit(solution)/shard_map/ppermute | solution.py:258
  23.1 23.2 %collective-permute-start.5 = (f32[6,12,8,128]{3,2,1,0:T(8,128)}, f32[6,12,8,128]{3,2,1,0:T(8,128)S(1)}, u32[]{:S(2)}, u32[]{:S(2)}) collective-permute-start(f32[6,12,8,128]{3,2,1,0:T(8,128)} %get-tuple-element.19), channel_id=1, source_target_pairs={{0,256},{128,384},{256,0},{384,128},{1,257},{129,385},{257,1},{385... | collective-permute-start | bytes 884744 | tf_op jit(solution)/shard_map/ppermute | solution.py:258
  27.6 18.7 %collective-permute-start.6 = (f32[6,12,8,128]{3,2,1,0:T(8,128)}, f32[6,12,8,128]{3,2,1,0:T(8,128)S(1)}, u32[]{:S(2)}, u32[]{:S(2)}) collective-permute-start(f32[6,12,8,128]{3,2,1,0:T(8,128)} %get-tuple-element.20), channel_id=1, source_target_pairs={{0,384},{128,0},{256,128},{384,256},{1,385},{129,1},{257,129},{385... | collective-permute-start | bytes 884744 | tf_op jit(solution)/shard_map/ppermute | solution.py:258
  32.0 17.5 %all-to-all-start.1 = ((f32[8,80,128]{2,1,0:T(8,128)}), f32[8,80,128]{2,1,0:T(8,128)S(1)}, u32[]{:S(2)}, u32[]{:S(2)}) async-start(f32[8,80,128]{2,1,0:T(8,128)} %shard_map.69), calls=%async_computation.1 | async-start | bytes 655360 | tf_op jit(solution)/shard_map/all_to_all | solution.py:264
  41.7 4.6 %collective-permute-start.2 = (f32[2,24,128]{2,1,0:T(8,128)S(1)}, f32[2,24,128]{2,1,0:T(8,128)S(1)}, u32[]{:S(2)}, u32[]{:S(2)}) collective-permute-start(f32[2,24,128]{2,1,0:T(8,128)S(1)} %get-tuple-element.33), channel_id=1, source_target_pairs={{0,128},{128,256},{256,384},{1,129},{129,257},{257,385},{2,130},{1... | collective-permute-start | bytes 73736 | tf_op jit(solution)/shard_map/ppermute | solution.py:260
  44.9 4.6 %collective-permute-start.3 = (f32[2,24,128]{2,1,0:T(8,128)S(1)}, f32[2,24,128]{2,1,0:T(8,128)S(1)}, u32[]{:S(2)}, u32[]{:S(2)}) collective-permute-start(f32[2,24,128]{2,1,0:T(8,128)S(1)} %get-tuple-element.32), channel_id=1, source_target_pairs={{128,0},{256,128},{384,256},{129,1},{257,129},{385,257},{130,2},{2... | collective-permute-start | bytes 73736 | tf_op jit(solution)/shard_map/ppermute | solution.py:261
  51.4 23.1 %copy-start.6 = (f32[2,24,128]{2,1,0:T(8,128)S(1)}, f32[2,24,128]{2,1,0:T(8,128)}, u32[]{:S(2)}) copy-start(f32[2,24,128]{2,1,0:T(8,128)} %get-tuple-element.29) | copy-start | bytes 73732
  51.4 25.6 %copy-start.5 = (f32[2,24,128]{2,1,0:T(8,128)S(1)}, f32[2,24,128]{2,1,0:T(8,128)}, u32[]{:S(2)}) copy-start(f32[2,24,128]{2,1,0:T(8,128)} %get-tuple-element.30) | copy-start | bytes 73732
  51.4 28.8 %copy-start.4 = (f32[2,24,128]{2,1,0:T(8,128)S(1)}, f32[2,24,128]{2,1,0:T(8,128)}, u32[]{:S(2)}) copy-start(f32[2,24,128]{2,1,0:T(8,128)} %get-tuple-element.31) | copy-start | bytes 73732
  51.4 36.3 %copy-start = (f32[192,192]{1,0:T(8,128)S(1)}, f32[192,192]{1,0:T(8,128)}, u32[]{:S(2)}) copy-start(f32[192,192]{1,0:T(8,128)} %zk.1) | copy-start | bytes 442372
  51.4 36.3 %copy-start.1 = (f32[192,192]{1,0:T(8,128)S(1)}, f32[192,192]{1,0:T(8,128)}, u32[]{:S(2)}) copy-start(f32[192,192]{1,0:T(8,128)} %xk.1) | copy-start | bytes 442372
  51.4 50.2 %all-to-all-start.2 = ((f32[16,72,128]{2,1,0:T(8,128)}), f32[16,72,128]{2,1,0:T(8,128)S(1)}, u32[]{:S(2)}, u32[]{:S(2)}) async-start(f32[16,72,128]{2,1,0:T(8,128)} %get-tuple-element.25), calls=%async_computation.2 | async-start | bytes 1179648 | tf_op jit(solution)/shard_map/all_to_all | solution.py:271
  62.2 7.5 %collective-permute-start = (f32[8,80,128]{2,1,0:T(8,128)S(1)}, f32[8,80,128]{2,1,0:T(8,128)S(1)}, u32[]{:S(2)}, u32[]{:S(2)}) collective-permute-start(f32[8,80,128]{2,1,0:T(8,128)S(1)} %all-to-all-done.1.mine.mixed), channel_id=1, source_target_pairs={{0,1},{1,4},{4,5},{5,8},{8,9},{9,12},{12,13},{13,128},{128,129},{1... | collective-permute-start | bytes 983048 | tf_op jit(solution)/shard_map/ppermute | solution.py:274
  65.8 8.4 %collective-permute-start.1 = (f32[8,80,128]{2,1,0:T(8,128)S(1)}, f32[8,80,128]{2,1,0:T(8,128)S(1)}, u32[]{:S(2)}, u32[]{:S(2)}) collective-permute-start(f32[8,80,128]{2,1,0:T(8,128)S(1)} %all-to-all-done.1.mine.mixed), channel_id=1, source_target_pairs={{1,0},{4,1},{5,4},{8,5},{9,8},{12,9},{13,12},{128,13},{129,128},{1... | collective-permute-start | bytes 983048 | tf_op jit(solution)/shard_map/ppermute | solution.py:275
  74.4 34.7 %collective-permute-start.7 = (f32[2,24,128]{2,1,0:T(8,128)S(1)}, f32[2,24,128]{2,1,0:T(8,128)S(1)}, u32[]{:S(2)}, u32[]{:S(2)}) collective-permute-start(f32[2,24,128]{2,1,0:T(8,128)S(1)} %copy-done.6), channel_id=1, source_target_pairs={{0,32},{16,48},{32,0},{48,16},{64,96},{80,112},{96,64},{112,80},{1... | collective-permute-start | bytes 73736 | tf_op jit(solution)/shard_map/ppermute | solution.py:290
  76.9 32.2 %collective-permute-start.8 = (f32[2,24,128]{2,1,0:T(8,128)S(1)}, f32[2,24,128]{2,1,0:T(8,128)S(1)}, u32[]{:S(2)}, u32[]{:S(2)}) collective-permute-start(f32[2,24,128]{2,1,0:T(8,128)S(1)} %copy-done.5), channel_id=1, source_target_pairs={{0,64},{16,80},{32,96},{48,112},{64,0},{80,16},{96,32},{112,48},{1... | collective-permute-start | bytes 73736 | tf_op jit(solution)/shard_map/ppermute | solution.py:290
  80.1 29.0 %collective-permute-start.9 = (f32[2,24,128]{2,1,0:T(8,128)S(1)}, f32[2,24,128]{2,1,0:T(8,128)S(1)}, u32[]{:S(2)}, u32[]{:S(2)}) collective-permute-start(f32[2,24,128]{2,1,0:T(8,128)S(1)} %copy-done.4), channel_id=1, source_target_pairs={{0,96},{16,112},{32,64},{48,80},{64,32},{80,48},{96,0},{112,16},{1... | collective-permute-start | bytes 73736 | tf_op jit(solution)/shard_map/ppermute | solution.py:290
  104.6 9.4 %copy-start.3 = (f32[12,1,192]{2,1,0:T(1,128)S(1)}, f32[12,1,192]{2,1,0:T(1,128)}, u32[]{:S(2)}) copy-start(f32[12,1,192]{2,1,0:T(1,128)} %row.1) | copy-start | bytes 27652
  104.6 20.4 %all-to-all-start.3 = ((f32[32,54,128]{2,1,0:T(8,128)}), f32[32,54,128]{2,1,0:T(8,128)S(1)}, u32[]{:S(2)}, u32[]{:S(2)}) async-start(f32[32,54,128]{2,1,0:T(8,128)} %shard_map.75), calls=%async_computation.3 | async-start | bytes 1835008 | tf_op jit(solution)/shard_map/all_to_all | solution.py:298
  109.2 4.7 %collective-permute-start.10 = (f32[24,128]{1,0:T(8,128)S(1)}, f32[24,128]{1,0:T(8,128)S(1)}, u32[]{:S(2)}, u32[]{:S(2)}) collective-permute-start(f32[24,128]{1,0:T(8,128)S(1)} %dynamic-slice_bitcast_fusion), channel_id=1, source_target_pairs={{0,16},{16,0},{32,48},{48,32},{64,80},{80,64},{96,112},{112,96},{1... | collective-permute-start | bytes 36872 | tf_op jit(solution)/shard_map/ppermute | solution.py:294

commit v11 on v10

--- a/solution.py
+++ b/solution.py
@@ -192,19 +192,20 @@
 
 def main_kernel(place, slopes, got, zw, xw, out, force):
     y = place[0]
-    for k in range(8):
-        at = slice(24 * k, 24 * k + 24)
+    for x in range(4):
+        at = slice(48 * x, 48 * x + 48)
         for b in range(6):
-            r = jnp.concatenate([got[2 * k, 12 * b : 12 * b + 12], got[2 * k + 1, 12 * b : 12 * b + 12]], 0)
+            r = jnp.concatenate([got[4 * x + k, 12 * b : 12 * b + 12] for k in range(4)], 0)
             for c in range(3):
                 half = slice(0, LANES) if b < 4 else slice(LANES, WIDE)
-                force[at, (c * 6 + b) * LANES : (c * 6 + b + 1) * LANES] = r * slopes[c, at, half]
+                to = slice((c * 6 + b) * LANES, (c * 6 + b + 1) * LANES)
+                force[0, at, to], force[1, at, to] = split(r * slopes[c, at, half])
 
     def times(a1, a0, b1, b0):
         dot = lambda p, q: jnp.dot(p, q, preferred_element_type=F32)
         return dot(a1, b1) + (dot(a1, b0) + dot(a0, b1))
 
-    smooth = times(zw[0], zw[1], *split(force[...]))
+    smooth = times(zw[0], zw[1], force[0], force[1])
 
     for odd in range(2):
         left = []
@@ -282,7 +283,7 @@
         None, prev, mixed, succ
     )
     slopes, *parts[1:] = lax.optimization_barrier((slopes, *parts[1:]))
-    (packed,) = call(main_kernel, (shape(32, 54, LANES),), (pltpu.VMEM((192, 18 * LANES), F32),))(
+    (packed,) = call(main_kernel, (shape(32, 54, LANES),), (pltpu.VMEM((2, 192, 18 * LANES), BF16),))(
         place, slopes, got, zw, xw
     )
 

time: 127 us -> 127 us (level)
  no operation moved by 1% of the time
where the time goes in v11:
time: 127 us; the launch traced here: 126 us
  starting transfers between devices  75.4 us (59%)
  waiting for transfers between devices  36.1 us (28%)
  Pallas kernels  11.9 us (9%)
  local copies, waits for them, and re-layouts  1.44 us (1%)
    all_to_all x1, starting transfers between devices, per_device(): lax.all_to_all(piece, COL, 0, 0, tiled=True).reshape(8, 2, 24, LANES)  14.7 us
    ppermute x3, starting transfers between devices, per_device(): parts[t] = lax.ppermute(parts[t], 'zl', [(i, i ^ 2 * t) for i in range(8)])  13.2 us
    all_to_all x1, waiting for transfers between devices, per_device(): got = lax.all_to_all(by_row, ('x', 'zh', 'c'), 0, 0, tiled=True)  13.2 us
    pallas_call x9, Pallas kernels, run(): pl.pallas_call(kernel, out_shape=outs, in_specs=[*[smem()] * len(first),...  11.9 us
    all_to_all x1, starting transfers between devices, per_device(): got = lax.all_to_all(by_row, ('x', 'zh', 'c'), 0, 0, tiled=True)  10.9 us
    ppermute x3, starting transfers between devices, per_device(): raws[s] = lax.ppermute(raws[s], 'y', [(i, (i + s) % 4) for i in range(4)])  10.7 us
    all_to_all x1, waiting for transfers between devices, per_device(): back = lax.all_to_all(packed, ROW, 0, 0, tiled=True)  10.4 us
    all_to_all x1, starting transfers between devices, per_device(): mixed = lax.all_to_all(mixed, ('x', 'c'), 0, 0, tiled=True)  9.66 us
  transfers between devices with their start and end apart: 15, of which 6 were waited for; matrix products, arithmetic and copies ran while one was open for 1% of the time, Pallas kernels for 6%

profile of v11, /device:TPU:33, one launch (start us, length us, event | category | flops | bytes accessed | tf_op | source)
XLA Modules:
  0.0 126.4 jit_solution(15408102410683436564)
XLA Ops:
  0.6 0.7 copy-done.2
  1.3 0.7 shard_map.68
  2.0 14.7 %all-to-all-start = ((f32[16,24,128]{2,1,0:T(8,128)}), f32[16,24,128]{2,1,0:T(8,128)S(1)}, u32[]{:S(2)}, u32[]{:S(2)}) async-start(f32[16,24,128]{2,1,0:T(8,128)} %shard_map.68), calls=%async_computation | async-start | bytes 393216 | tf_op jit(solution)/shard_map/all_to_all | solution.py:252
  16.7 0.7 stack.23.place
  17.4 2.5 %shard_map.72 = (f32[6,12,8,128]{3,2,1,0:T(8,128)S(1)}, f32[6,12,8,128]{3,2,1,0:T(8,128)}, f32[6,12,8,128]{3,2,1,0:T(8,128)}, f32[6,12,8,128]{3,2,1,0:T(8,128)}) custom-call(s32[5]{0:T(128)} %stack.23.place, f32[12,32,192]{2,1,0:T(8,128)} %bitcast.19, f32[3,12,32,192]{3,2,1,0:T(8,128)} %bitcast.17), custom_call_target="tpu_custom_call" | custom-call | tf_op jit(solution)/shard_map/pallas_call | solution.py:36
  19.9 3.2 %collective-permute-start.4 = (f32[6,12,8,128]{3,2,1,0:T(8,128)}, f32[6,12,8,128]{3,2,1,0:T(8,128)S(1)}, u32[]{:S(2)}, u32[]{:S(2)}) collective-permute-start(f32[6,12,8,128]{3,2,1,0:T(8,128)} %get-tuple-element.18), channel_id=1, source_target_pairs={{0,128},{128,256},{256,384},{384,0},{1,129},{129,257},{257,385},{3... | collective-permute-start | bytes 884744 | tf_op jit(solution)/shard_map/ppermute | solution.py:259
  23.1 4.5 %collective-permute-start.5 = (f32[6,12,8,128]{3,2,1,0:T(8,128)}, f32[6,12,8,128]{3,2,1,0:T(8,128)S(1)}, u32[]{:S(2)}, u32[]{:S(2)}) collective-permute-start(f32[6,12,8,128]{3,2,1,0:T(8,128)} %get-tuple-element.19), channel_id=1, source_target_pairs={{0,256},{128,384},{256,0},{384,128},{1,257},{129,385},{257,1},{385... | collective-permute-start | bytes 884744 | tf_op jit(solution)/shard_map/ppermute | solution.py:259
  27.6 3.0 %collective-permute-start.6 = (f32[6,12,8,128]{3,2,1,0:T(8,128)}, f32[6,12,8,128]{3,2,1,0:T(8,128)S(1)}, u32[]{:S(2)}, u32[]{:S(2)}) collective-permute-start(f32[6,12,8,128]{3,2,1,0:T(8,128)} %get-tuple-element.20), channel_id=1, source_target_pairs={{0,384},{128,0},{256,128},{384,256},{1,385},{129,1},{257,129},{385... | collective-permute-start | bytes 884744 | tf_op jit(solution)/shard_map/ppermute | solution.py:259
  30.6 1.4 %shard_map.69 = f32[8,80,128]{2,1,0:T(8,128)} custom-call(s32[5]{0:T(128)} %stack.23.place, f32[8,2,24,128]{3,2,1,0:T(8,128)S(1)} %bitcast.15), custom_call_target="tpu_custom_call" | custom-call | tf_op jit(solution)/shard_map/pallas_call | solution.py:36
  32.0 9.7 %all-to-all-start.1 = ((f32[8,80,128]{2,1,0:T(8,128)}), f32[8,80,128]{2,1,0:T(8,128)S(1)}, u32[]{:S(2)}, u32[]{:S(2)}) async-start(f32[8,80,128]{2,1,0:T(8,128)} %shard_map.69), calls=%async_computation.1 | async-start | bytes 655360 | tf_op jit(solution)/shard_map/all_to_all | solution.py:265
  41.7 3.2 %collective-permute-start.2 = (f32[2,24,128]{2,1,0:T(8,128)S(1)}, f32[2,24,128]{2,1,0:T(8,128)S(1)}, u32[]{:S(2)}, u32[]{:S(2)}) collective-permute-start(f32[2,24,128]{2,1,0:T(8,128)S(1)} %get-tuple-element.33), channel_id=1, source_target_pairs={{0,128},{128,256},{256,384},{1,129},{129,257},{257,385},{2,130},{1... | collective-permute-start | bytes 73736 | tf_op jit(solution)/shard_map/ppermute | solution.py:261
  44.9 1.3 %collective-permute-start.3 = (f32[2,24,128]{2,1,0:T(8,128)S(1)}, f32[2,24,128]{2,1,0:T(8,128)S(1)}, u32[]{:S(2)}, u32[]{:S(2)}) collective-permute-start(f32[2,24,128]{2,1,0:T(8,128)S(1)} %get-tuple-element.32), channel_id=1, source_target_pairs={{128,0},{256,128},{384,256},{129,1},{257,129},{385,257},{130,2},{2... | collective-permute-start | bytes 73736 | tf_op jit(solution)/shard_map/ppermute | solution.py:262
  46.3 3.3 %collective-permute-done.3.next_row = f32[2,24,128]{2,1,0:T(8,128)S(1)} collective-permute-done((f32[2,24,128]{2,1,0:T(8,128)S(1)}, f32[2,24,128]{2,1,0:T(8,128)S(1)}, u32[]{:S(2)}, u32[]{:S(2)}) %collective-permute-start.3) | collective-permute-done | bytes 24608 | tf_op jit(solution)/shard_map/ppermute | solution.py:262
  49.5 1.8 %shard_map.73 = (f32[16,72,128]{2,1,0:T(8,128)}, f32[2,24,128]{2,1,0:T(8,128)S(1)}, f32[2,24,128]{2,1,0:T(8,128)}, f32[2,24,128]{2,1,0:T(8,128)}, f32[2,24,128]{2,1,0:T(8,128)}) custom-call(s32[5]{0:T(128)} %stack.23.place, f32[2,24,8,128]{3,2,1,0:T(8,128)S(1)} %shard_map.71.tmpl, f32[2,24,128]{2,1,0:T(8,128)S(1)} %collective-permute-done.2.prev_row, ...), custom_call_target="tpu_custom_call" | custom-call | tf_op jit(solution)/shard_map/pallas_call | solution.py:36
  51.4 10.9 %all-to-all-start.2 = ((f32[16,72,128]{2,1,0:T(8,128)}), f32[16,72,128]{2,1,0:T(8,128)S(1)}, u32[]{:S(2)}, u32[]{:S(2)}) async-start(f32[16,72,128]{2,1,0:T(8,128)} %get-tuple-element.25), calls=%async_computation.2 | async-start | bytes 1179648 | tf_op jit(solution)/shard_map/all_to_all | solution.py:272
  62.2 3.5 %collective-permute-start = (f32[8,80,128]{2,1,0:T(8,128)S(1)}, f32[8,80,128]{2,1,0:T(8,128)S(1)}, u32[]{:S(2)}, u32[]{:S(2)}) collective-permute-start(f32[8,80,128]{2,1,0:T(8,128)S(1)} %all-to-all-done.1.mine.mixed), channel_id=1, source_target_pairs={{0,1},{1,4},{4,5},{5,8},{8,9},{9,12},{12,13},{13,128},{128,129},{1... | collective-permute-start | bytes 983048 | tf_op jit(solution)/shard_map/ppermute | solution.py:275
  65.8 1.9 %collective-permute-start.1 = (f32[8,80,128]{2,1,0:T(8,128)S(1)}, f32[8,80,128]{2,1,0:T(8,128)S(1)}, u32[]{:S(2)}, u32[]{:S(2)}) collective-permute-start(f32[8,80,128]{2,1,0:T(8,128)S(1)} %all-to-all-done.1.mine.mixed), channel_id=1, source_target_pairs={{1,0},{4,1},{5,4},{8,5},{9,8},{12,9},{13,12},{128,13},{129,128},{1... | collective-permute-start | bytes 983048 | tf_op jit(solution)/shard_map/ppermute | solution.py:276
  67.7 2.1 %collective-permute-done.prev = f32[8,80,128]{2,1,0:T(8,128)S(1)} collective-permute-done((f32[8,80,128]{2,1,0:T(8,128)S(1)}, f32[8,80,128]{2,1,0:T(8,128)S(1)}, u32[]{:S(2)}, u32[]{:S(2)}) %collective-permute-start) | collective-permute-done | bytes 327712 | tf_op jit(solution)/shard_map/ppermute | solution.py:275
  69.8 4.4 %collective-permute-done.1.succ = f32[8,80,128]{2,1,0:T(8,128)S(1)} collective-permute-done((f32[8,80,128]{2,1,0:T(8,128)S(1)}, f32[8,80,128]{2,1,0:T(8,128)S(1)}, u32[]{:S(2)}, u32[]{:S(2)}) %collective-permute-start.1) | collective-permute-done | bytes 327712 | tf_op jit(solution)/shard_map/ppermute | solution.py:276
  74.2 0.2 shard_map.70.slopes
  74.4 2.5 %collective-permute-start.7 = (f32[2,24,128]{2,1,0:T(8,128)S(1)}, f32[2,24,128]{2,1,0:T(8,128)S(1)}, u32[]{:S(2)}, u32[]{:S(2)}) collective-permute-start(f32[2,24,128]{2,1,0:T(8,128)S(1)} %copy-done.6), channel_id=1, source_target_pairs={{0,32},{16,48},{32,0},{48,16},{64,96},{80,112},{96,64},{112,80},{1... | collective-permute-start | bytes 73736 | tf_op jit(solution)/shard_map/ppermute | solution.py:291
  76.9 3.2 %collective-permute-start.8 = (f32[2,24,128]{2,1,0:T(8,128)S(1)}, f32[2,24,128]{2,1,0:T(8,128)S(1)}, u32[]{:S(2)}, u32[]{:S(2)}) collective-permute-start(f32[2,24,128]{2,1,0:T(8,128)S(1)} %copy-done.5), channel_id=1, source_target_pairs={{0,64},{16,80},{32,96},{48,112},{64,0},{80,16},{96,32},{112,48},{1... | collective-permute-start | bytes 73736 | tf_op jit(solution)/shard_map/ppermute | solution.py:291
  80.1 7.5 %collective-permute-start.9 = (f32[2,24,128]{2,1,0:T(8,128)S(1)}, f32[2,24,128]{2,1,0:T(8,128)S(1)}, u32[]{:S(2)}, u32[]{:S(2)}) collective-permute-start(f32[2,24,128]{2,1,0:T(8,128)S(1)} %copy-done.4), channel_id=1, source_target_pairs={{0,96},{16,112},{32,64},{48,80},{64,32},{80,48},{96,0},{112,16},{1... | collective-permute-start | bytes 73736 | tf_op jit(solution)/shard_map/ppermute | solution.py:291
  87.7 0.8 shard_map.74
  88.5 13.2 %all-to-all-done.2.got = f32[16,72,128]{2,1,0:T(8,128)S(1)} async-done(((f32[16,72,128]{2,1,0:T(8,128)}), f32[16,72,128]{2,1,0:T(8,128)S(1)}, u32[]{:S(2)}, u32[]{:S(2)}) %all-to-all-start.2) | async-done | bytes 589856 | tf_op jit(solution)/shard_map/all_to_all | solution.py:272
  101.6 3.2 %shard_map.75 = f32[32,54,128]{2,1,0:T(8,128)} custom-call(s32[5]{0:T(128)} %stack.23.place, f32[3,192,256]{2,1,0:T(8,128)S(1)} %shard_map.70.slopes, f32[16,72,128]{2,1,0:T(8,128)S(1)} %all-to-all-done.2.got, bf16[2,96,192]{2,1,0:T(8,128)(2,1)S(1)} %get-tuple-element.26.zw, bf16[2,2,256,192]{3,2,1,0:T(8,128)(2,1)S(1)} %get-tuple-element.27.xw), custom_call_target="tpu_custom_call" | custom-call | tf_op jit(solution)/shard_map/pallas_call | solution.py:36
  104.8 4.5 %all-to-all-start.3 = ((f32[32,54,128]{2,1,0:T(8,128)}), f32[32,54,128]{2,1,0:T(8,128)S(1)}, u32[]{:S(2)}, u32[]{:S(2)}) async-start(f32[32,54,128]{2,1,0:T(8,128)} %shard_map.75), calls=%async_computation.3 | async-start | bytes 1835008 | tf_op jit(solution)/shard_map/all_to_all | solution.py:299
  109.4 1.9 %collective-permute-start.10 = (f32[24,128]{1,0:T(8,128)S(1)}, f32[24,128]{1,0:T(8,128)S(1)}, u32[]{:S(2)}, u32[]{:S(2)}) collective-permute-start(f32[24,128]{1,0:T(8,128)S(1)} %dynamic-slice_bitcast_fusion), channel_id=1, source_target_pairs={{0,16},{16,0},{32,48},{48,32},{64,80},{80,64},{96,112},{112,96},{1... | collective-permute-start | bytes 36872 | tf_op jit(solution)/shard_map/ppermute | solution.py:295
  111.3 2.8 %collective-permute-done.10 = f32[24,128]{1,0:T(8,128)S(1)} collective-permute-done((f32[24,128]{1,0:T(8,128)S(1)}, f32[24,128]{1,0:T(8,128)S(1)}, u32[]{:S(2)}, u32[]{:S(2)}) %collective-permute-start.10) | collective-permute-done | bytes 12320 | tf_op jit(solution)/shard_map/ppermute | solution.py:295
  114.2 0.6 fusion
  114.8 10.4 %all-to-all-done.3.packed = f32[32,54,128]{2,1,0:T(8,128)S(1)} async-done(((f32[32,54,128]{2,1,0:T(8,128)}), f32[32,54,128]{2,1,0:T(8,128)S(1)}, u32[]{:S(2)}, u32[]{:S(2)}) %all-to-all-start.3) | async-done | bytes 884768 | tf_op jit(solution)/shard_map/all_to_all | solution.py:299
  125.2 1.2 shard_map.76
  (31 shorter events, 0.2 us)
Async XLA Ops:
  0.6 0.7 copy-start.2
  2.0 28.5 %all-to-all-start = ((f32[16,24,128]{2,1,0:T(8,128)}), f32[16,24,128]{2,1,0:T(8,128)S(1)}, u32[]{:S(2)}, u32[]{:S(2)}) async-start(f32[16,24,128]{2,1,0:T(8,128)} %shard_map.68), calls=%async_computation | async-start | bytes 393216 | tf_op jit(solution)/shard_map/all_to_all | solution.py:252
  19.9 26.4 %collective-permute-start.4 = (f32[6,12,8,128]{3,2,1,0:T(8,128)}, f32[6,12,8,128]{3,2,1,0:T(8,128)S(1)}, u32[]{:S(2)}, u32[]{:S(2)}) collective-permute-start(f32[6,12,8,128]{3,2,1,0:T(8,128)} %get-tuple-element.18), channel_id=1, source_target_pairs={{0,128},{128,256},{256,384},{384,0},{1,129},{129,257},{257,385},{3... | collective-permute-start | bytes 884744 | tf_op jit(solution)/shard_map/ppermute | solution.py:259
  23.1 23.2 %collective-permute-start.5 = (f32[6,12,8,128]{3,2,1,0:T(8,128)}, f32[6,12,8,128]{3,2,1,0:T(8,128)S(1)}, u32[]{:S(2)}, u32[]{:S(2)}) collective-permute-start(f32[6,12,8,128]{3,2,1,0:T(8,128)} %get-tuple-element.19), channel_id=1, source_target_pairs={{0,256},{128,384},{256,0},{384,128},{1,257},{129,385},{257,1},{385... | collective-permute-start | bytes 884744 | tf_op jit(solution)/shard_map/ppermute | solution.py:259
  27.6 18.7 %collective-permute-start.6 = (f32[6,12,8,128]{3,2,1,0:T(8,128)}, f32[6,12,8,128]{3,2,1,0:T(8,128)S(1)}, u32[]{:S(2)}, u32[]{:S(2)}) collective-permute-start(f32[6,12,8,128]{3,2,1,0:T(8,128)} %get-tuple-element.20), channel_id=1, source_target_pairs={{0,384},{128,0},{256,128},{384,256},{1,385},{129,1},{257,129},{385... | collective-permute-start | bytes 884744 | tf_op jit(solution)/shard_map/ppermute | solution.py:259
  32.0 17.5 %all-to-all-start.1 = ((f32[8,80,128]{2,1,0:T(8,128)}), f32[8,80,128]{2,1,0:T(8,128)S(1)}, u32[]{:S(2)}, u32[]{:S(2)}) async-start(f32[8,80,128]{2,1,0:T(8,128)} %shard_map.69), calls=%async_computation.1 | async-start | bytes 655360 | tf_op jit(solution)/shard_map/all_to_all | solution.py:265
  41.7 4.6 %collective-permute-start.2 = (f32[2,24,128]{2,1,0:T(8,128)S(1)}, f32[2,24,128]{2,1,0:T(8,128)S(1)}, u32[]{:S(2)}, u32[]{:S(2)}) collective-permute-start(f32[2,24,128]{2,1,0:T(8,128)S(1)} %get-tuple-element.33), channel_id=1, source_target_pairs={{0,128},{128,256},{256,384},{1,129},{129,257},{257,385},{2,130},{1... | collective-permute-start | bytes 73736 | tf_op jit(solution)/shard_map/ppermute | solution.py:261
  44.9 4.6 %collective-permute-start.3 = (f32[2,24,128]{2,1,0:T(8,128)S(1)}, f32[2,24,128]{2,1,0:T(8,128)S(1)}, u32[]{:S(2)}, u32[]{:S(2)}) collective-permute-start(f32[2,24,128]{2,1,0:T(8,128)S(1)} %get-tuple-element.32), channel_id=1, source_target_pairs={{128,0},{256,128},{384,256},{129,1},{257,129},{385,257},{130,2},{2... | collective-permute-start | bytes 73736 | tf_op jit(solution)/shard_map/ppermute | solution.py:262
  51.4 23.1 %copy-start.6 = (f32[2,24,128]{2,1,0:T(8,128)S(1)}, f32[2,24,128]{2,1,0:T(8,128)}, u32[]{:S(2)}) copy-start(f32[2,24,128]{2,1,0:T(8,128)} %get-tuple-element.29) | copy-start | bytes 73732
  51.4 25.6 %copy-start.5 = (f32[2,24,128]{2,1,0:T(8,128)S(1)}, f32[2,24,128]{2,1,0:T(8,128)}, u32[]{:S(2)}) copy-start(f32[2,24,128]{2,1,0:T(8,128)} %get-tuple-element.30) | copy-start | bytes 73732
  51.4 28.8 %copy-start.4 = (f32[2,24,128]{2,1,0:T(8,128)S(1)}, f32[2,24,128]{2,1,0:T(8,128)}, u32[]{:S(2)}) copy-start(f32[2,24,128]{2,1,0:T(8,128)} %get-tuple-element.31) | copy-start | bytes 73732
  51.4 36.3 %copy-start = (f32[192,192]{1,0:T(8,128)S(1)}, f32[192,192]{1,0:T(8,128)}, u32[]{:S(2)}) copy-start(f32[192,192]{1,0:T(8,128)} %zk.1) | copy-start | bytes 442372
  51.4 36.3 %copy-start.1 = (f32[192,192]{1,0:T(8,128)S(1)}, f32[192,192]{1,0:T(8,128)}, u32[]{:S(2)}) copy-start(f32[192,192]{1,0:T(8,128)} %xk.1) | copy-start | bytes 442372
  51.4 50.2 %all-to-all-start.2 = ((f32[16,72,128]{2,1,0:T(8,128)}), f32[16,72,128]{2,1,0:T(8,128)S(1)}, u32[]{:S(2)}, u32[]{:S(2)}) async-start(f32[16,72,128]{2,1,0:T(8,128)} %get-tuple-element.25), calls=%async_computation.2 | async-start | bytes 1179648 | tf_op jit(solution)/shard_map/all_to_all | solution.py:272
  62.2 7.5 %collective-permute-start = (f32[8,80,128]{2,1,0:T(8,128)S(1)}, f32[8,80,128]{2,1,0:T(8,128)S(1)}, u32[]{:S(2)}, u32[]{:S(2)}) collective-permute-start(f32[8,80,128]{2,1,0:T(8,128)S(1)} %all-to-all-done.1.mine.mixed), channel_id=1, source_target_pairs={{0,1},{1,4},{4,5},{5,8},{8,9},{9,12},{12,13},{13,128},{128,129},{1... | collective-permute-start | bytes 983048 | tf_op jit(solution)/shard_map/ppermute | solution.py:275
  65.8 8.4 %collective-permute-start.1 = (f32[8,80,128]{2,1,0:T(8,128)S(1)}, f32[8,80,128]{2,1,0:T(8,128)S(1)}, u32[]{:S(2)}, u32[]{:S(2)}) collective-permute-start(f32[8,80,128]{2,1,0:T(8,128)S(1)} %all-to-all-done.1.mine.mixed), channel_id=1, source_target_pairs={{1,0},{4,1},{5,4},{8,5},{9,8},{12,9},{13,12},{128,13},{129,128},{1... | collective-permute-start | bytes 983048 | tf_op jit(solution)/shard_map/ppermute | solution.py:276
  74.4 34.9 %collective-permute-start.7 = (f32[2,24,128]{2,1,0:T(8,128)S(1)}, f32[2,24,128]{2,1,0:T(8,128)S(1)}, u32[]{:S(2)}, u32[]{:S(2)}) collective-permute-start(f32[2,24,128]{2,1,0:T(8,128)S(1)} %copy-done.6), channel_id=1, source_target_pairs={{0,32},{16,48},{32,0},{48,16},{64,96},{80,112},{96,64},{112,80},{1... | collective-permute-start | bytes 73736 | tf_op jit(solution)/shard_map/ppermute | solution.py:291
  76.9 32.4 %collective-permute-start.8 = (f32[2,24,128]{2,1,0:T(8,128)S(1)}, f32[2,24,128]{2,1,0:T(8,128)S(1)}, u32[]{:S(2)}, u32[]{:S(2)}) collective-permute-start(f32[2,24,128]{2,1,0:T(8,128)S(1)} %copy-done.5), channel_id=1, source_target_pairs={{0,64},{16,80},{32,96},{48,112},{64,0},{80,16},{96,32},{112,48},{1... | collective-permute-start | bytes 73736 | tf_op jit(solution)/shard_map/ppermute | solution.py:291
  80.1 29.2 %collective-permute-start.9 = (f32[2,24,128]{2,1,0:T(8,128)S(1)}, f32[2,24,128]{2,1,0:T(8,128)S(1)}, u32[]{:S(2)}, u32[]{:S(2)}) collective-permute-start(f32[2,24,128]{2,1,0:T(8,128)S(1)} %copy-done.4), channel_id=1, source_target_pairs={{0,96},{16,112},{32,64},{48,80},{64,32},{80,48},{96,0},{112,16},{1... | collective-permute-start | bytes 73736 | tf_op jit(solution)/shard_map/ppermute | solution.py:291
  104.8 9.4 %copy-start.3 = (f32[12,1,192]{2,1,0:T(1,128)S(1)}, f32[12,1,192]{2,1,0:T(1,128)}, u32[]{:S(2)}) copy-start(f32[12,1,192]{2,1,0:T(1,128)} %row.1) | copy-start | bytes 27652
  104.8 20.4 %all-to-all-start.3 = ((f32[32,54,128]{2,1,0:T(8,128)}), f32[32,54,128]{2,1,0:T(8,128)S(1)}, u32[]{:S(2)}, u32[]{:S(2)}) async-start(f32[32,54,128]{2,1,0:T(8,128)} %shard_map.75), calls=%async_computation.3 | async-start | bytes 1835008 | tf_op jit(solution)/shard_map/all_to_all | solution.py:299
  109.4 4.7 %collective-permute-start.10 = (f32[24,128]{1,0:T(8,128)S(1)}, f32[24,128]{1,0:T(8,128)S(1)}, u32[]{:S(2)}, u32[]{:S(2)}) collective-permute-start(f32[24,128]{1,0:T(8,128)S(1)} %dynamic-slice_bitcast_fusion), channel_id=1, source_target_pairs={{0,16},{16,0},{32,48},{48,32},{64,80},{80,64},{96,112},{112,96},{1... | collective-permute-start | bytes 36872 | tf_op jit(solution)/shard_map/ppermute | solution.py:295
